TPU v7x, 32 devices: a whole 2x2x4 slice. The times are simulated.
32 devices in a mesh: vel: 4 (over y, x), cell: 8 (over z, core).
Axes of the slice: x: 2, y: 2, z: 4, core: 2. Of those that a mesh axis runs over, the one named last changes fastest.
Arguments:
- distribution: float32 [32, 32, 13824], P('cell', None, 'vel'), may hold values from -6 to 6
- collision: bfloat16 [4, 8, 432, 13824], P(None, 'cell', None, 'vel'), may hold values from -0.0546875 to 0.0546875
- directions: int32 [13824], P('vel'), may hold values from 0 to 1
- wall_mask: int32 [32, 32], P('cell'), may hold values 0 or 1
Outputs:
- relaxed: float32 [32, 32, 13824], P('cell', None, 'vel')
All inputs are finite; a program needn't handle non-finite values. No bound on the sum of `wall_mask` on one device may be relied on, other than what follows from the above.
Results may differ from a plain program's by a relative error of at most 0.0012.
Values may be sent and summed in bfloat16 or wider, within the bound.
No kernel may reach another device: no remote copies, remote signals or barrier semaphores. Data moves between devices by JAX's collectives and lax.ppermute only.
A program may use at most 128 MiB of HBM per device.

v0:
```python
import jax
import jax.numpy as jnp
from jax import lax
from jax.sharding import PartitionSpec as P

VG = 24


courant = 0.8
relax = 0.5


def extended(shard, sides, width):
    for axis, dim in sides:
        size, length = (lax.axis_size(axis), shard.shape[dim])
        up = [(i, (i + 1) % size) for i in range(size)]
        down = [(j, i) for i, j in up]
        last = lax.slice_in_dim(shard, length - width, length, axis=dim)
        first = lax.slice_in_dim(shard, 0, width, axis=dim)
        before = lax.ppermute(last, axis, up)
        after = lax.ppermute(first, axis, down)
        shard = jnp.concatenate([before, shard, after], axis=dim)
    return shard


def speeds(directions, offset, length):
    vel_index = offset + jnp.arange(length, dtype=jnp.int32)
    grid_x = vel_index // (VG * VG)
    grid_y = vel_index // VG % VG
    moving = 2 * directions - 1
    speed_x = courant * (grid_x.astype(jnp.float32) + 0.5) / VG
    speed_y = courant * (grid_y.astype(jnp.float32) - 0.5 * (VG - 1)) / VG
    return (moving, speed_x, speed_y)


def transverse(distribution, speed_y):
    width_y = distribution.shape[1]
    padded = jnp.pad(distribution, ((0, 0), (2, 2), (0, 0)))
    upward = speed_y > 0
    first_up = jnp.where(upward, padded[:, 1 : width_y + 1], padded[:, 3 : width_y + 3])
    second_up = jnp.where(upward, padded[:, 0:width_y], padded[:, 4 : width_y + 4])
    return jnp.abs(speed_y) * (1.5 * distribution - 2.0 * first_up + 0.5 * second_up)


def body(distribution, collision, directions, wall_mask):
    tile_len, width_y, local_vel = distribution.shape
    cell_count = lax.axis_size("cell")
    vel_count = lax.axis_size("vel")
    piece_len = local_vel // cell_count
    total_x = tile_len * cell_count
    moving, speed_x, speed_y = speeds(directions, lax.axis_index("vel") * local_vel, local_vel)
    rounded = distribution.astype(jnp.bfloat16)
    whole = lax.all_gather(rounded, "vel", axis=2, tiled=True)
    pieces = whole.reshape(tile_len, width_y, vel_count, cell_count, piece_len)
    spread = lax.all_to_all(pieces, "cell", split_axis=3, concat_axis=0, tiled=True)
    panel_block = spread.reshape(total_x * width_y, vel_count * piece_len)
    local_matrix = collision.reshape(vel_count * piece_len, local_vel)
    padded_x = extended(distribution, (("cell", 0),), 2)
    first_up = jnp.where(moving > 0, padded_x[1 : tile_len + 1], padded_x[3 : tile_len + 3])
    second_up = jnp.where(moving > 0, padded_x[0:tile_len], padded_x[4 : tile_len + 4])
    adv_x = speed_x * (1.5 * distribution - 2.0 * first_up + 0.5 * second_up)
    adv_y = transverse(distribution, speed_y)
    gain = lax.psum_scatter(
        jnp.dot(panel_block, local_matrix, preferred_element_type=jnp.float32),
        "cell",
        scatter_dimension=0,
        tiled=True,
    )
    gain = gain.reshape(tile_len, width_y, local_vel)
    open_cells = (1 - wall_mask).astype(jnp.float32)[:, :, None]
    return open_cells * (distribution - adv_x - adv_y + relax * gain)


def solution(mesh):
    in_specs = (P("cell", None, "vel"), P(None, "cell", None, "vel"), P("vel"), P("cell", None))
    out_specs = P("cell", None, "vel")
    return jax.shard_map(body, mesh=mesh, in_specs=in_specs, out_specs=out_specs, check_vma=False)
```

profile of v0, /device:TPU:0, one launch (start us, length us, event | category | flops | bytes accessed | tf_op | source)
XLA Modules:
  0.0 377.6 jit_solution(18030812726621182540)
XLA Ops:
  6.5 0.0 all-gather.2.cloned.1.call-start
  6.5 1.5 fusion.26
  8.1 0.0 copy-start
  8.1 0.5 collective-permute-start
  8.6 14.8 %collective-permute-done = f32[2,32,3456]{2,1,0:T(8,128)S(1)} collective-permute-done((f32[2,32,3456]{2,1,0:T(8,128)S(1)}, f32[2,32,3456]{2,1,0:T(8,128)S(1)}, u32[]{:S(2)}, u32[]{:S(2)}) %collective-permute-start) | collective-permute-done | bytes 884768 | tf_op jit(solution)/shard_map/ppermute | solution.py:20
  23.4 1.0 constant_dynamic-update-slice_fusion.1
  24.4 0.0 copy-done
  24.4 2.4 constant_dynamic-update-slice_fusion
  26.7 0.0 all-gather.2.cloned.1.call-update
  26.8 0.0 reduce-scatter.2.cloned.1.call-start
  26.8 47.3 %all-gather.2.cloned.1.call-done = bf16[4,32,13824]{2,1,0:T(8,128)(2,1)} async-done(((bf16[4,32,3456]{2,1,0:T(8,128)(2,1)}), bf16[4,32,13824]{2,1,0:T(8,128)(2,1)}) %all-gather.2.cloned.1.call-update) | async-done | bytes 3538960 | tf_op jit(solution)/shard_map/all_gather | solution.py:53
  74.1 11.2 %reshape.47 = bf16[4,32,4,8,432]{4,3,2,1,0:T(8,128)(2,1)} reshape(bf16[4,32,13824]{2,1,0:T(8,128)(2,1)} %all-gather.2.cloned.1.call-done) | data formatting | bytes 7077888 | tf_op jit(solution)/shard_map/reshape | solution.py:54
  85.3 4.3 %copy.5 = bf16[4,32,4,8,432]{4,2,1,0,3:T(4,128)(2,1)S(1)} copy(bf16[4,32,4,8,432]{4,3,2,1,0:T(8,128)(2,1)} %reshape.47) | data formatting | bytes 7077888 | tf_op jit(solution)/shard_map/reshape | solution.py:54
  89.6 98.5 %all_to_all.15 = bf16[4,32,4,8,432]{4,2,1,0,3:T(4,128)(2,1)} all-to-all(bf16[4,32,4,8,432]{4,2,1,0,3:T(4,128)(2,1)S(1)} %copy.5), channel_id=1, replica_groups=mesh['vel'=4,'cell'=8] {'cell'}, dimensions={3} | all-to-all | bytes 7077888 | tf_op jit(solution)/shard_map/all_to_all | solution.py:55
  188.2 9.1 %reshape.48 = bf16[1024,1728]{1,0:T(8,128)(2,1)} reshape(bf16[8,4,32,4,1,432]{5,3,2,1,0,4:T(4,128)(2,1)} %bitcast.9) | data formatting | bytes 7077888 | tf_op jit(solution)/shard_map/reshape | solution.py:56
  197.3 20.3 %fusion.27 = f32[1024,3456]{1,0:T(8,128)} fusion(bf16[1024,1728]{1,0:T(8,128)(2,1)} %reshape.48, bf16[1728,3456]{1,0:T(8,128)(2,1)} %bitcast.11), kind=kOutput, calls=%fused_computation.48 | convolution fusion | flops 12230590464 | bytes 29638656 | tf_op jit(solution)/shard_map/dot_general | solution.py:64
  217.6 0.0 reduce-scatter.2.cloned.1.call-update
  217.6 1.0 collective-permute-start.1
  218.5 0.7 fusion.18
  219.2 1.2 subtract_convert_fusion
  220.4 1.3 add_compare_fusion
  221.7 22.6 %collective-permute-done.1 = f32[2,32,3456]{2,1,0:T(8,128)S(1)} collective-permute-done((f32[2,32,3456]{2,1,0:T(8,128)S(1)}, f32[2,32,3456]{2,1,0:T(8,128)S(1)}, u32[]{:S(2)}, u32[]{:S(2)}) %collective-permute-start.1) | collective-permute-done | bytes 884768 | tf_op jit(solution)/shard_map/ppermute | solution.py:21
  244.3 1.0 constant_dynamic-update-slice_fusion.2
  245.3 0.0 copy-start.2
  245.3 0.0 copy-start.3
  245.3 0.0 copy-start.4
  245.3 0.0 copy-start.5
  245.3 119.1 %reduce-scatter.2.cloned.1.call-done = f32[128,3456]{1,0:T(8,128)} async-done(((f32[1024,3456]{1,0:T(8,128)}), f32[128,3456]{1,0:T(8,128)}) %reduce-scatter.2.cloned.1.call-update) | async-done | bytes 1769488 | tf_op jit(solution)/shard_map/reduce_scatter | solution.py:63
  364.4 0.0 copy-start.1
  364.4 1.7 broadcast_multiply_fusion
  366.1 0.0 copy-done.2
  366.1 0.0 copy-done.3
  366.1 0.0 copy-done.4
  366.1 0.0 copy-done.5
  366.2 0.5 copy-done.1
  366.7 4.1 %fusion.7 = f32[4,32,3456]{2,1,0:T(8,128)} fusion(f32[4,32,3456]{2,1,0:T(8,128)S(1)} %bitcast.10, f32[4,32,3456]{2,1,0:T(8,128)S(1)} %copy-done, f32[6,32,3456]{2,1,0:T(8,128)S(1)} %copy-done.1, f32[6,32,3456]{2,1,0:T(8,128)} %get-tuple-element.5, f32[3456]{0:T(1024)S(1)} %copy-done.2, f32[3456]{0:T(1024)S(1)} %get-tuple-element.10, ...), kind=kLoop, calls=%fused_computation.11 | loop fusion | flops 8404992 | bytes 12421376 | tf_op jit(solution)/shard_map/mul | solution.py:71
Async XLA Ops:
  6.5 67.6 %all-gather.2.cloned.1.call-start = ((), (), s32[]{:S(2)}) async-start(), calls=%async_computation.2 | async-start | bytes 4423680 | tf_op jit(solution)/shard_map/all_gather | solution.py:53
  8.1 16.3 %copy-start = (f32[4,32,3456]{2,1,0:T(8,128)S(1)}, f32[4,32,3456]{2,1,0:T(8,128)}, u32[]{:S(2)}) copy-start(f32[4,32,3456]{2,1,0:T(8,128)} %param.4) | copy-start | bytes 5308420
  8.1 15.3 %collective-permute-start = (f32[2,32,3456]{2,1,0:T(8,128)S(1)}, f32[2,32,3456]{2,1,0:T(8,128)S(1)}, u32[]{:S(2)}, u32[]{:S(2)}) collective-permute-start(f32[2,32,3456]{2,1,0:T(8,128)S(1)} %get-tuple-element.8), channel_id=1, source_target_pairs={{0,1},{1,2},{2,3},{3,4},{4,5},{5,6},{6,7},{7,0},{8,9},{9,10},{10,1... | collective-permute-start | bytes 2654216 | tf_op jit(solution)/shard_map/ppermute | solution.py:20
  26.8 337.6 %reduce-scatter.2.cloned.1.call-start = ((), (), s32[]{:S(2)}) async-start(), calls=%async_computation.3 | async-start | bytes 15925248 | tf_op jit(solution)/shard_map/reduce_scatter | solution.py:63
  217.6 26.7 %collective-permute-start.1 = (f32[2,32,3456]{2,1,0:T(8,128)S(1)}, f32[2,32,3456]{2,1,0:T(8,128)S(1)}, u32[]{:S(2)}, u32[]{:S(2)}) collective-permute-start(f32[2,32,3456]{2,1,0:T(8,128)S(1)} %get-tuple-element.9), channel_id=1, source_target_pairs={{1,0},{2,1},{3,2},{4,3},{5,4},{6,5},{7,6},{0,7},{9,8},{10,9},{11,1... | collective-permute-start | bytes 2654216 | tf_op jit(solution)/shard_map/ppermute | solution.py:21
  245.3 120.8 %copy-start.2 = (f32[3456]{0:T(1024)S(1)}, f32[3456]{0:T(1024)}, u32[]{:S(2)}) copy-start(f32[3456]{0:T(1024)} %get-tuple-element.11) | copy-start | bytes 41476
  245.3 120.9 %copy-start.3 = (pred[3456]{0:T(1024)(128)(4,1)S(1)}, pred[3456]{0:T(1024)(128)(4,1)}, u32[]{:S(2)}) copy-start(pred[3456]{0:T(1024)(128)(4,1)} %get-tuple-element.12) | copy-start | bytes 10372
  245.3 120.9 %copy-start.4 = (pred[3456]{0:T(1024)(128)(4,1)S(1)}, pred[3456]{0:T(1024)(128)(4,1)}, u32[]{:S(2)}) copy-start(pred[3456]{0:T(1024)(128)(4,1)} %get-tuple-element.13) | copy-start | bytes 10372
  245.3 120.9 %copy-start.5 = (f32[4,32]{1,0:T(4,128)S(1)}, f32[4,32]{1,0:T(4,128)}, u32[]{:S(2)}) copy-start(f32[4,32]{1,0:T(4,128)} %subtract_convert_fusion) | copy-start | bytes 1540
  364.4 2.3 copy-start.1
Sparse Core Ops, SparseCore 0:
  26.9 47.1 all-gather.1
  217.7 146.6 reduce-scatter.1
where the time goes:
time: 378 us
  waiting for transfers between devices  204 us (54%)
  blocking collectives  98.5 us (26%)
  local copies, waits for them, and re-layouts  28.7 us (8%)
  matrix products  20.3 us (5%)
  between operations  13.5 us (4%)
  other arithmetic  11.4 us (3%)
    reduce_scatter x1, waiting for transfers between devices, body(): lax.psum_scatter(jnp.dot(panel_block, local_matrix, preferred_element_typ...  119 us
    all_to_all x1, blocking collectives, body(): lax.all_to_all(pieces, 'cell', split_axis=3, concat_axis=0, tiled=True)  98.5 us
    all_gather x1, waiting for transfers between devices, body(): whole = lax.all_gather(rounded, 'vel', axis=2, tiled=True)  47.3 us
    ppermute x1, waiting for transfers between devices, extended(): after = lax.ppermute(first, axis, down)  22.6 us
    dot_general x1, matrix products, body(): jnp.dot(panel_block, local_matrix, preferred_element_type=jnp.float32)  20.3 us
    reshape x2, local copies, waits for them, and re-layouts, body(): pieces = whole.reshape(tile_len, width_y, vel_count, cell_count, piece_len)  15.5 us
    ppermute x1, waiting for transfers between devices, extended(): before = lax.ppermute(last, axis, up)  14.8 us
    reshape x1, local copies, waits for them, and re-layouts, body(): panel_block = spread.reshape(total_x * width_y, vel_count * piece_len)  9.1 us
  transfers between devices with their start and end apart: 4, of which 4 were waited for; matrix products, arithmetic and copies ran while one was open for 1% of the time, Pallas kernels for 0%

commit v1 on v0

v1 whole, which is shorter than its diff:
```python
import functools

import jax
import jax.numpy as jnp
from jax import lax
from jax.experimental import pallas as pl
from jax.experimental.pallas import tpu as pltpu
from jax.sharding import PartitionSpec as P

VG = 24
courant = 0.8
relax = 0.5
COLLISION_MAX = 0.0546875
TAIL = 16
LANES = 128
BF16 = jnp.bfloat16
F16 = jnp.float16
F32 = jnp.float32


def speeds(directions, offset, length):
    vel_index = offset + jnp.arange(length, dtype=jnp.int32)
    grid_x = vel_index // (VG * VG)
    grid_y = vel_index // VG % VG
    moving = 2 * directions - 1
    speed_x = courant * (grid_x.astype(F32) + 0.5) / VG
    speed_y = courant * (grid_y.astype(F32) - 0.5 * (VG - 1)) / VG
    return (moving, speed_x, speed_y)


def transverse(distribution, speed_y):
    width_y = distribution.shape[1]
    padded = jnp.pad(distribution, ((0, 0), (2, 2), (0, 0)))
    upward = speed_y > 0
    first_up = jnp.where(upward, padded[:, 1 : width_y + 1], padded[:, 3 : width_y + 3])
    second_up = jnp.where(upward, padded[:, 0:width_y], padded[:, 4 : width_y + 4])
    return jnp.abs(speed_y) * (1.5 * distribution - 2.0 * first_up + 0.5 * second_up)


def halo_pairs(size):
    up = [(i, i + 1) for i in range(size - 1)]
    down = [(j, i) for i, j in up]
    around = [(0, size - 1), (size - 1, 0)]
    return up, down, around


def advected(distribution, below, above, directions, wall_mask):
    tile_len, _, local_vel = distribution.shape
    moving, speed_x, speed_y = speeds(directions, lax.axis_index("vel") * local_vel, local_vel)
    padded_x = jnp.concatenate([below, distribution, above], axis=0)
    first_up = jnp.where(moving > 0, padded_x[1 : tile_len + 1], padded_x[3 : tile_len + 3])
    second_up = jnp.where(moving > 0, padded_x[0:tile_len], padded_x[4 : tile_len + 4])
    adv_x = speed_x * (1.5 * distribution - 2.0 * first_up + 0.5 * second_up)
    adv_y = transverse(distribution, speed_y)
    open_cells = (1 - wall_mask).astype(F32)[:, :, None]
    return open_cells, open_cells * (distribution - adv_x - adv_y)


def pieces_kernel(place, f_ref, keep_ref, send_ref, turned, *, cells, piece):
    chip, core = place[0], place[1]
    length = cells * piece
    peak = jnp.zeros((LANES, LANES), F32)
    for start in range(0, length, LANES):
        block = f_ref[:, start : start + LANES]
        peak = jnp.maximum(peak, jnp.abs(block))
        turned[start : start + LANES, :] = block.T.astype(BF16)
    top = jnp.max(peak, axis=(0, 1), keepdims=True) * 1.02 + 1e-30
    tail = jnp.broadcast_to(top, (TAIL, LANES)).astype(BF16)
    for q in range(cells // 2):
        other = chip ^ q
        for out, side in ((keep_ref, core), (send_ref, 1 - core)):
            at = pl.multiple_of((2 * other + side) * piece, TAIL)
            out[q, :piece, :] = turned[pl.ds(at, piece), :]
            out[q, piece:, :] = tail


def split_pieces(distribution, chip, core, cells):
    tile_len, width, local_vel = distribution.shape
    piece = local_vel // cells
    out = jax.ShapeDtypeStruct((cells // 2, piece + TAIL, LANES), BF16)
    return pl.pallas_call(
        functools.partial(pieces_kernel, cells=cells, piece=piece),
        out_shape=(out, out),
        in_specs=[pl.BlockSpec(memory_space=pltpu.SMEM), pl.BlockSpec(memory_space=pltpu.VMEM)],
        out_specs=(pl.BlockSpec(memory_space=pltpu.VMEM), pl.BlockSpec(memory_space=pltpu.VMEM)),
        scratch_shapes=[pltpu.VMEM((local_vel, LANES), BF16)],
        compiler_params=pltpu.CompilerParams(vmem_limit_bytes=24 << 20),
        cost_estimate=pl.CostEstimate(flops=local_vel * LANES, bytes_accessed=local_vel * LANES * 6, transcendentals=0),
        name="pieces",
    )(jnp.stack([chip, core]).astype(jnp.int32), distribution.reshape(tile_len * width, local_vel))


def product_kernel(vel, own, gx, gy, dx, dy, c_ref, keep_ref, send_ref, scale_ref, rows, lhs, *, piece, bound):
    slots = own.shape[0]

    @pl.when(pl.program_id(0) == 0)
    def _():
        for s in range(slots):
            for side in range(2):
                diagonal = dx if side == 0 else dy
                parts = ((0, own.at[s, side]), (1, gx.at[s, side]), (2, gy.at[s, side]), (3, diagonal.at[s]))
                top = jnp.zeros((TAIL, LANES), F32)
                for q, part in parts:
                    at = pl.multiple_of((vel[0] ^ q) * piece, TAIL)
                    rows[pl.ds(at, piece), :] = part[:piece, :]
                    top = jnp.maximum(top, part[piece:, :].astype(F32))
                lhs[(2 * s + side) * LANES : (2 * s + side + 1) * LANES, :] = rows[...].T
                scale_ref[s, side] = bound / top[:8, :]

    for s in range(slots):
        out = jnp.dot(lhs[2 * s * LANES : 2 * (s + 1) * LANES, :], c_ref[...], preferred_element_type=F32)
        keep_ref[s] = out[:LANES] * scale_ref[s, 0, 0:1, 0:1]
        send_ref[s] = out[LANES:] * scale_ref[s, 1, 0:1, 0:1]


def product(vel, own, gx, gy, dx, dy, matrix, block):
    slots = own.shape[0]
    piece = own.shape[2] - TAIL
    depth, columns = matrix.shape
    total = columns * 4
    whole = lambda a: pl.BlockSpec(a.shape, lambda n: (0,) * a.ndim)
    out = jax.ShapeDtypeStruct((slots, LANES, columns), F32)
    out_spec = pl.BlockSpec((slots, LANES, block), lambda n: (0, 0, n))
    return pl.pallas_call(
        functools.partial(product_kernel, piece=piece, bound=60000.0 / (total * COLLISION_MAX)),
        grid=(columns // block,),
        out_shape=(out, out, jax.ShapeDtypeStruct((slots, 2, 8, LANES), F32)),
        in_specs=[pl.BlockSpec(memory_space=pltpu.SMEM)]
        + [whole(a) for a in (own, gx, gy, dx, dy)]
        + [pl.BlockSpec((depth, block), lambda n: (0, n))],
        out_specs=(out_spec, out_spec, pl.BlockSpec((slots, 2, 8, LANES), lambda n: (0, 0, 0, 0))),
        scratch_shapes=[pltpu.VMEM((depth, LANES), BF16), pltpu.VMEM((slots * 2 * LANES, depth), BF16)],
        compiler_params=pltpu.CompilerParams(vmem_limit_bytes=40 << 20),
        cost_estimate=pl.CostEstimate(
            flops=2 * slots * 2 * LANES * depth * columns,
            bytes_accessed=depth * columns * 2 + slots * 2 * LANES * columns * 4,
            transcendentals=0,
        ),
        name="product",
    )(jnp.reshape(vel, (1,)).astype(jnp.int32), own, gx, gy, dx, dy, matrix)


def after(value, *earlier):
    return lax.optimization_barrier((value,) + earlier)[0]


def chain_body(distribution, collision, directions, wall_mask):
    tile_len, width, local_vel = distribution.shape
    cells = lax.axis_size("cell")
    cell = lax.axis_index("cell")
    vel = lax.axis_index("vel")
    chip, core = cell // 2, cell % 2
    matrix = collision.reshape(-1, local_vel)

    up, down, around = halo_pairs(cells)
    head, foot = distribution[:2], distribution[tile_len - 2 :]
    from_below = lax.ppermute(foot, "cell", up)
    from_above = lax.ppermute(head, "cell", down)

    other_core = [(i, i ^ 1) for i in range(cells)]
    across = lambda q: [(i, 2 * ((i // 2) ^ q) + i % 2) for i in range(cells)]
    in_x = [(i, i ^ 1) for i in range(4)]
    in_y = [(i, i ^ 2) for i in range(4)]
    chips = lambda *pairs: [(2 * a + c, 2 * b + c) for a, b in pairs for c in range(2)]
    ends = chips((0, 1), (3, 2))
    middle = chips((1, 2), (2, 1))
    outward = chips((2, 3), (1, 0))

    keep, send = split_pieces(distribution, chip, core, cells)
    got = lax.ppermute(send, "cell", other_core)
    both = [jnp.stack([keep[q], got[q]])[None] for q in range(4)]

    def gathered(own):
        gx = lax.ppermute(own, "vel", in_x)
        gy = lax.ppermute(own, "vel", in_y)
        dx = lax.ppermute(gx[:, 0], "vel", in_y)
        dy = lax.ppermute(gy[:, 1], "vel", in_x)
        return own, gx, gy, dx, dy

    def partial(parts):
        mine, theirs, scale = product(vel, *parts, matrix, 384)
        return mine, lax.ppermute(theirs, "cell", other_core), scale

    z3 = lax.ppermute(both[3], "cell", across(3))
    g0 = gathered(both[0])
    z2 = lax.ppermute(after(both[2], z3), "cell", across(2))
    z1 = lax.ppermute(after(both[1], z3), "cell", across(1))
    g3 = gathered(z3)
    wrapping = jnp.where(cell == 0, head, foot)
    from_around = lax.ppermute(after(wrapping, z2, z1), "cell", around)
    mine3, theirs3, _ = partial(g3)
    p3 = (mine3 + theirs3)[0]
    a0 = lax.ppermute(p3.astype(F16), "cell", ends)
    g2 = gathered(after(z2, g3[3], g3[4]))
    mine2, theirs2, _ = partial(g2)
    p2 = (mine2 + theirs2)[0]
    a1 = lax.ppermute(after(p2.astype(F16), a0), "cell", ends)
    b1 = lax.ppermute((p2 + a0.astype(F32)).astype(F16), "cell", middle)
    g1 = gathered(after(z1, g2[3], g2[4]))
    mine1, theirs1, _ = partial(g1)
    p1 = (mine1 + theirs1)[0]
    a2 = lax.ppermute(after(p1.astype(F16), a1), "cell", ends)
    b2 = lax.ppermute((p3 + a1.astype(F32)).astype(F16), "cell", middle)
    c2 = lax.ppermute((p1 + b1.astype(F32)).astype(F16), "cell", outward)
    mine0, theirs0, scale = partial(g0)

    below = jnp.where(cell == 0, from_around, from_below)
    above = jnp.where(cell == cells - 1, from_around, from_above)
    open_cells, base = advected(distribution, below, above, directions, wall_mask)
    shape = distribution.shape
    rest = (mine0 + theirs0).reshape(shape)
    arrived = (a2.astype(F32) + b2.astype(F32) + c2.astype(F32)).reshape(shape)
    return base + open_cells * (relax / scale[0, 0, 0, 0]) * (rest + arrived)


def plain_body(distribution, collision, directions, wall_mask):
    tile_len, width, local_vel = distribution.shape
    cells = lax.axis_size("cell")
    vels = lax.axis_size("vel")
    cell = lax.axis_index("cell")
    piece = local_vel // cells
    up, down, around = halo_pairs(cells)
    head, foot = distribution[:2], distribution[tile_len - 2 :]
    from_around = lax.ppermute(jnp.where(cell == 0, head, foot), "cell", around)
    below = jnp.where(cell == 0, from_around, lax.ppermute(foot, "cell", up))
    above = jnp.where(cell == cells - 1, from_around, lax.ppermute(head, "cell", down))
    open_cells, base = advected(distribution, below, above, directions, wall_mask)
    pieces = distribution.astype(BF16).reshape(tile_len * width, cells, piece)
    spread = lax.all_to_all(pieces, "cell", split_axis=1, concat_axis=0, tiled=True)
    panel = lax.all_gather(spread.reshape(-1, piece), "vel", axis=1, tiled=True)
    part = jnp.dot(panel, collision.reshape(vels * piece, local_vel), preferred_element_type=F32)
    gain = lax.psum_scatter(part, "cell", scatter_dimension=0, tiled=True)
    return base + open_cells * relax * gain.reshape(distribution.shape)


def body(distribution, collision, directions, wall_mask):
    tile_len, width, local_vel = distribution.shape
    cells = lax.axis_size("cell")
    piece = local_vel // cells
    fits = tile_len * width == LANES and piece % TAIL == 0 and local_vel % (3 * LANES) == 0
    if cells == 8 and lax.axis_size("vel") == 4 and fits:
        return chain_body(distribution, collision, directions, wall_mask)
    return plain_body(distribution, collision, directions, wall_mask)


def solution(mesh):
    in_specs = (P("cell", None, "vel"), P(None, "cell", None, "vel"), P("vel"), P("cell", None))
    out_specs = P("cell", None, "vel")
    return jax.shard_map(body, mesh=mesh, in_specs=in_specs, out_specs=out_specs, check_vma=False)
```

time: 378 us -> 225 us (0.60)
  waiting for transfers between devices: 204 us -> 85.7 us
  blocking collectives: 98.5 us -> 0 us
  starting transfers between devices: 1.51 us -> 81.3 us
  Pallas kernels: 0 us -> 44.7 us
  local copies, waits for them, and re-layouts: 28.7 us -> 3.19 us
  matrix products: 20.3 us -> 0 us
  between operations: 13.5 us -> 1.05 us
    reduce_scatter x1 -> x0, waiting for transfers between devices: 119 us -> none  [body(): lax.psum_scatter(jnp.dot(panel_block, local_matrix, preferred_element_typ...]
    all_to_all x1 -> x0, blocking collectives: 98.5 us -> none  [body(): lax.all_to_all(pieces, 'cell', split_axis=3, concat_axis=0, tiled=True)]
    ppermute x2 -> x33, starting transfers between devices: 1.47 us -> 81.3 us  [the longest x1 24.3 us: chain_body(): a2 = lax.ppermute(after(p1.astype(F16), a1), 'cell', ends)]
    ppermute x2 -> x33, waiting for transfers between devices: 37.3 us -> 85.7 us  [the longest x1 32.2 us: chain_body(): a0 = lax.ppermute(p3.astype(F16), 'cell', ends)]
    all_gather x1 -> x0, waiting for transfers between devices: 47.3 us -> none  [body(): whole = lax.all_gather(rounded, 'vel', axis=2, tiled=True)]
    pallas_call x0 -> x5, Pallas kernels: none -> 44.7 us  [the longest x4 43.7 us: product(): pl.pallas_call(functools.partial(product_kernel, piece=piece, bound=60000...]
    reshape x3 -> x0, local copies, waits for them, and re-layouts: 24.6 us -> none  [the longest x2 15.5 us: body(): pieces = whole.reshape(tile_len, width_y, vel_count, cell_count, piece_len)]
    dot_general x1 -> x0, matrix products: 20.3 us -> none  [body(): jnp.dot(panel_block, local_matrix, preferred_element_type=jnp.float32)]
  transfers between devices with their start and end apart: 4 -> 33, of which waited for: 4 -> 11; matrix products, arithmetic and copies ran while one was open for 1% -> 2% of each run, Pallas kernels for 0% -> 20%
where the time goes in v1:
time: 225 us; the launch traced here: 224 us
  waiting for transfers between devices  85.7 us (38%)
  starting transfers between devices  81.3 us (36%)
  Pallas kernels  44.7 us (20%)
  other arithmetic  7.83 us (3%)
  local copies, waits for them, and re-layouts  3.19 us (1%)
    pallas_call x4, Pallas kernels, product(): pl.pallas_call(functools.partial(product_kernel, piece=piece, bound=60000...  43.7 us
    ppermute x1, waiting for transfers between devices, chain_body(): a0 = lax.ppermute(p3.astype(F16), 'cell', ends)  32.2 us
    ppermute x1, starting transfers between devices, chain_body(): a2 = lax.ppermute(after(p1.astype(F16), a1), 'cell', ends)  24.3 us
    ppermute x1, waiting for transfers between devices, chain_body(): a2 = lax.ppermute(after(p1.astype(F16), a1), 'cell', ends)  13.8 us
    ppermute x4, starting transfers between devices, partial(): return (mine, lax.ppermute(theirs, 'cell', other_core), scale)  11.4 us
    ppermute x4, waiting for transfers between devices, gathered(): gy = lax.ppermute(own, 'vel', in_y)  10.5 us
    ppermute x1, waiting for transfers between devices, chain_body(): a1 = lax.ppermute(after(p2.astype(F16), a0), 'cell', ends)  10.1 us
    ppermute x4, starting transfers between devices, gathered(): gx = lax.ppermute(own, 'vel', in_x)  6.09 us
  transfers between devices with their start and end apart: 33, of which 11 were waited for; matrix products, arithmetic and copies ran while one was open for 2% of the time, Pallas kernels for 20%

profile of v1, /device:TPU:0, one launch (start us, length us, event | category | flops | bytes accessed | tf_op | source)
XLA Modules:
  0.0 223.8 jit_solution(11600153864515740161)
XLA Ops:
  0.0 0.1 pad_add_fusion.place
  0.1 1.5 copy-done
  1.6 1.1 pieces.1
  2.6 0.5 collective-permute-start
  3.2 1.6 fusion.33
  4.8 3.1 %collective-permute-start.5 = (f32[2,32,3456]{2,1,0:T(8,128)}, f32[2,32,3456]{2,1,0:T(8,128)}, u32[]{:S(2)}, u32[]{:S(2)}) collective-permute-start(f32[2,32,3456]{2,1,0:T(8,128)} %get-tuple-element.41), channel_id=1, source_target_pairs={{0,1},{1,2},{2,3},{3,4},{4,5},{5,6},{6,7},{8,9},{9,10},{10,11},{11... | collective-permute-start | bytes 2654216 | tf_op jit(solution)/shard_map/ppermute | solution.py:157
  8.1 4.0 %collective-permute-start.1 = (bf16[1,2,448,128]{3,2,1,0:T(8,128)(2,1)S(1)}, bf16[1,2,448,128]{3,2,1,0:T(8,128)(2,1)S(1)}, u32[]{:S(2)}, u32[]{:S(2)}) collective-permute-start(bf16[1,2,448,128]{3,2,1,0:T(8,128)(2,1)S(1)} %maximum_bitcast_fusion.1), channel_id=1, source_target_pairs={{0,6},{1,7},{2,4},{3,5},{4,2},{5,3},{6,0},{7,1},{8,14},{9,15},{10,... | collective-permute-start | bytes 688136 | tf_op jit(solution)/shard_map/ppermute | solution.py:184
  12.1 1.6 collective-permute-start.8
  13.7 1.6 collective-permute-start.7
  15.3 2.8 %collective-permute-done.1.own = bf16[1,2,448,128]{3,2,1,0:T(8,128)(2,1)S(1)} collective-permute-done((bf16[1,2,448,128]{3,2,1,0:T(8,128)(2,1)S(1)}, bf16[1,2,448,128]{3,2,1,0:T(8,128)(2,1)S(1)}, u32[]{:S(2)}, u32[]{:S(2)}) %collective-permute-start.1) | collective-permute-done | bytes 229408 | tf_op jit(solution)/shard_map/ppermute | solution.py:184
  18.1 3.8 %collective-permute-start.2 = (bf16[1,2,448,128]{3,2,1,0:T(8,128)(2,1)S(1)}, bf16[1,2,448,128]{3,2,1,0:T(8,128)(2,1)S(1)}, u32[]{:S(2)}, u32[]{:S(2)}) collective-permute-start(bf16[1,2,448,128]{3,2,1,0:T(8,128)(2,1)S(1)} %get-tuple-element.25), channel_id=1, source_target_pairs={{0,4},{1,5},{2,6},{3,7},{4,0},{5,1},{6,2},{7,3},{8,12},{9,13},{10,... | collective-permute-start | bytes 688136 | tf_op jit(solution)/shard_map/ppermute | solution.py:186
  22.0 1.0 collective-permute-start.3
  23.0 0.0 collective-permute-done.8.gy
  23.0 1.5 collective-permute-start.12
  24.5 4.5 %collective-permute-done.12.gx = bf16[1,2,448,128]{3,2,1,0:T(8,128)(2,1)S(1)} collective-permute-done((bf16[1,2,448,128]{3,2,1,0:T(8,128)(2,1)S(1)}, bf16[1,2,448,128]{3,2,1,0:T(8,128)(2,1)S(1)}, u32[]{:S(2)}, u32[]{:S(2)}) %collective-permute-start.12) | collective-permute-done | bytes 229408 | tf_op jit(solution)/shard_map/ppermute | solution.py:174
  29.0 1.5 collective-permute-start.14
  30.6 4.5 %collective-permute-done.14.gy = bf16[1,2,448,128]{3,2,1,0:T(8,128)(2,1)S(1)} collective-permute-done((bf16[1,2,448,128]{3,2,1,0:T(8,128)(2,1)S(1)}, bf16[1,2,448,128]{3,2,1,0:T(8,128)(2,1)S(1)}, u32[]{:S(2)}, u32[]{:S(2)}) %collective-permute-start.14) | collective-permute-done | bytes 229408 | tf_op jit(solution)/shard_map/ppermute | solution.py:175
  35.0 1.5 collective-permute-start.13
  36.6 0.0 collective-permute-done.7.gx
  36.6 1.6 collective-permute-start.15
  38.2 0.6 collective-permute-start.10
  38.8 1.1 collective-permute-done.13.dx
  39.8 1.5 collective-permute-start.9
  41.4 1.1 collective-permute-done.15.dy
  42.5 1.5 collective-permute-start.16
  44.0 11.1 %product.7 = (f32[1,128,3456]{2,1,0:T(8,128)S(1)}, f32[1,128,3456]{2,1,0:T(8,128)S(1)}, f32[1,2,8,128]{3,2,1,0:T(8,128)}) custom-call(s32[1]{0:T(128)} %bitcast.6.vel, bf16[1,2,448,128]{3,2,1,0:T(8,128)(2,1)S(1)} %collective-permute-done.1.own, bf16[1,2,448,128]{3,2,1,0:T(8,128)(2,1)S(1)} %collective-permute-done.12.gx, ...), custom_call_target="tpu_custom_call" | custom-call | flops 3057647616 | bytes 15482880 | tf_op jit(solution)/shard_map/product/pallas_call | solution.py:124
  55.1 6.0 %collective-permute-done.18.gy = bf16[1,2,448,128]{3,2,1,0:T(8,128)(2,1)S(1)} collective-permute-done((bf16[1,2,448,128]{3,2,1,0:T(8,128)(2,1)S(1)}, bf16[1,2,448,128]{3,2,1,0:T(8,128)(2,1)S(1)}, u32[]{:S(2)}, u32[]{:S(2)}) %collective-permute-start.18) | collective-permute-done | bytes 229408 | tf_op jit(solution)/shard_map/ppermute | solution.py:175
  61.1 10.2 %collective-permute-start.26 = (f32[1,128,3456]{2,1,0:T(8,128)S(1)}, f32[1,128,3456]{2,1,0:T(8,128)S(1)}, u32[]{:S(2)}, u32[]{:S(2)}) collective-permute-start(f32[1,128,3456]{2,1,0:T(8,128)S(1)} %get-tuple-element.38), channel_id=1, source_target_pairs={{0,1},{1,0},{2,3},{3,2},{4,5},{5,4},{6,7},{7,6},{8,9},{9,8},{10,11... | collective-permute-start | bytes 5308424 | tf_op jit(solution)/shard_map/ppermute | solution.py:182
  71.3 1.4 collective-permute-start.17
  72.7 0.5 collective-permute-start.19
  73.2 10.5 %product.4 = (f32[1,128,3456]{2,1,0:T(8,128)S(1)}, f32[1,128,3456]{2,1,0:T(8,128)S(1)}, f32[1,2,8,128]{3,2,1,0:T(8,128)S(1)}) custom-call(s32[1]{0:T(128)} %bitcast.6.vel, bf16[1,2,448,128]{3,2,1,0:T(8,128)(2,1)S(1)} %maximum_bitcast_fusion.3.own, bf16[1,2,448,128]{3,2,1,0:T(8,128)(2,1)S(1)} %collective-permute-done.7.gx, ...), custom_call_target="tpu_custom_call" | custom-call | flops 3057647616 | bytes 15482880 | tf_op jit(solution)/shard_map/product/pallas_call | solution.py:124
  83.7 0.6 slice.105
  85.0 1.6 collective-permute-start.20
  86.5 0.7 collective-permute-start.21
  87.3 11.1 %product.6 = (f32[1,128,3456]{2,1,0:T(8,128)S(1)}, f32[1,128,3456]{2,1,0:T(8,128)S(1)}, f32[1,2,8,128]{3,2,1,0:T(8,128)}) custom-call(s32[1]{0:T(128)} %bitcast.6.vel, bf16[1,2,448,128]{3,2,1,0:T(8,128)(2,1)S(1)} %collective-permute-done.2.own, bf16[1,2,448,128]{3,2,1,0:T(8,128)(2,1)S(1)} %collective-permute-done.16.gx, ...), custom_call_target="tpu_custom_call" | custom-call | flops 3057647616 | bytes 15482880 | tf_op jit(solution)/shard_map/product/pallas_call | solution.py:124
  98.3 1.4 collective-permute-start.22
  99.7 0.6 collective-permute-start.23
  100.3 3.6 %collective-permute-done.22.dx = bf16[1,448,128]{2,1,0:T(8,128)(2,1)S(1)} collective-permute-done((bf16[1,448,128]{2,1,0:T(8,128)(2,1)S(1)}, bf16[1,448,128]{2,1,0:T(8,128)(2,1)S(1)}, u32[]{:S(2)}, u32[]{:S(2)}) %collective-permute-start.22) | collective-permute-done | bytes 114720 | tf_op jit(solution)/shard_map/ppermute | solution.py:176
  104.0 1.3 collective-permute-start.6
  105.3 1.2 collective-permute-start.11
  106.5 11.1 %product.5 = (f32[1,128,3456]{2,1,0:T(8,128)S(1)}, f32[1,128,3456]{2,1,0:T(8,128)S(1)}, f32[1,2,8,128]{3,2,1,0:T(8,128)}) custom-call(s32[1]{0:T(128)} %bitcast.6.vel, bf16[1,2,448,128]{3,2,1,0:T(8,128)(2,1)S(1)} %collective-permute-done.3.own, bf16[1,2,448,128]{3,2,1,0:T(8,128)(2,1)S(1)} %collective-permute-done.20.gx, ...), custom_call_target="tpu_custom_call" | custom-call | flops 3057647616 | bytes 15482880 | tf_op jit(solution)/shard_map/product/pallas_call | solution.py:124
  117.5 0.0 collective-permute-start.24
  117.6 0.2 bitcast_convert_fusion
  117.7 1.0 copy-done.2
  118.7 4.3 %collective-permute-start.4 = (f32[2,32,3456]{2,1,0:T(8,128)S(1)}, f32[2,32,3456]{2,1,0:T(8,128)S(1)}, u32[]{:S(2)}, u32[]{:S(2)}) collective-permute-start(f32[2,32,3456]{2,1,0:T(8,128)S(1)} %copy-done.2), channel_id=1, source_target_pairs={{0,7},{7,0},{8,15},{15,8},{16,23},{23,16},{24,31},{31,24}} | collective-permute-start | bytes 2654216 | tf_op jit(solution)/shard_map/ppermute | solution.py:190
  123.1 0.2 bitcast_convert_fusion.1
  123.3 1.3 collective-permute-start.27
  124.6 0.2 bitcast_convert_fusion.2
  124.9 32.2 %collective-permute-done.27 = f16[128,3456]{1,0:T(8,128)(2,1)S(1)} collective-permute-done((f16[128,3456]{1,0:T(8,128)(2,1)S(1)}, f16[128,3456]{1,0:T(8,128)(2,1)S(1)}, u32[]{:S(2)}, u32[]{:S(2)}) %collective-permute-start.27) | collective-permute-done | bytes 884768 | tf_op jit(solution)/shard_map/ppermute | solution.py:193
  157.0 4.4 %collective-permute-start.28 = (f16[128,3456]{1,0:T(8,128)(2,1)S(1)}, f16[128,3456]{1,0:T(8,128)(2,1)S(1)}, u32[]{:S(2)}, u32[]{:S(2)}) collective-permute-start(f16[128,3456]{1,0:T(8,128)(2,1)S(1)} %bitcast_convert_fusion.1), channel_id=1, source_target_pairs={{0,2},{1,3},{6,4},{7,5},{8,10},{9,11},{14,12},{15,13},{16,18},{17,... | collective-permute-start | bytes 2654216 | tf_op jit(solution)/shard_map/ppermute | solution.py:197
  161.5 0.4 fusion.21
  161.9 10.1 %collective-permute-done.28 = f16[128,3456]{1,0:T(8,128)(2,1)S(1)} collective-permute-done((f16[128,3456]{1,0:T(8,128)(2,1)S(1)}, f16[128,3456]{1,0:T(8,128)(2,1)S(1)}, u32[]{:S(2)}, u32[]{:S(2)}) %collective-permute-start.28) | collective-permute-done | bytes 884768 | tf_op jit(solution)/shard_map/ppermute | solution.py:197
  172.0 0.7 collective-permute-start.31
  172.7 0.4 fusion.20
  173.1 24.3 %collective-permute-start.29 = (f16[128,3456]{1,0:T(8,128)(2,1)S(1)}, f16[128,3456]{1,0:T(8,128)(2,1)S(1)}, u32[]{:S(2)}, u32[]{:S(2)}) collective-permute-start(f16[128,3456]{1,0:T(8,128)(2,1)S(1)} %bitcast_convert_fusion.2), channel_id=1, source_target_pairs={{0,2},{1,3},{6,4},{7,5},{8,10},{9,11},{14,12},{15,13},{16,18},{17,... | collective-permute-start | bytes 2654216 | tf_op jit(solution)/shard_map/ppermute | solution.py:202
  197.4 0.4 fusion.22
  197.8 0.7 collective-permute-start.30
  198.5 1.3 collective-permute-start.32
  199.8 0.2 broadcast_select_fusion.1
  200.0 0.2 add.103
  200.2 13.8 %collective-permute-done.29 = f16[128,3456]{1,0:T(8,128)(2,1)S(1)} collective-permute-done((f16[128,3456]{1,0:T(8,128)(2,1)S(1)}, f16[128,3456]{1,0:T(8,128)(2,1)S(1)}, u32[]{:S(2)}, u32[]{:S(2)}) %collective-permute-start.29) | collective-permute-done | bytes 884768 | tf_op jit(solution)/shard_map/ppermute | solution.py:202
  214.0 5.9 %collective-permute-done.32 = f16[128,3456]{1,0:T(8,128)(2,1)S(1)} collective-permute-done((f16[128,3456]{1,0:T(8,128)(2,1)S(1)}, f16[128,3456]{1,0:T(8,128)(2,1)S(1)}, u32[]{:S(2)}, u32[]{:S(2)}) %collective-permute-start.32) | collective-permute-done | bytes 884768 | tf_op jit(solution)/shard_map/ppermute | solution.py:204
  219.9 0.3 convert_add_fusion
  220.2 3.6 %fusion.7 = f32[4,32,3456]{2,1,0:T(8,128)} fusion(f32[4,32,3456]{2,1,0:T(8,128)S(1)} %copy-done.1, f32[2,32,3456]{2,1,0:T(8,128)S(1)} %get-tuple-element.45, f32[2,32,3456]{2,1,0:T(8,128)S(1)} %get-tuple-element.44, f32[4,32,3456]{2,1,0:T(8,128)S(1)} %bitcast.53, f32[4,32,3456]{2,1,0:T(8,128)S(1)} %bitcast.52, f32[4,32]{1,0:T(4,128)S(1)} %broadcast_multiply_fusion, ...), kind=kLoop, calls=%fused_computation.15 | loop fusion | flops 11059200 | bytes 8882944 | tf_op jit(solution)/shard_map/add | solution.py:213
  (50 shorter events, 0.4 us)
Async XLA Ops:
  0.1 1.5 copy-start
  1.6 1.6 copy-start.1
  2.6 5.4 %collective-permute-start = (bf16[4,448,128]{2,1,0:T(8,128)(2,1)S(1)}, bf16[4,448,128]{2,1,0:T(8,128)(2,1)S(1)}, u32[]{:S(2)}, u32[]{:S(2)}) collective-permute-start(bf16[4,448,128]{2,1,0:T(8,128)(2,1)S(1)} %get-tuple-element.24), channel_id=1, source_target_pairs={{0,1},{1,0},{2,3},{3,2},{4,5},{5,4},{6,7},{7,6},{8,9},{9,8},{10,11... | collective-permute-start | bytes 1376264 | tf_op jit(solution)/shard_map/ppermute | solution.py:170
  3.2 4.8 %copy-start.4 = (s32[3456]{0:T(1024)S(1)}, s32[3456]{0:T(1024)}, u32[]{:S(2)}) copy-start(s32[3456]{0:T(1024)} %param.6) | copy-start | bytes 41476
  3.2 4.8 %copy-start.5 = (s32[4,32]{1,0:T(4,128)S(1)}, s32[4,32]{1,0:T(4,128)}, u32[]{:S(2)}) copy-start(s32[4,32]{1,0:T(4,128)} %param.7) | copy-start | bytes 1540
  4.8 193.0 %collective-permute-start.5 = (f32[2,32,3456]{2,1,0:T(8,128)}, f32[2,32,3456]{2,1,0:T(8,128)}, u32[]{:S(2)}, u32[]{:S(2)}) collective-permute-start(f32[2,32,3456]{2,1,0:T(8,128)} %get-tuple-element.41), channel_id=1, source_target_pairs={{0,1},{1,2},{2,3},{3,4},{4,5},{5,6},{6,7},{8,9},{9,10},{10,11},{11... | collective-permute-start | bytes 2654216 | tf_op jit(solution)/shard_map/ppermute | solution.py:157
  8.1 10.0 %collective-permute-start.1 = (bf16[1,2,448,128]{3,2,1,0:T(8,128)(2,1)S(1)}, bf16[1,2,448,128]{3,2,1,0:T(8,128)(2,1)S(1)}, u32[]{:S(2)}, u32[]{:S(2)}) collective-permute-start(bf16[1,2,448,128]{3,2,1,0:T(8,128)(2,1)S(1)} %maximum_bitcast_fusion.1), channel_id=1, source_target_pairs={{0,6},{1,7},{2,4},{3,5},{4,2},{5,3},{6,0},{7,1},{8,14},{9,15},{10,... | collective-permute-start | bytes 688136 | tf_op jit(solution)/shard_map/ppermute | solution.py:184
  12.1 10.9 %collective-permute-start.8 = (bf16[1,2,448,128]{3,2,1,0:T(8,128)(2,1)S(1)}, bf16[1,2,448,128]{3,2,1,0:T(8,128)(2,1)S(1)}, u32[]{:S(2)}, u32[]{:S(2)}) collective-permute-start(bf16[1,2,448,128]{3,2,1,0:T(8,128)(2,1)S(1)} %maximum_bitcast_fusion.3.own), channel_id=1, source_target_pairs={{0,16},{8,24},{16,0},{24,8},{1,17},{9,25},{17,1},{25,9},{2,18},{10... | collective-permute-start | bytes 688136 | tf_op jit(solution)/shard_map/ppermute | solution.py:175
  13.7 22.8 %collective-permute-start.7 = (bf16[1,2,448,128]{3,2,1,0:T(8,128)(2,1)S(1)}, bf16[1,2,448,128]{3,2,1,0:T(8,128)(2,1)S(1)}, u32[]{:S(2)}, u32[]{:S(2)}) collective-permute-start(bf16[1,2,448,128]{3,2,1,0:T(8,128)(2,1)S(1)} %maximum_bitcast_fusion.3.own), channel_id=1, source_target_pairs={{0,8},{8,0},{16,24},{24,16},{1,9},{9,1},{17,25},{25,17},{2,10},{10... | collective-permute-start | bytes 688136 | tf_op jit(solution)/shard_map/ppermute | solution.py:174
  18.1 20.0 %collective-permute-start.2 = (bf16[1,2,448,128]{3,2,1,0:T(8,128)(2,1)S(1)}, bf16[1,2,448,128]{3,2,1,0:T(8,128)(2,1)S(1)}, u32[]{:S(2)}, u32[]{:S(2)}) collective-permute-start(bf16[1,2,448,128]{3,2,1,0:T(8,128)(2,1)S(1)} %get-tuple-element.25), channel_id=1, source_target_pairs={{0,4},{1,5},{2,6},{3,7},{4,0},{5,1},{6,2},{7,3},{8,12},{9,13},{10,... | collective-permute-start | bytes 688136 | tf_op jit(solution)/shard_map/ppermute | solution.py:186
  22.0 63.0 %collective-permute-start.3 = (bf16[1,2,448,128]{3,2,1,0:T(8,128)(2,1)S(1)}, bf16[1,2,448,128]{3,2,1,0:T(8,128)(2,1)S(1)}, u32[]{:S(2)}, u32[]{:S(2)}) collective-permute-start(bf16[1,2,448,128]{3,2,1,0:T(8,128)(2,1)S(1)} %get-tuple-element.26), channel_id=1, source_target_pairs={{0,2},{1,3},{2,0},{3,1},{4,6},{5,7},{6,4},{7,5},{8,10},{9,11},{10,... | collective-permute-start | bytes 688136 | tf_op jit(solution)/shard_map/ppermute | solution.py:187
  23.0 6.0 %collective-permute-start.12 = (bf16[1,2,448,128]{3,2,1,0:T(8,128)(2,1)S(1)}, bf16[1,2,448,128]{3,2,1,0:T(8,128)(2,1)S(1)}, u32[]{:S(2)}, u32[]{:S(2)}) collective-permute-start(bf16[1,2,448,128]{3,2,1,0:T(8,128)(2,1)S(1)} %collective-permute-done.1.own), channel_id=1, source_target_pairs={{0,8},{8,0},{16,24},{24,16},{1,9},{9,1},{17,25},{25,17},{2,10},{10... | collective-permute-start | bytes 688136 | tf_op jit(solution)/shard_map/ppermute | solution.py:174
  29.0 6.0 %collective-permute-start.14 = (bf16[1,2,448,128]{3,2,1,0:T(8,128)(2,1)S(1)}, bf16[1,2,448,128]{3,2,1,0:T(8,128)(2,1)S(1)}, u32[]{:S(2)}, u32[]{:S(2)}) collective-permute-start(bf16[1,2,448,128]{3,2,1,0:T(8,128)(2,1)S(1)} %collective-permute-done.1.own), channel_id=1, source_target_pairs={{0,16},{8,24},{16,0},{24,8},{1,17},{9,25},{17,1},{25,9},{2,18},{10... | collective-permute-start | bytes 688136 | tf_op jit(solution)/shard_map/ppermute | solution.py:175
  35.0 4.8 %collective-permute-start.13 = (bf16[1,448,128]{2,1,0:T(8,128)(2,1)S(1)}, bf16[1,448,128]{2,1,0:T(8,128)(2,1)S(1)}, u32[]{:S(2)}, u32[]{:S(2)}) collective-permute-start(bf16[1,448,128]{2,1,0:T(8,128)(2,1)S(1)} %slice_bitcast_fusion.5), channel_id=1, source_target_pairs={{0,16},{8,24},{16,0},{24,8},{1,17},{9,25},{17,1},{25,9},{2,18},{10... | collective-permute-start | bytes 344072 | tf_op jit(solution)/shard_map/ppermute | solution.py:176
  36.6 5.9 %collective-permute-start.15 = (bf16[1,448,128]{2,1,0:T(8,128)(2,1)S(1)}, bf16[1,448,128]{2,1,0:T(8,128)(2,1)S(1)}, u32[]{:S(2)}, u32[]{:S(2)}) collective-permute-start(bf16[1,448,128]{2,1,0:T(8,128)(2,1)S(1)} %slice_bitcast_fusion.4), channel_id=1, source_target_pairs={{0,8},{8,0},{16,24},{24,16},{1,9},{9,1},{17,25},{25,17},{2,10},{10... | collective-permute-start | bytes 344072 | tf_op jit(solution)/shard_map/ppermute | solution.py:177
  38.2 33.1 %collective-permute-start.10 = (bf16[1,448,128]{2,1,0:T(8,128)(2,1)S(1)}, bf16[1,448,128]{2,1,0:T(8,128)(2,1)S(1)}, u32[]{:S(2)}, u32[]{:S(2)}) collective-permute-start(bf16[1,448,128]{2,1,0:T(8,128)(2,1)S(1)} %slice_bitcast_fusion.6), channel_id=1, source_target_pairs={{0,8},{8,0},{16,24},{24,16},{1,9},{9,1},{17,25},{25,17},{2,10},{10... | collective-permute-start | bytes 344072 | tf_op jit(solution)/shard_map/ppermute | solution.py:177
  39.8 32.8 %collective-permute-start.9 = (bf16[1,448,128]{2,1,0:T(8,128)(2,1)S(1)}, bf16[1,448,128]{2,1,0:T(8,128)(2,1)S(1)}, u32[]{:S(2)}, u32[]{:S(2)}) collective-permute-start(bf16[1,448,128]{2,1,0:T(8,128)(2,1)S(1)} %slice_bitcast_fusion.7), channel_id=1, source_target_pairs={{0,16},{8,24},{16,0},{24,8},{1,17},{9,25},{17,1},{25,9},{2,18},{10... | collective-permute-start | bytes 344072 | tf_op jit(solution)/shard_map/ppermute | solution.py:176
  42.5 12.5 %collective-permute-start.16 = (bf16[1,2,448,128]{3,2,1,0:T(8,128)(2,1)S(1)}, bf16[1,2,448,128]{3,2,1,0:T(8,128)(2,1)S(1)}, u32[]{:S(2)}, u32[]{:S(2)}) collective-permute-start(bf16[1,2,448,128]{3,2,1,0:T(8,128)(2,1)S(1)} %collective-permute-done.2.own), channel_id=1, source_target_pairs={{0,8},{8,0},{16,24},{24,16},{1,9},{9,1},{17,25},{25,17},{2,10},{10... | collective-permute-start | bytes 688136 | tf_op jit(solution)/shard_map/ppermute | solution.py:174
  55.0 6.0 %collective-permute-start.18 = (bf16[1,2,448,128]{3,2,1,0:T(8,128)(2,1)S(1)}, bf16[1,2,448,128]{3,2,1,0:T(8,128)(2,1)S(1)}, u32[]{:S(2)}, u32[]{:S(2)}) collective-permute-start(bf16[1,2,448,128]{3,2,1,0:T(8,128)(2,1)S(1)} %collective-permute-done.2.own), channel_id=1, source_target_pairs={{0,16},{8,24},{16,0},{24,8},{1,17},{9,25},{17,1},{25,9},{2,18},{10... | collective-permute-start | bytes 688136 | tf_op jit(solution)/shard_map/ppermute | solution.py:175
  61.1 56.5 %collective-permute-start.26 = (f32[1,128,3456]{2,1,0:T(8,128)S(1)}, f32[1,128,3456]{2,1,0:T(8,128)S(1)}, u32[]{:S(2)}, u32[]{:S(2)}) collective-permute-start(f32[1,128,3456]{2,1,0:T(8,128)S(1)} %get-tuple-element.38), channel_id=1, source_target_pairs={{0,1},{1,0},{2,3},{3,2},{4,5},{5,4},{6,7},{7,6},{8,9},{9,8},{10,11... | collective-permute-start | bytes 5308424 | tf_op jit(solution)/shard_map/ppermute | solution.py:182
  71.3 13.7 %collective-permute-start.17 = (bf16[1,448,128]{2,1,0:T(8,128)(2,1)S(1)}, bf16[1,448,128]{2,1,0:T(8,128)(2,1)S(1)}, u32[]{:S(2)}, u32[]{:S(2)}) collective-permute-start(bf16[1,448,128]{2,1,0:T(8,128)(2,1)S(1)} %slice_bitcast_fusion.3), channel_id=1, source_target_pairs={{0,16},{8,24},{16,0},{24,8},{1,17},{9,25},{17,1},{25,9},{2,18},{10... | collective-permute-start | bytes 344072 | tf_op jit(solution)/shard_map/ppermute | solution.py:176
  72.7 12.3 %collective-permute-start.19 = (bf16[1,448,128]{2,1,0:T(8,128)(2,1)S(1)}, bf16[1,448,128]{2,1,0:T(8,128)(2,1)S(1)}, u32[]{:S(2)}, u32[]{:S(2)}) collective-permute-start(bf16[1,448,128]{2,1,0:T(8,128)(2,1)S(1)} %slice_bitcast_fusion.2), channel_id=1, source_target_pairs={{0,8},{8,0},{16,24},{24,16},{1,9},{9,1},{17,25},{25,17},{2,10},{10... | collective-permute-start | bytes 344072 | tf_op jit(solution)/shard_map/ppermute | solution.py:177
  84.9 19.0 %copy-start.3 = (f32[2,32,3456]{2,1,0:T(8,128)S(1)}, f32[2,32,3456]{2,1,0:T(8,128)}, u32[]{:S(2)}) copy-start(f32[2,32,3456]{2,1,0:T(8,128)} %get-tuple-element.43) | copy-start | bytes 2654212
  85.0 13.3 %collective-permute-start.20 = (bf16[1,2,448,128]{3,2,1,0:T(8,128)(2,1)S(1)}, bf16[1,2,448,128]{3,2,1,0:T(8,128)(2,1)S(1)}, u32[]{:S(2)}, u32[]{:S(2)}) collective-permute-start(bf16[1,2,448,128]{3,2,1,0:T(8,128)(2,1)S(1)} %collective-permute-done.3.own), channel_id=1, source_target_pairs={{0,8},{8,0},{16,24},{24,16},{1,9},{9,1},{17,25},{25,17},{2,10},{10... | collective-permute-start | bytes 688136 | tf_op jit(solution)/shard_map/ppermute | solution.py:174
  86.5 13.2 %collective-permute-start.21 = (bf16[1,2,448,128]{3,2,1,0:T(8,128)(2,1)S(1)}, bf16[1,2,448,128]{3,2,1,0:T(8,128)(2,1)S(1)}, u32[]{:S(2)}, u32[]{:S(2)}) collective-permute-start(bf16[1,2,448,128]{3,2,1,0:T(8,128)(2,1)S(1)} %collective-permute-done.3.own), channel_id=1, source_target_pairs={{0,16},{8,24},{16,0},{24,8},{1,17},{9,25},{17,1},{25,9},{2,18},{10... | collective-permute-start | bytes 688136 | tf_op jit(solution)/shard_map/ppermute | solution.py:175
  98.3 19.4 %collective-permute-start.25 = (f32[1,128,3456]{2,1,0:T(8,128)S(1)}, f32[1,128,3456]{2,1,0:T(8,128)S(1)}, u32[]{:S(2)}, u32[]{:S(2)}) collective-permute-start(f32[1,128,3456]{2,1,0:T(8,128)S(1)} %get-tuple-element.36), channel_id=1, source_target_pairs={{0,1},{1,0},{2,3},{3,2},{4,5},{5,4},{6,7},{7,6},{8,9},{9,8},{10,11... | collective-permute-start | bytes 5308424 | tf_op jit(solution)/shard_map/ppermute | solution.py:182
  98.3 5.6 %collective-permute-start.22 = (bf16[1,448,128]{2,1,0:T(8,128)(2,1)S(1)}, bf16[1,448,128]{2,1,0:T(8,128)(2,1)S(1)}, u32[]{:S(2)}, u32[]{:S(2)}) collective-permute-start(bf16[1,448,128]{2,1,0:T(8,128)(2,1)S(1)} %slice_bitcast_fusion.1), channel_id=1, source_target_pairs={{0,16},{8,24},{16,0},{24,8},{1,17},{9,25},{17,1},{25,9},{2,18},{10... | collective-permute-start | bytes 344072 | tf_op jit(solution)/shard_map/ppermute | solution.py:176
  99.7 5.5 %collective-permute-start.23 = (bf16[1,448,128]{2,1,0:T(8,128)(2,1)S(1)}, bf16[1,448,128]{2,1,0:T(8,128)(2,1)S(1)}, u32[]{:S(2)}, u32[]{:S(2)}) collective-permute-start(bf16[1,448,128]{2,1,0:T(8,128)(2,1)S(1)} %slice_bitcast_fusion), channel_id=1, source_target_pairs={{0,8},{8,0},{16,24},{24,16},{1,9},{9,1},{17,25},{25,17},{2,10},{10... | collective-permute-start | bytes 344072 | tf_op jit(solution)/shard_map/ppermute | solution.py:177
  104.0 94.5 %collective-permute-start.6 = (f32[2,32,3456]{2,1,0:T(8,128)S(1)}, f32[2,32,3456]{2,1,0:T(8,128)S(1)}, u32[]{:S(2)}, u32[]{:S(2)}) collective-permute-start(f32[2,32,3456]{2,1,0:T(8,128)S(1)} %copy-done.3), channel_id=1, source_target_pairs={{1,0},{2,1},{3,2},{4,3},{5,4},{6,5},{7,6},{9,8},{10,9},{11,10},{12... | collective-permute-start | bytes 2654216 | tf_op jit(solution)/shard_map/ppermute | solution.py:158
  105.3 94.8 %collective-permute-start.11 = (f32[1,128,3456]{2,1,0:T(8,128)S(1)}, f32[1,128,3456]{2,1,0:T(8,128)S(1)}, u32[]{:S(2)}, u32[]{:S(2)}) collective-permute-start(f32[1,128,3456]{2,1,0:T(8,128)S(1)} %get-tuple-element.30), channel_id=1, source_target_pairs={{0,1},{1,0},{2,3},{3,2},{4,5},{5,4},{6,7},{7,6},{8,9},{9,8},{10,11... | collective-permute-start | bytes 5308424 | tf_op jit(solution)/shard_map/ppermute | solution.py:182
  117.5 5.7 %collective-permute-start.24 = (f32[1,128,3456]{2,1,0:T(8,128)S(1)}, f32[1,128,3456]{2,1,0:T(8,128)S(1)}, u32[]{:S(2)}, u32[]{:S(2)}) collective-permute-start(f32[1,128,3456]{2,1,0:T(8,128)S(1)} %get-tuple-element.34), channel_id=1, source_target_pairs={{0,1},{1,0},{2,3},{3,2},{4,5},{5,4},{6,7},{7,6},{8,9},{9,8},{10,11... | collective-permute-start | bytes 5308424 | tf_op jit(solution)/shard_map/ppermute | solution.py:182
  117.6 1.2 copy-start.2
  118.7 81.1 %collective-permute-start.4 = (f32[2,32,3456]{2,1,0:T(8,128)S(1)}, f32[2,32,3456]{2,1,0:T(8,128)S(1)}, u32[]{:S(2)}, u32[]{:S(2)}) collective-permute-start(f32[2,32,3456]{2,1,0:T(8,128)S(1)} %copy-done.2), channel_id=1, source_target_pairs={{0,7},{7,0},{8,15},{15,8},{16,23},{23,16},{24,31},{31,24}} | collective-permute-start | bytes 2654216 | tf_op jit(solution)/shard_map/ppermute | solution.py:190
  123.3 33.8 %collective-permute-start.27 = (f16[128,3456]{1,0:T(8,128)(2,1)S(1)}, f16[128,3456]{1,0:T(8,128)(2,1)S(1)}, u32[]{:S(2)}, u32[]{:S(2)}) collective-permute-start(f16[128,3456]{1,0:T(8,128)(2,1)S(1)} %bitcast_convert_fusion), channel_id=1, source_target_pairs={{0,2},{1,3},{6,4},{7,5},{8,10},{9,11},{14,12},{15,13},{16,18},{17,... | collective-permute-start | bytes 2654216 | tf_op jit(solution)/shard_map/ppermute | solution.py:193
  157.0 14.9 %collective-permute-start.28 = (f16[128,3456]{1,0:T(8,128)(2,1)S(1)}, f16[128,3456]{1,0:T(8,128)(2,1)S(1)}, u32[]{:S(2)}, u32[]{:S(2)}) collective-permute-start(f16[128,3456]{1,0:T(8,128)(2,1)S(1)} %bitcast_convert_fusion.1), channel_id=1, source_target_pairs={{0,2},{1,3},{6,4},{7,5},{8,10},{9,11},{14,12},{15,13},{16,18},{17,... | collective-permute-start | bytes 2654216 | tf_op jit(solution)/shard_map/ppermute | solution.py:197
  172.0 1.1 collective-permute-start.31
  173.1 40.9 %collective-permute-start.29 = (f16[128,3456]{1,0:T(8,128)(2,1)S(1)}, f16[128,3456]{1,0:T(8,128)(2,1)S(1)}, u32[]{:S(2)}, u32[]{:S(2)}) collective-permute-start(f16[128,3456]{1,0:T(8,128)(2,1)S(1)} %bitcast_convert_fusion.2), channel_id=1, source_target_pairs={{0,2},{1,3},{6,4},{7,5},{8,10},{9,11},{14,12},{15,13},{16,18},{17,... | collective-permute-start | bytes 2654216 | tf_op jit(solution)/shard_map/ppermute | solution.py:202
  197.8 16.2 %collective-permute-start.30 = (f16[128,3456]{1,0:T(8,128)(2,1)S(1)}, f16[128,3456]{1,0:T(8,128)(2,1)S(1)}, u32[]{:S(2)}, u32[]{:S(2)}) collective-permute-start(f16[128,3456]{1,0:T(8,128)(2,1)S(1)} %fusion.20), channel_id=1, source_target_pairs={{2,4},{3,5},{4,2},{5,3},{10,12},{11,13},{12,10},{13,11},{18,20},{1... | collective-permute-start | bytes 2654216 | tf_op jit(solution)/shard_map/ppermute | solution.py:203
  198.5 21.4 %collective-permute-start.32 = (f16[128,3456]{1,0:T(8,128)(2,1)S(1)}, f16[128,3456]{1,0:T(8,128)(2,1)S(1)}, u32[]{:S(2)}, u32[]{:S(2)}) collective-permute-start(f16[128,3456]{1,0:T(8,128)(2,1)S(1)} %fusion.22), channel_id=1, source_target_pairs={{4,6},{5,7},{2,0},{3,1},{12,14},{13,15},{10,8},{11,9},{20,22},{21,... | collective-permute-start | bytes 2654216 | tf_op jit(solution)/shard_map/ppermute | solution.py:204

commit v2 on v1

--- a/solution.py
+++ b/solution.py
@@ -16,6 +16,7 @@
 BF16 = jnp.bfloat16
 F16 = jnp.float16
 F32 = jnp.float32
+HALF_MAX = 60000.0
 
 
 def speeds(directions, offset, length):
@@ -44,9 +45,9 @@
     return up, down, around
 
 
-def advected(distribution, below, above, directions, wall_mask):
+def advected(distribution, below, above, directions, wall_mask, offset):
     tile_len, _, local_vel = distribution.shape
-    moving, speed_x, speed_y = speeds(directions, lax.axis_index("vel") * local_vel, local_vel)
+    moving, speed_x, speed_y = speeds(directions, offset, local_vel)
     padded_x = jnp.concatenate([below, distribution, above], axis=0)
     first_up = jnp.where(moving > 0, padded_x[1 : tile_len + 1], padded_x[3 : tile_len + 3])
     second_up = jnp.where(moving > 0, padded_x[0:tile_len], padded_x[4 : tile_len + 4])
@@ -74,7 +75,7 @@
             out[q, piece:, :] = tail
 
 
-def split_pieces(distribution, chip, core, cells):
+def split_pieces(distribution, place, cells):
     tile_len, width, local_vel = distribution.shape
     piece = local_vel // cells
     out = jax.ShapeDtypeStruct((cells // 2, piece + TAIL, LANES), BF16)
@@ -84,13 +85,13 @@
         in_specs=[pl.BlockSpec(memory_space=pltpu.SMEM), pl.BlockSpec(memory_space=pltpu.VMEM)],
         out_specs=(pl.BlockSpec(memory_space=pltpu.VMEM), pl.BlockSpec(memory_space=pltpu.VMEM)),
         scratch_shapes=[pltpu.VMEM((local_vel, LANES), BF16)],
-        compiler_params=pltpu.CompilerParams(vmem_limit_bytes=24 << 20),
+        compiler_params=pltpu.CompilerParams(vmem_limit_bytes=10 << 20),
         cost_estimate=pl.CostEstimate(flops=local_vel * LANES, bytes_accessed=local_vel * LANES * 6, transcendentals=0),
         name="pieces",
-    )(jnp.stack([chip, core]).astype(jnp.int32), distribution.reshape(tile_len * width, local_vel))
-
-
-def product_kernel(vel, own, gx, gy, dx, dy, c_ref, keep_ref, send_ref, scale_ref, rows, lhs, *, piece, bound):
+    )(place, distribution.reshape(tile_len * width, local_vel))
+
+
+def product_kernel(place, own, gx, gy, dx, dy, c_ref, keep_ref, send_ref, scale_ref, rows, lhs, *, piece, bound):
     slots = own.shape[0]
 
     @pl.when(pl.program_id(0) == 0)
@@ -101,7 +102,7 @@
                 parts = ((0, own.at[s, side]), (1, gx.at[s, side]), (2, gy.at[s, side]), (3, diagonal.at[s]))
                 top = jnp.zeros((TAIL, LANES), F32)
                 for q, part in parts:
-                    at = pl.multiple_of((vel[0] ^ q) * piece, TAIL)
+                    at = pl.multiple_of((place[2] ^ q) * piece, TAIL)
                     rows[pl.ds(at, piece), :] = part[:piece, :]
                     top = jnp.maximum(top, part[piece:, :].astype(F32))
                 lhs[(2 * s + side) * LANES : (2 * s + side + 1) * LANES, :] = rows[...].T
@@ -113,16 +114,16 @@
         send_ref[s] = out[LANES:] * scale_ref[s, 1, 0:1, 0:1]
 
 
-def product(vel, own, gx, gy, dx, dy, matrix, block):
+def product(place, own, gx, gy, dx, dy, matrix, vels):
     slots = own.shape[0]
     piece = own.shape[2] - TAIL
     depth, columns = matrix.shape
-    total = columns * 4
+    block = columns // 3
     whole = lambda a: pl.BlockSpec(a.shape, lambda n: (0,) * a.ndim)
     out = jax.ShapeDtypeStruct((slots, LANES, columns), F32)
     out_spec = pl.BlockSpec((slots, LANES, block), lambda n: (0, 0, n))
     return pl.pallas_call(
-        functools.partial(product_kernel, piece=piece, bound=60000.0 / (total * COLLISION_MAX)),
+        functools.partial(product_kernel, piece=piece, bound=HALF_MAX / (vels * columns * COLLISION_MAX)),
         grid=(columns // block,),
         out_shape=(out, out, jax.ShapeDtypeStruct((slots, 2, 8, LANES), F32)),
         in_specs=[pl.BlockSpec(memory_space=pltpu.SMEM)]
@@ -130,14 +131,43 @@
         + [pl.BlockSpec((depth, block), lambda n: (0, n))],
         out_specs=(out_spec, out_spec, pl.BlockSpec((slots, 2, 8, LANES), lambda n: (0, 0, 0, 0))),
         scratch_shapes=[pltpu.VMEM((depth, LANES), BF16), pltpu.VMEM((slots * 2 * LANES, depth), BF16)],
-        compiler_params=pltpu.CompilerParams(vmem_limit_bytes=40 << 20),
+        compiler_params=pltpu.CompilerParams(vmem_limit_bytes=18 << 20),
         cost_estimate=pl.CostEstimate(
             flops=2 * slots * 2 * LANES * depth * columns,
             bytes_accessed=depth * columns * 2 + slots * 2 * LANES * columns * 4,
             transcendentals=0,
         ),
         name="product",
-    )(jnp.reshape(vel, (1,)).astype(jnp.int32), own, gx, gy, dx, dy, matrix)
+    )(place, own, gx, gy, dx, dy, matrix)
+
+
+def edge_kernel(place, a_ref, c_ref, d_ref, out_ref, *, cells):
+    chip, core = place[0], place[1]
+    cell = 2 * chip + core
+    last = cells // 2 - 1
+    is_end = jnp.logical_or(chip == 0, chip == last)
+    held = ((a_ref, jnp.where(is_end, 3, 0)), (c_ref, jnp.where(is_end, 1, 3)), (d_ref, jnp.where(is_end, 0, 1)))
+    for k, other in enumerate(((cell + cells - 1) % cells, (cell + 1) % cells)):
+        total = jnp.zeros((TAIL, LANES), F32)
+        for ref, q in held:
+            for side in range(2):
+                here = jnp.logical_and((other // 2) ^ chip == q, (other % 2) ^ core == side)
+                tail = ref[0, side, ref.shape[2] - TAIL :, :].astype(F32)
+                total = total + jnp.where(here, tail, jnp.zeros_like(tail))
+        out_ref[k] = total[:8] * (1.0 / HALF_MAX)
+
+
+def edge_scales(place, a, c, d, cells):
+    vmem = pl.BlockSpec(memory_space=pltpu.VMEM)
+    return pl.pallas_call(
+        functools.partial(edge_kernel, cells=cells),
+        out_shape=jax.ShapeDtypeStruct((2, 8, LANES), F32),
+        in_specs=[pl.BlockSpec(memory_space=pltpu.SMEM), vmem, vmem, vmem],
+        out_specs=vmem,
+        compiler_params=pltpu.CompilerParams(vmem_limit_bytes=4 << 20),
+        cost_estimate=pl.CostEstimate(flops=10000, bytes_accessed=10000, transcendentals=0),
+        name="edges",
+    )(place, a, c, d)
 
 
 def after(value, *earlier):
@@ -149,13 +179,10 @@
     cells = lax.axis_size("cell")
     cell = lax.axis_index("cell")
     vel = lax.axis_index("vel")
-    chip, core = cell // 2, cell % 2
-    matrix = collision.reshape(-1, local_vel)
-
-    up, down, around = halo_pairs(cells)
-    head, foot = distribution[:2], distribution[tile_len - 2 :]
-    from_below = lax.ppermute(foot, "cell", up)
-    from_above = lax.ppermute(head, "cell", down)
+    place = jnp.stack([cell >> 1, cell & 1, vel])
+    is_end = jnp.logical_or(cell < 2, cell >= cells - 2)
+    distribution, place, is_end, offset = lax.optimization_barrier((distribution, place, is_end, vel * local_vel))
+    matrix = pltpu.with_memory_space_constraint(collision.reshape(-1, local_vel), pltpu.HBM)
 
     other_core = [(i, i ^ 1) for i in range(cells)]
     across = lambda q: [(i, 2 * ((i // 2) ^ q) + i % 2) for i in range(cells)]
@@ -165,52 +192,72 @@
     ends = chips((0, 1), (3, 2))
     middle = chips((1, 2), (2, 1))
     outward = chips((2, 3), (1, 0))
-
-    keep, send = split_pieces(distribution, chip, core, cells)
+    ring = [(i, (i + 1) % cells) for i in range(cells)]
+
+    def gather_x_y(own):
+        return own, lax.ppermute(own, "vel", in_x), lax.ppermute(own, "vel", in_y)
+
+    def gather_diagonal(parts, *earlier):
+        own, gx, gy = parts
+        dx = lax.ppermute(after(gx[:, 0], *earlier), "vel", in_y)
+        dy = lax.ppermute(after(gy[:, 1], *earlier), "vel", in_x)
+        return own, gx, gy, dx, dy
+
+    def exchanged(mine, theirs):
+        theirs = lax.ppermute(theirs.astype(F16), "cell", other_core)
+        return [mine[s] + theirs[s].astype(F32) for s in range(mine.shape[0])]
+
+    def behind(parts, *earlier):
+        return (after(parts[0], *earlier),) + tuple(parts[1:])
+
+    keep, send = split_pieces(distribution, place, cells)
     got = lax.ppermute(send, "cell", other_core)
     both = [jnp.stack([keep[q], got[q]])[None] for q in range(4)]
 
-    def gathered(own):
-        gx = lax.ppermute(own, "vel", in_x)
-        gy = lax.ppermute(own, "vel", in_y)
-        dx = lax.ppermute(gx[:, 0], "vel", in_y)
-        dy = lax.ppermute(gy[:, 1], "vel", in_x)
-        return own, gx, gy, dx, dy
-
-    def partial(parts):
-        mine, theirs, scale = product(vel, *parts, matrix, 384)
-        return mine, lax.ppermute(theirs, "cell", other_core), scale
-
-    z3 = lax.ppermute(both[3], "cell", across(3))
-    g0 = gathered(both[0])
-    z2 = lax.ppermute(after(both[2], z3), "cell", across(2))
-    z1 = lax.ppermute(after(both[1], z3), "cell", across(1))
-    g3 = gathered(z3)
-    wrapping = jnp.where(cell == 0, head, foot)
-    from_around = lax.ppermute(after(wrapping, z2, z1), "cell", around)
-    mine3, theirs3, _ = partial(g3)
-    p3 = (mine3 + theirs3)[0]
-    a0 = lax.ppermute(p3.astype(F16), "cell", ends)
-    g2 = gathered(after(z2, g3[3], g3[4]))
-    mine2, theirs2, _ = partial(g2)
-    p2 = (mine2 + theirs2)[0]
-    a1 = lax.ppermute(after(p2.astype(F16), a0), "cell", ends)
-    b1 = lax.ppermute((p2 + a0.astype(F32)).astype(F16), "cell", middle)
-    g1 = gathered(after(z1, g2[3], g2[4]))
-    mine1, theirs1, _ = partial(g1)
-    p1 = (mine1 + theirs1)[0]
-    a2 = lax.ppermute(after(p1.astype(F16), a1), "cell", ends)
-    b2 = lax.ppermute((p3 + a1.astype(F32)).astype(F16), "cell", middle)
-    c2 = lax.ppermute((p1 + b1.astype(F32)).astype(F16), "cell", outward)
-    mine0, theirs0, scale = partial(g0)
-
-    below = jnp.where(cell == 0, from_around, from_below)
-    above = jnp.where(cell == cells - 1, from_around, from_above)
-    open_cells, base = advected(distribution, below, above, directions, wall_mask)
-    shape = distribution.shape
-    rest = (mine0 + theirs0).reshape(shape)
-    arrived = (a2.astype(F32) + b2.astype(F32) + c2.astype(F32)).reshape(shape)
-    return base + open_cells * (relax / scale[0, 0, 0, 0]) * (rest + arrived)
+    from_end = lax.ppermute(both[3], "cell", chips((0, 3), (3, 0)))
+    slot_a = jnp.where(is_end, from_end, both[0])
+    ga = gather_x_y(slot_a)
+    slot_b = lax.ppermute(after(both[2], from_end), "cell", across(2))
+    z1 = lax.ppermute(after(both[1], from_end), "cell", across(1))
+    from_middle = lax.ppermute(after(both[3], from_end), "cell", middle)
+    ga = gather_diagonal(ga)
+    own_top = keep[0:1, keep.shape[1] - 1 :, 0:1].astype(F32)
+    edges = after(distribution, slot_b, z1, from_middle) * (HALF_MAX / own_top)
+    from_below = lax.ppermute(edges[tile_len - 2 :].astype(F16), "cell", ring)
+    from_above = lax.ppermute(edges[:2].astype(F16), "cell", [(j, i) for i, j in ring])
+
+    mine_a, theirs_a, scale_a = product(place, *behind(ga, slot_b), matrix, 4)
+    gb = gather_x_y(after(slot_b, theirs_a))
+    (pa,) = exchanged(mine_a, theirs_a)
+    ma = after(pa.astype(F16), from_below, from_above)
+    a0 = lax.ppermute(ma, "cell", ends)
+    gb = gather_diagonal(gb, ma)
+    mine_b, theirs_b, _ = product(place, *behind(gb, ma), matrix, 4)
+    z1, from_middle, both0, _ = lax.optimization_barrier((z1, from_middle, both[0], theirs_b))
+    slot_c = jnp.where(is_end, z1, from_middle)
+    slot_d = jnp.where(is_end, both0, z1)
+    gcd = gather_x_y(jnp.concatenate([slot_c, slot_d]))
+    (pb,) = exchanged(mine_b, theirs_b)
+    mb = pb.astype(F16)
+    a1 = lax.ppermute(after(mb, a0), "cell", ends)
+    b1 = lax.ppermute((pb + a0.astype(F32)).astype(F16), "cell", middle)
+    gcd = gather_diagonal(gcd, mb)
+    mine_cd, theirs_cd, scale_cd = product(place, *behind(gcd, mb), matrix, 4)
+    pc, pd = exchanged(mine_cd, theirs_cd)
+    a2 = lax.ppermute(after(pc.astype(F16), a1), "cell", ends)
+    b2 = lax.ppermute((pc + a1.astype(F32)).astype(F16), "cell", middle)
+    c2 = lax.ppermute((pd + b1.astype(F32)).astype(F16), "cell", outward)
+
+    edge = edge_scales(place, *lax.optimization_barrier((slot_a, slot_c, slot_d, mb))[:3], cells)
+    below = from_below.astype(F32) * edge[0:1, :1, :1]
+    above = from_above.astype(F32) * edge[1:2, :1, :1]
+    open_cells, base = advected(after(distribution, mb), below, above, directions, wall_mask, offset)
+    scale = jnp.where(is_end, scale_cd[1, 0:1, :1, :1], scale_a[0, 0:1, :1, :1])
+    own = jnp.where(is_end, pd, pa)
+    factor = open_cells * (relax / scale)
+    base, factor, own = lax.optimization_barrier((base, factor, own))
+    arrived = a2.astype(F32) + b2.astype(F32) + c2.astype(F32)
+    return base + factor * (own + arrived).reshape(distribution.shape)
 
 
 def plain_body(distribution, collision, directions, wall_mask):
@@ -224,7 +271,8 @@
     from_around = lax.ppermute(jnp.where(cell == 0, head, foot), "cell", around)
     below = jnp.where(cell == 0, from_around, lax.ppermute(foot, "cell", up))
     above = jnp.where(cell == cells - 1, from_around, lax.ppermute(head, "cell", down))
-    open_cells, base = advected(distribution, below, above, directions, wall_mask)
+    offset = lax.axis_index("vel") * local_vel
+    open_cells, base = advected(distribution, below, above, directions, wall_mask, offset)
     pieces = distribution.astype(BF16).reshape(tile_len * width, cells, piece)
     spread = lax.all_to_all(pieces, "cell", split_axis=1, concat_axis=0, tiled=True)
     panel = lax.all_gather(spread.reshape(-1, piece), "vel", axis=1, tiled=True)

time: 225 us -> 156 us (0.69)
  starting transfers between devices: 81.3 us -> 41.8 us
  Pallas kernels: 44.7 us -> 28.2 us
  waiting for transfers between devices: 85.7 us -> 70.1 us
    ppermute x32 -> x27, starting transfers between devices: 80.8 us -> 41.3 us  [the longest x6 7.38 us: gather_x_y(): return (own, lax.ppermute(own, 'vel', in_x), lax.ppermute(own, 'vel', in_y))]
    ppermute x32 -> x27, waiting for transfers between devices: 85.7 us -> 68.7 us  [the longest x6 12.9 us: gather_x_y(): return (own, lax.ppermute(own, 'vel', in_x), lax.ppermute(own, 'vel', in_y))]
    pallas_call x4, Pallas kernels: 43.7 us -> 27.2 us  [the longest x3 26.6 us: product(): pl.pallas_call(functools.partial(product_kernel, piece=piece, bound=HALF_...]
    mul x1 -> x4, other arithmetic: 0.01 us -> 3.96 us  [the longest x1 2.52 us: advected(): return (open_cells, open_cells * (distribution - adv_x - adv_y))]
  transfers between devices with their start and end apart: 33 -> 28, of which waited for: 11 -> 18; matrix products, arithmetic and copies ran while one was open for 2% -> 6% of each run, Pallas kernels for 20% -> 7%
where the time goes in v2:
time: 156 us; the launch traced here: 155 us
  waiting for transfers between devices  70.1 us (45%)
  starting transfers between devices  41.8 us (27%)
  Pallas kernels  28.2 us (18%)
  other arithmetic  8.58 us (6%)
  local copies, waits for them, and re-layouts  3.99 us (3%)
  between operations  2.4 us (2%)
    pallas_call x3, Pallas kernels, product(): pl.pallas_call(functools.partial(product_kernel, piece=piece, bound=HALF_...  26.6 us
    ppermute x6, waiting for transfers between devices, gather_x_y(): return (own, lax.ppermute(own, 'vel', in_x), lax.ppermute(own, 'vel', in_y))  12.9 us
    ppermute x1, waiting for transfers between devices, chain_body(): a0 = lax.ppermute(ma, 'cell', ends)  12 us
    ppermute x1, waiting for transfers between devices, chain_body(): a2 = lax.ppermute(after(pc.astype(F16), a1), 'cell', ends)  10.1 us
    ppermute x6, starting transfers between devices, gather_x_y(): return (own, lax.ppermute(own, 'vel', in_x), lax.ppermute(own, 'vel', in_y))  7.38 us
    ppermute x1, starting transfers between devices, chain_body(): from_end = lax.ppermute(both[3], 'cell', chips((0, 3), (3, 0)))  6.88 us
    ppermute x3, waiting for transfers between devices, gather_diagonal(): dx = lax.ppermute(after(gx[:, 0], *earlier), 'vel', in_y)  6.16 us
    ppermute x1, waiting for transfers between devices, chain_body(): from_end = lax.ppermute(both[3], 'cell', chips((0, 3), (3, 0)))  5.84 us
  transfers between devices with their start and end apart: 28, of which 18 were waited for; matrix products, arithmetic and copies ran while one was open for 6% of the time, Pallas kernels for 7%

profile of v2, /device:TPU:0, one launch (start us, length us, event | category | flops | bytes accessed | tf_op | source)
XLA Modules:
  0.0 155.1 jit_solution(2856499959183441254)
XLA Ops:
  0.1 1.5 copy-done
  1.6 1.1 pieces.1
  2.6 0.5 collective-permute-start
  3.2 1.4 collective-permute-done
  4.7 6.9 %collective-permute-start.1 = (bf16[1,2,448,128]{3,2,0,1:T(8,128)(2,1)S(1)}, bf16[1,2,448,128]{3,2,0,1:T(8,128)(2,1)S(1)}, u32[]{:S(2)}, u32[]{:S(2)}) collective-permute-start(bf16[1,2,448,128]{3,2,0,1:T(8,128)(2,1)S(1)} %maximum_bitcast_fusion.1), channel_id=1, source_target_pairs={{0,6},{1,7},{6,0},{7,1},{8,14},{9,15},{14,8},{15,9},{16,22},{17,23... | collective-permute-start | bytes 688136 | tf_op jit(solution)/shard_map/ppermute | solution.py:217
  11.6 5.8 %collective-permute-done.1 = bf16[1,2,448,128]{3,2,0,1:T(8,128)(2,1)S(1)} collective-permute-done((bf16[1,2,448,128]{3,2,0,1:T(8,128)(2,1)S(1)}, bf16[1,2,448,128]{3,2,0,1:T(8,128)(2,1)S(1)}, u32[]{:S(2)}, u32[]{:S(2)}) %collective-permute-start.1) | collective-permute-done | bytes 229408 | tf_op jit(solution)/shard_map/ppermute | solution.py:217
  17.4 4.1 %collective-permute-start.8 = (bf16[1,2,448,128]{3,2,0,1:T(8,128)(2,1)S(1)}, bf16[1,2,448,128]{3,2,0,1:T(8,128)(2,1)S(1)}, u32[]{:S(2)}, u32[]{:S(2)}) collective-permute-start(bf16[1,2,448,128]{3,2,0,1:T(8,128)(2,1)S(1)} %bitcast.74), channel_id=1, source_target_pairs={{0,2},{1,3},{2,0},{3,1},{4,6},{5,7},{6,4},{7,5},{8,10},{9,11},{10,... | collective-permute-start | bytes 688136 | tf_op jit(solution)/shard_map/ppermute | solution.py:221
  21.5 0.7 collective-permute-start.9
  22.2 1.6 %collective-permute-start.4 = (bf16[1,2,448,128]{3,2,0,1:T(8,128)(2,1)S(1)}, bf16[1,2,448,128]{3,2,0,1:T(8,128)(2,1)S(1)}, u32[]{:S(2)}, u32[]{:S(2)}) collective-permute-start(bf16[1,2,448,128]{3,2,0,1:T(8,128)(2,1)S(1)} %broadcast_select_fusion.2), channel_id=1, source_target_pairs={{0,16},{8,24},{16,0},{24,8},{1,17},{9,25},{17,1},{25,9},{2,18},{10... | collective-permute-start | bytes 688136 | tf_op jit(solution)/shard_map/ppermute | solution.py:198
  23.8 0.5 slice.115
  25.1 1.6 %collective-permute-start.3 = (bf16[1,2,448,128]{3,2,0,1:T(8,128)(2,1)S(1)}, bf16[1,2,448,128]{3,2,0,1:T(8,128)(2,1)S(1)}, u32[]{:S(2)}, u32[]{:S(2)}) collective-permute-start(bf16[1,2,448,128]{3,2,0,1:T(8,128)(2,1)S(1)} %broadcast_select_fusion.2), channel_id=1, source_target_pairs={{0,8},{8,0},{16,24},{24,16},{1,9},{9,1},{17,25},{25,17},{2,10},{10... | collective-permute-start | bytes 688136 | tf_op jit(solution)/shard_map/ppermute | solution.py:198
  26.7 4.5 %collective-permute-done.2.own = bf16[1,2,448,128]{3,2,1,0:T(8,128)(2,1)S(1)} collective-permute-done((bf16[1,2,448,128]{3,2,1,0:T(8,128)(2,1)S(1)}, bf16[1,2,448,128]{3,2,1,0:T(8,128)(2,1)S(1)}, u32[]{:S(2)}, u32[]{:S(2)}) %collective-permute-start.2) | collective-permute-done | bytes 229408 | tf_op jit(solution)/shard_map/ppermute | solution.py:220
  31.2 1.6 %collective-permute-start.6 = (bf16[1,448,128]{2,1,0:T(8,128)(2,1)S(1)}, bf16[1,448,128]{2,1,0:T(8,128)(2,1)S(1)}, u32[]{:S(2)}, u32[]{:S(2)}) collective-permute-start(bf16[1,448,128]{2,1,0:T(8,128)(2,1)S(1)} %slice_bitcast_fusion.4), channel_id=1, source_target_pairs={{0,8},{8,0},{16,24},{24,16},{1,9},{9,1},{17,25},{25,17},{2,10},{10... | collective-permute-start | bytes 344072 | tf_op jit(solution)/shard_map/ppermute | solution.py:203
  32.8 1.6 %collective-permute-start.5 = (bf16[1,448,128]{2,1,0:T(8,128)(2,1)S(1)}, bf16[1,448,128]{2,1,0:T(8,128)(2,1)S(1)}, u32[]{:S(2)}, u32[]{:S(2)}) collective-permute-start(bf16[1,448,128]{2,1,0:T(8,128)(2,1)S(1)} %slice_bitcast_fusion.5), channel_id=1, source_target_pairs={{0,16},{8,24},{16,0},{24,8},{1,17},{9,25},{17,1},{25,9},{2,18},{10... | collective-permute-start | bytes 344072 | tf_op jit(solution)/shard_map/ppermute | solution.py:202
  34.4 0.1 multiply_convert_fusion
  34.5 1.5 collective-permute-done.6.dy
  36.0 1.6 %collective-permute-done.5.dx = bf16[1,448,128]{2,1,0:T(8,128)(2,1)S(1)} collective-permute-done((bf16[1,448,128]{2,1,0:T(8,128)(2,1)S(1)}, bf16[1,448,128]{2,1,0:T(8,128)(2,1)S(1)}, u32[]{:S(2)}, u32[]{:S(2)}) %collective-permute-start.5) | collective-permute-done | bytes 114720 | tf_op jit(solution)/shard_map/ppermute | solution.py:202
  37.6 7.5 %product.3 = (f32[1,128,3456]{2,1,0:T(8,128)S(1)}, f32[1,128,3456]{2,1,0:T(8,128)S(1)}, f32[1,2,8,128]{3,2,1,0:T(8,128)S(1)}) custom-call(s32[3]{0:T(128)S(1)} %pad_add_fusion.place, bf16[1,2,448,128]{3,2,1,0:T(8,128)(2,1)S(1)} %bitcast.66, bf16[1,2,448,128]{3,2,1,0:T(8,128)(2,1)S(1)} %bitcast.69, bf16[1,2,448,128]{3,2,1,0:T(8,128)(2,1)S(1)} %bitcast.68, ...), custom_call_target="tpu_custom_call" | custom-call | flops 3057647616 | bytes 15482880 | tf_op jit(solution)/shard_map/product/pallas_call | solution.py:125
  45.3 1.6 %collective-permute-start.13 = (bf16[1,2,448,128]{3,2,1,0:T(8,128)(2,1)S(1)}, bf16[1,2,448,128]{3,2,1,0:T(8,128)(2,1)S(1)}, u32[]{:S(2)}, u32[]{:S(2)}) collective-permute-start(bf16[1,2,448,128]{3,2,1,0:T(8,128)(2,1)S(1)} %collective-permute-done.2.own), channel_id=1, source_target_pairs={{0,16},{8,24},{16,0},{24,8},{1,17},{9,25},{17,1},{25,9},{2,18},{10... | collective-permute-start | bytes 688136 | tf_op jit(solution)/shard_map/ppermute | solution.py:198
  46.9 0.1 fusion.32
  47.0 1.7 %collective-permute-start.11 = (f16[2,32,3456]{2,1,0:T(8,128)(2,1)S(1)}, f16[2,32,3456]{2,1,0:T(8,128)(2,1)S(1)}, u32[]{:S(2)}, u32[]{:S(2)}) collective-permute-start(f16[2,32,3456]{2,1,0:T(8,128)(2,1)S(1)} %get-tuple-element.86), channel_id=1, source_target_pairs={{1,0},{2,1},{3,2},{4,3},{5,4},{6,5},{7,6},{0,7},{9,8},{10,9},{11,1... | collective-permute-start | bytes 1327112 | tf_op jit(solution)/shard_map/ppermute | solution.py:227
  48.7 0.5 collective-permute-start.12
  49.3 2.1 %collective-permute-done.13.gy = bf16[1,2,448,128]{3,2,1,0:T(8,128)(2,1)S(1)} collective-permute-done((bf16[1,2,448,128]{3,2,1,0:T(8,128)(2,1)S(1)}, bf16[1,2,448,128]{3,2,1,0:T(8,128)(2,1)S(1)}, u32[]{:S(2)}, u32[]{:S(2)}) %collective-permute-start.13) | collective-permute-done | bytes 229408 | tf_op jit(solution)/shard_map/ppermute | solution.py:198
  51.4 3.7 %collective-permute-done.12.gx = bf16[1,2,448,128]{3,2,1,0:T(8,128)(2,1)S(1)} collective-permute-done((bf16[1,2,448,128]{3,2,1,0:T(8,128)(2,1)S(1)}, bf16[1,2,448,128]{3,2,1,0:T(8,128)(2,1)S(1)}, u32[]{:S(2)}, u32[]{:S(2)}) %collective-permute-start.12) | collective-permute-done | bytes 229408 | tf_op jit(solution)/shard_map/ppermute | solution.py:198
  55.1 0.2 bitcast_convert_fusion.2
  55.3 1.6 %collective-permute-done.11 = f16[2,32,3456]{2,1,0:T(8,128)(2,1)S(1)} collective-permute-done((f16[2,32,3456]{2,1,0:T(8,128)(2,1)S(1)}, f16[2,32,3456]{2,1,0:T(8,128)(2,1)S(1)}, u32[]{:S(2)}, u32[]{:S(2)}) %collective-permute-start.11) | collective-permute-done | bytes 442400 | tf_op jit(solution)/shard_map/ppermute | solution.py:227
  56.9 5.2 %collective-permute-done.10 = f16[2,32,3456]{2,1,0:T(8,128)(2,1)S(1)} collective-permute-done((f16[2,32,3456]{2,1,0:T(8,128)(2,1)S(1)}, f16[2,32,3456]{2,1,0:T(8,128)(2,1)S(1)}, u32[]{:S(2)}, u32[]{:S(2)}) %collective-permute-start.10) | collective-permute-done | bytes 442400 | tf_op jit(solution)/shard_map/ppermute | solution.py:226
  62.1 0.5 collective-permute-start.14
  62.6 0.3 collective-permute-start.15
  62.9 4.6 %collective-permute-done.14.dx = bf16[1,448,128]{2,1,0:T(8,128)(2,1)S(1)} collective-permute-done((bf16[1,448,128]{2,1,0:T(8,128)(2,1)S(1)}, bf16[1,448,128]{2,1,0:T(8,128)(2,1)S(1)}, u32[]{:S(2)}, u32[]{:S(2)}) %collective-permute-start.14) | collective-permute-done | bytes 114720 | tf_op jit(solution)/shard_map/ppermute | solution.py:202
  67.5 0.2 collective-permute-done.15.dy
  67.7 8.1 %product.4 = (f32[1,128,3456]{2,1,0:T(8,128)S(1)}, f32[1,128,3456]{2,1,0:T(8,128)S(1)}, f32[1,2,8,128]{3,2,1,0:T(8,128)}) custom-call(s32[3]{0:T(128)S(1)} %pad_add_fusion.place, bf16[1,2,448,128]{3,2,1,0:T(8,128)(2,1)S(1)} %collective-permute-done.2.own, bf16[1,2,448,128]{3,2,1,0:T(8,128)(2,1)S(1)} %collective-permute-done.12.gx, ...), custom_call_target="tpu_custom_call" | custom-call | flops 3057647616 | bytes 15482880 | tf_op jit(solution)/shard_map/product/pallas_call | solution.py:125
  75.9 1.6 %collective-permute-start.18 = (bf16[2,2,448,128]{3,2,0,1:T(8,128)(2,1)S(1)}, bf16[2,2,448,128]{3,2,0,1:T(8,128)(2,1)S(1)}, u32[]{:S(2)}, u32[]{:S(2)}) collective-permute-start(bf16[2,2,448,128]{3,2,0,1:T(8,128)(2,1)S(1)} %pad_maximum_fusion.2), channel_id=1, source_target_pairs={{0,16},{8,24},{16,0},{24,8},{1,17},{9,25},{17,1},{25,9},{2,18},{10... | collective-permute-start | bytes 1376264 | tf_op jit(solution)/shard_map/ppermute | solution.py:198
  77.5 0.5 collective-permute-start.17
  78.3 0.5 slice.133
  78.8 2.8 %collective-permute-start.22 = (f16[128,3456]{1,0:T(8,128)(2,1)S(1)}, f16[128,3456]{1,0:T(8,128)(2,1)S(1)}, u32[]{:S(2)}, u32[]{:S(2)}) collective-permute-start(f16[128,3456]{1,0:T(8,128)(2,1)S(1)} %bitcast_convert_fusion.2), channel_id=1, source_target_pairs={{0,2},{1,3},{6,4},{7,5},{8,10},{9,11},{14,12},{15,13},{16,18},{17,... | collective-permute-start | bytes 2654216 | tf_op jit(solution)/shard_map/ppermute | solution.py:233
  81.7 6.0 %collective-permute-done.18 = bf16[2,2,448,128]{3,2,0,1:T(8,128)(2,1)S(1)} collective-permute-done((bf16[2,2,448,128]{3,2,0,1:T(8,128)(2,1)S(1)}, bf16[2,2,448,128]{3,2,0,1:T(8,128)(2,1)S(1)}, u32[]{:S(2)}, u32[]{:S(2)}) %collective-permute-start.18) | collective-permute-done | bytes 458784 | tf_op jit(solution)/shard_map/ppermute | solution.py:198
  87.7 1.1 collective-permute-done.17
  88.9 0.3 bitcast_convert_fusion.1
  89.2 12.0 %collective-permute-done.22 = f16[128,3456]{1,0:T(8,128)(2,1)S(1)} collective-permute-done((f16[128,3456]{1,0:T(8,128)(2,1)S(1)}, f16[128,3456]{1,0:T(8,128)(2,1)S(1)}, u32[]{:S(2)}, u32[]{:S(2)}) %collective-permute-start.22) | collective-permute-done | bytes 884768 | tf_op jit(solution)/shard_map/ppermute | solution.py:233
  101.2 0.8 collective-permute-start.19
  101.9 1.3 collective-permute-start.20
  103.2 4.4 %collective-permute-start.23 = (f16[128,3456]{1,0:T(8,128)(2,1)S(1)}, f16[128,3456]{1,0:T(8,128)(2,1)S(1)}, u32[]{:S(2)}, u32[]{:S(2)}) collective-permute-start(f16[128,3456]{1,0:T(8,128)(2,1)S(1)} %bitcast_convert_fusion.1), channel_id=1, source_target_pairs={{0,2},{1,3},{6,4},{7,5},{8,10},{9,11},{14,12},{15,13},{16,18},{17,... | collective-permute-start | bytes 2654216 | tf_op jit(solution)/shard_map/ppermute | solution.py:242
  107.7 0.4 fusion.21
  108.1 0.7 collective-permute-start.26
  108.8 0.6 edges.1
  109.4 0.6 fusion.35
  110.0 10.9 %product.5 = (f32[2,128,3456]{2,1,0:T(8,128)S(1)}, f32[2,128,3456]{2,1,0:T(8,128)S(1)}, f32[2,2,8,128]{3,2,1,0:T(8,128)S(1)}) custom-call(s32[3]{0:T(128)S(1)} %pad_add_fusion.place, bf16[2,2,448,128]{3,2,1,0:T(8,128)(2,1)S(1)} %copy.12.own, bf16[2,2,448,128]{3,2,1,0:T(8,128)(2,1)S(1)} %copy.13.gx, bf16[2,2,448,128]{3,2,1,0:T(8,128)(2,1)S(1)} %copy.14.gy, ...), custom_call_target="tpu_custom_call" | custom-call | flops 6115295232 | bytes 19021824 | tf_op jit(solution)/shard_map/product/pallas_call | solution.py:125
  120.9 0.2 convert_element_type.103
  121.2 0.7 convert_multiply_fusion.1
  121.9 0.7 convert_multiply_fusion
  122.7 2.2 %collective-permute-done.21 = f16[2,128,3456]{2,1,0:T(8,128)(2,1)S(1)} collective-permute-done((f16[2,128,3456]{2,1,0:T(8,128)(2,1)S(1)}, f16[2,128,3456]{2,1,0:T(8,128)(2,1)S(1)}, u32[]{:S(2)}, u32[]{:S(2)}) %collective-permute-start.21) | collective-permute-done | bytes 1769504 | tf_op jit(solution)/shard_map/ppermute | solution.py:207
  124.9 0.2 bitcast_convert_fusion
  125.1 0.7 collective-permute-done.23
  125.8 4.4 %collective-permute-start.24 = (f16[128,3456]{1,0:T(8,128)(2,1)S(1)}, f16[128,3456]{1,0:T(8,128)(2,1)S(1)}, u32[]{:S(2)}, u32[]{:S(2)}) collective-permute-start(f16[128,3456]{1,0:T(8,128)(2,1)S(1)} %bitcast_convert_fusion), channel_id=1, source_target_pairs={{0,2},{1,3},{6,4},{7,5},{8,10},{9,11},{14,12},{15,13},{16,18},{17,... | collective-permute-start | bytes 2654216 | tf_op jit(solution)/shard_map/ppermute | solution.py:247
  130.3 0.8 fusion.19
  131.1 0.7 collective-permute-start.25
  131.8 1.3 collective-permute-start.27
  133.1 2.5 %fusion.6 = f32[4,32,3456]{2,1,0:T(8,128)S(1)} fusion(f32[4,32,3456]{2,1,0:T(8,128)S(1)} %copy-done.1, f32[2,32,3456]{2,1,0:T(8,128)S(1)} %convert_multiply_fusion, f32[2,32,3456]{2,1,0:T(8,128)S(1)} %convert_multiply_fusion.1, f32[3456]{0:T(1024)S(1)} %get-tuple-element.101, f32[3456]{0:T(1024)S(1)} %get-tuple-element.100, ...), kind=kLoop, calls=%fused_computation.14 | loop fusion | flops 9732096 | bytes 5343488 | tf_op jit(solution)/shard_map/mul | solution.py:57
  135.6 0.5 slice.132
  137.5 10.1 %collective-permute-done.24 = f16[128,3456]{1,0:T(8,128)(2,1)S(1)} collective-permute-done((f16[128,3456]{1,0:T(8,128)(2,1)S(1)}, f16[128,3456]{1,0:T(8,128)(2,1)S(1)}, u32[]{:S(2)}, u32[]{:S(2)}) %collective-permute-start.24) | collective-permute-done | bytes 884768 | tf_op jit(solution)/shard_map/ppermute | solution.py:247
  147.6 5.7 %collective-permute-done.27 = f16[128,3456]{1,0:T(8,128)(2,1)S(1)} collective-permute-done((f16[128,3456]{1,0:T(8,128)(2,1)S(1)}, f16[128,3456]{1,0:T(8,128)(2,1)S(1)}, u32[]{:S(2)}, u32[]{:S(2)}) %collective-permute-start.27) | collective-permute-done | bytes 884768 | tf_op jit(solution)/shard_map/ppermute | solution.py:249
  153.3 0.4 add_add_fusion
  153.7 1.4 multiply_add_fusion
  (47 shorter events, 1.0 us)
Async XLA Ops:
  0.1 1.5 copy-start
  2.6 2.0 %collective-permute-start = (bf16[4,448,128]{2,1,0:T(8,128)(2,1)S(1)}, bf16[4,448,128]{2,1,0:T(8,128)(2,1)S(1)}, u32[]{:S(2)}, u32[]{:S(2)}) collective-permute-start(bf16[4,448,128]{2,1,0:T(8,128)(2,1)S(1)} %get-tuple-element.47), channel_id=1, source_target_pairs={{0,1},{1,0},{2,3},{3,2},{4,5},{5,4},{6,7},{7,6},{8,9},{9,8},{10,11... | collective-permute-start | bytes 1376264 | tf_op jit(solution)/shard_map/ppermute | solution.py:214
  3.2 31.2 %copy-start.1 = (f32[4,32,3456]{2,1,0:T(8,128)S(1)}, f32[4,32,3456]{2,1,0:T(8,128)}, u32[]{:S(2)}) copy-start(f32[4,32,3456]{2,1,0:T(8,128)} %param.4) | copy-start | bytes 5308420
  4.7 12.8 %collective-permute-start.1 = (bf16[1,2,448,128]{3,2,0,1:T(8,128)(2,1)S(1)}, bf16[1,2,448,128]{3,2,0,1:T(8,128)(2,1)S(1)}, u32[]{:S(2)}, u32[]{:S(2)}) collective-permute-start(bf16[1,2,448,128]{3,2,0,1:T(8,128)(2,1)S(1)} %maximum_bitcast_fusion.1), channel_id=1, source_target_pairs={{0,6},{1,7},{6,0},{7,1},{8,14},{9,15},{14,8},{15,9},{16,22},{17,23... | collective-permute-start | bytes 688136 | tf_op jit(solution)/shard_map/ppermute | solution.py:217
  17.4 13.7 %collective-permute-start.2 = (bf16[1,2,448,128]{3,2,1,0:T(8,128)(2,1)S(1)}, bf16[1,2,448,128]{3,2,1,0:T(8,128)(2,1)S(1)}, u32[]{:S(2)}, u32[]{:S(2)}) collective-permute-start(bf16[1,2,448,128]{3,2,1,0:T(8,128)(2,1)S(1)} %get-tuple-element.48), channel_id=1, source_target_pairs={{0,4},{1,5},{2,6},{3,7},{4,0},{5,1},{6,2},{7,3},{8,12},{9,13},{10,... | collective-permute-start | bytes 688136 | tf_op jit(solution)/shard_map/ppermute | solution.py:220
  17.4 13.7 %collective-permute-start.8 = (bf16[1,2,448,128]{3,2,0,1:T(8,128)(2,1)S(1)}, bf16[1,2,448,128]{3,2,0,1:T(8,128)(2,1)S(1)}, u32[]{:S(2)}, u32[]{:S(2)}) collective-permute-start(bf16[1,2,448,128]{3,2,0,1:T(8,128)(2,1)S(1)} %bitcast.74), channel_id=1, source_target_pairs={{0,2},{1,3},{2,0},{3,1},{4,6},{5,7},{6,4},{7,5},{8,10},{9,11},{10,... | collective-permute-start | bytes 688136 | tf_op jit(solution)/shard_map/ppermute | solution.py:221
  21.5 9.6 %collective-permute-start.9 = (bf16[1,2,448,128]{3,2,0,1:T(8,128)(2,1)S(1)}, bf16[1,2,448,128]{3,2,0,1:T(8,128)(2,1)S(1)}, u32[]{:S(2)}, u32[]{:S(2)}) collective-permute-start(bf16[1,2,448,128]{3,2,0,1:T(8,128)(2,1)S(1)} %maximum_bitcast_fusion.1), channel_id=1, source_target_pairs={{2,4},{3,5},{4,2},{5,3},{10,12},{11,13},{12,10},{13,11},{18,20},{1... | collective-permute-start | bytes 688136 | tf_op jit(solution)/shard_map/ppermute | solution.py:222
  22.2 8.9 %collective-permute-start.4 = (bf16[1,2,448,128]{3,2,0,1:T(8,128)(2,1)S(1)}, bf16[1,2,448,128]{3,2,0,1:T(8,128)(2,1)S(1)}, u32[]{:S(2)}, u32[]{:S(2)}) collective-permute-start(bf16[1,2,448,128]{3,2,0,1:T(8,128)(2,1)S(1)} %broadcast_select_fusion.2), channel_id=1, source_target_pairs={{0,16},{8,24},{16,0},{24,8},{1,17},{9,25},{17,1},{25,9},{2,18},{10... | collective-permute-start | bytes 688136 | tf_op jit(solution)/shard_map/ppermute | solution.py:198
  25.1 7.7 %collective-permute-start.3 = (bf16[1,2,448,128]{3,2,0,1:T(8,128)(2,1)S(1)}, bf16[1,2,448,128]{3,2,0,1:T(8,128)(2,1)S(1)}, u32[]{:S(2)}, u32[]{:S(2)}) collective-permute-start(bf16[1,2,448,128]{3,2,0,1:T(8,128)(2,1)S(1)} %broadcast_select_fusion.2), channel_id=1, source_target_pairs={{0,8},{8,0},{16,24},{24,16},{1,9},{9,1},{17,25},{25,17},{2,10},{10... | collective-permute-start | bytes 688136 | tf_op jit(solution)/shard_map/ppermute | solution.py:198
  31.2 4.9 %collective-permute-start.6 = (bf16[1,448,128]{2,1,0:T(8,128)(2,1)S(1)}, bf16[1,448,128]{2,1,0:T(8,128)(2,1)S(1)}, u32[]{:S(2)}, u32[]{:S(2)}) collective-permute-start(bf16[1,448,128]{2,1,0:T(8,128)(2,1)S(1)} %slice_bitcast_fusion.4), channel_id=1, source_target_pairs={{0,8},{8,0},{16,24},{24,16},{1,9},{9,1},{17,25},{25,17},{2,10},{10... | collective-permute-start | bytes 344072 | tf_op jit(solution)/shard_map/ppermute | solution.py:203
  32.8 4.9 %collective-permute-start.5 = (bf16[1,448,128]{2,1,0:T(8,128)(2,1)S(1)}, bf16[1,448,128]{2,1,0:T(8,128)(2,1)S(1)}, u32[]{:S(2)}, u32[]{:S(2)}) collective-permute-start(bf16[1,448,128]{2,1,0:T(8,128)(2,1)S(1)} %slice_bitcast_fusion.5), channel_id=1, source_target_pairs={{0,16},{8,24},{16,0},{24,8},{1,17},{9,25},{17,1},{25,9},{2,18},{10... | collective-permute-start | bytes 344072 | tf_op jit(solution)/shard_map/ppermute | solution.py:202
  45.3 6.1 %collective-permute-start.13 = (bf16[1,2,448,128]{3,2,1,0:T(8,128)(2,1)S(1)}, bf16[1,2,448,128]{3,2,1,0:T(8,128)(2,1)S(1)}, u32[]{:S(2)}, u32[]{:S(2)}) collective-permute-start(bf16[1,2,448,128]{3,2,1,0:T(8,128)(2,1)S(1)} %collective-permute-done.2.own), channel_id=1, source_target_pairs={{0,16},{8,24},{16,0},{24,8},{1,17},{9,25},{17,1},{25,9},{2,18},{10... | collective-permute-start | bytes 688136 | tf_op jit(solution)/shard_map/ppermute | solution.py:198
  46.9 8.2 %collective-permute-start.7 = (f16[1,128,3456]{2,1,0:T(8,128)(2,1)S(1)}, f16[1,128,3456]{2,1,0:T(8,128)(2,1)S(1)}, u32[]{:S(2)}, u32[]{:S(2)}) collective-permute-start(f16[1,128,3456]{2,1,0:T(8,128)(2,1)S(1)} %convert_element_type.92), channel_id=1, source_target_pairs={{0,1},{1,0},{2,3},{3,2},{4,5},{5,4},{6,7},{7,6},{8,9},{9,8},{10,11... | collective-permute-start | bytes 2654216 | tf_op jit(solution)/shard_map/ppermute | solution.py:207
  47.0 9.8 %collective-permute-start.11 = (f16[2,32,3456]{2,1,0:T(8,128)(2,1)S(1)}, f16[2,32,3456]{2,1,0:T(8,128)(2,1)S(1)}, u32[]{:S(2)}, u32[]{:S(2)}) collective-permute-start(f16[2,32,3456]{2,1,0:T(8,128)(2,1)S(1)} %get-tuple-element.86), channel_id=1, source_target_pairs={{1,0},{2,1},{3,2},{4,3},{5,4},{6,5},{7,6},{0,7},{9,8},{10,9},{11,1... | collective-permute-start | bytes 1327112 | tf_op jit(solution)/shard_map/ppermute | solution.py:227
  48.7 13.4 %collective-permute-start.10 = (f16[2,32,3456]{2,1,0:T(8,128)(2,1)S(1)}, f16[2,32,3456]{2,1,0:T(8,128)(2,1)S(1)}, u32[]{:S(2)}, u32[]{:S(2)}) collective-permute-start(f16[2,32,3456]{2,1,0:T(8,128)(2,1)S(1)} %get-tuple-element.87), channel_id=1, source_target_pairs={{0,1},{1,2},{2,3},{3,4},{4,5},{5,6},{6,7},{7,0},{8,9},{9,10},{10,1... | collective-permute-start | bytes 1327112 | tf_op jit(solution)/shard_map/ppermute | solution.py:226
  48.7 6.4 %collective-permute-start.12 = (bf16[1,2,448,128]{3,2,1,0:T(8,128)(2,1)S(1)}, bf16[1,2,448,128]{3,2,1,0:T(8,128)(2,1)S(1)}, u32[]{:S(2)}, u32[]{:S(2)}) collective-permute-start(bf16[1,2,448,128]{3,2,1,0:T(8,128)(2,1)S(1)} %collective-permute-done.2.own), channel_id=1, source_target_pairs={{0,8},{8,0},{16,24},{24,16},{1,9},{9,1},{17,25},{25,17},{2,10},{10... | collective-permute-start | bytes 688136 | tf_op jit(solution)/shard_map/ppermute | solution.py:198
  62.1 5.3 %collective-permute-start.14 = (bf16[1,448,128]{2,1,0:T(8,128)(2,1)S(1)}, bf16[1,448,128]{2,1,0:T(8,128)(2,1)S(1)}, u32[]{:S(2)}, u32[]{:S(2)}) collective-permute-start(bf16[1,448,128]{2,1,0:T(8,128)(2,1)S(1)} %slice_bitcast_fusion.3), channel_id=1, source_target_pairs={{0,16},{8,24},{16,0},{24,8},{1,17},{9,25},{17,1},{25,9},{2,18},{10... | collective-permute-start | bytes 344072 | tf_op jit(solution)/shard_map/ppermute | solution.py:202
  62.6 5.1 %collective-permute-start.15 = (bf16[1,448,128]{2,1,0:T(8,128)(2,1)S(1)}, bf16[1,448,128]{2,1,0:T(8,128)(2,1)S(1)}, u32[]{:S(2)}, u32[]{:S(2)}) collective-permute-start(bf16[1,448,128]{2,1,0:T(8,128)(2,1)S(1)} %slice_bitcast_fusion.2), channel_id=1, source_target_pairs={{0,8},{8,0},{16,24},{24,16},{1,9},{9,1},{17,25},{25,17},{2,10},{10... | collective-permute-start | bytes 344072 | tf_op jit(solution)/shard_map/ppermute | solution.py:203
  75.8 2.4 %copy-start.3 = (s32[4,32]{1,0:T(4,128)S(1)}, s32[4,32]{1,0:T(4,128)}, u32[]{:S(2)}) copy-start(s32[4,32]{1,0:T(4,128)} %param.7) | copy-start | bytes 1540
  75.8 2.4 %copy-start.2 = (s32[3456]{0:T(1024)S(1)}, s32[3456]{0:T(1024)}, u32[]{:S(2)}) copy-start(s32[3456]{0:T(1024)} %param.6) | copy-start | bytes 41476
  75.9 11.8 %collective-permute-start.18 = (bf16[2,2,448,128]{3,2,0,1:T(8,128)(2,1)S(1)}, bf16[2,2,448,128]{3,2,0,1:T(8,128)(2,1)S(1)}, u32[]{:S(2)}, u32[]{:S(2)}) collective-permute-start(bf16[2,2,448,128]{3,2,0,1:T(8,128)(2,1)S(1)} %pad_maximum_fusion.2), channel_id=1, source_target_pairs={{0,16},{8,24},{16,0},{24,8},{1,17},{9,25},{17,1},{25,9},{2,18},{10... | collective-permute-start | bytes 1376264 | tf_op jit(solution)/shard_map/ppermute | solution.py:198
  77.5 11.3 %collective-permute-start.17 = (bf16[2,2,448,128]{3,2,0,1:T(8,128)(2,1)S(1)}, bf16[2,2,448,128]{3,2,0,1:T(8,128)(2,1)S(1)}, u32[]{:S(2)}, u32[]{:S(2)}) collective-permute-start(bf16[2,2,448,128]{3,2,0,1:T(8,128)(2,1)S(1)} %pad_maximum_fusion.2), channel_id=1, source_target_pairs={{0,8},{8,0},{16,24},{24,16},{1,9},{9,1},{17,25},{25,17},{2,10},{10... | collective-permute-start | bytes 1376264 | tf_op jit(solution)/shard_map/ppermute | solution.py:198
  78.2 10.7 %collective-permute-start.16 = (f16[1,128,3456]{2,1,0:T(8,128)(2,1)S(1)}, f16[1,128,3456]{2,1,0:T(8,128)(2,1)S(1)}, u32[]{:S(2)}, u32[]{:S(2)}) collective-permute-start(f16[1,128,3456]{2,1,0:T(8,128)(2,1)S(1)} %convert_element_type.96), channel_id=1, source_target_pairs={{0,1},{1,0},{2,3},{3,2},{4,5},{5,4},{6,7},{7,6},{8,9},{9,8},{10,11... | collective-permute-start | bytes 2654216 | tf_op jit(solution)/shard_map/ppermute | solution.py:207
  78.8 22.3 %collective-permute-start.22 = (f16[128,3456]{1,0:T(8,128)(2,1)S(1)}, f16[128,3456]{1,0:T(8,128)(2,1)S(1)}, u32[]{:S(2)}, u32[]{:S(2)}) collective-permute-start(f16[128,3456]{1,0:T(8,128)(2,1)S(1)} %bitcast_convert_fusion.2), channel_id=1, source_target_pairs={{0,2},{1,3},{6,4},{7,5},{8,10},{9,11},{14,12},{15,13},{16,18},{17,... | collective-permute-start | bytes 2654216 | tf_op jit(solution)/shard_map/ppermute | solution.py:233
  101.2 8.8 %collective-permute-start.19 = (bf16[2,448,128]{2,1,0:T(8,128)(2,1)S(1)}, bf16[2,448,128]{2,1,0:T(8,128)(2,1)S(1)}, u32[]{:S(2)}, u32[]{:S(2)}) collective-permute-start(bf16[2,448,128]{2,1,0:T(8,128)(2,1)S(1)} %slice_bitcast_fusion.1), channel_id=1, source_target_pairs={{0,16},{8,24},{16,0},{24,8},{1,17},{9,25},{17,1},{25,9},{2,18},{10... | collective-permute-start | bytes 688136 | tf_op jit(solution)/shard_map/ppermute | solution.py:202
  101.9 8.0 %collective-permute-start.20 = (bf16[2,448,128]{2,1,0:T(8,128)(2,1)S(1)}, bf16[2,448,128]{2,1,0:T(8,128)(2,1)S(1)}, u32[]{:S(2)}, u32[]{:S(2)}) collective-permute-start(bf16[2,448,128]{2,1,0:T(8,128)(2,1)S(1)} %slice_bitcast_fusion), channel_id=1, source_target_pairs={{0,8},{8,0},{16,24},{24,16},{1,9},{9,1},{17,25},{25,17},{2,10},{10... | collective-permute-start | bytes 688136 | tf_op jit(solution)/shard_map/ppermute | solution.py:203
  103.2 22.6 %collective-permute-start.23 = (f16[128,3456]{1,0:T(8,128)(2,1)S(1)}, f16[128,3456]{1,0:T(8,128)(2,1)S(1)}, u32[]{:S(2)}, u32[]{:S(2)}) collective-permute-start(f16[128,3456]{1,0:T(8,128)(2,1)S(1)} %bitcast_convert_fusion.1), channel_id=1, source_target_pairs={{0,2},{1,3},{6,4},{7,5},{8,10},{9,11},{14,12},{15,13},{16,18},{17,... | collective-permute-start | bytes 2654216 | tf_op jit(solution)/shard_map/ppermute | solution.py:242
  108.1 22.2 %collective-permute-start.26 = (f16[128,3456]{1,0:T(8,128)(2,1)S(1)}, f16[128,3456]{1,0:T(8,128)(2,1)S(1)}, u32[]{:S(2)}, u32[]{:S(2)}) collective-permute-start(f16[128,3456]{1,0:T(8,128)(2,1)S(1)} %fusion.21), channel_id=1, source_target_pairs={{2,4},{3,5},{4,2},{5,3},{10,12},{11,13},{12,10},{13,11},{18,20},{1... | collective-permute-start | bytes 2654216 | tf_op jit(solution)/shard_map/ppermute | solution.py:243
  121.1 3.8 %collective-permute-start.21 = (f16[2,128,3456]{2,1,0:T(8,128)(2,1)S(1)}, f16[2,128,3456]{2,1,0:T(8,128)(2,1)S(1)}, u32[]{:S(2)}, u32[]{:S(2)}) collective-permute-start(f16[2,128,3456]{2,1,0:T(8,128)(2,1)S(1)} %convert_element_type.103), channel_id=1, source_target_pairs={{0,1},{1,0},{2,3},{3,2},{4,5},{5,4},{6,7},{7,6},{8,9},{9,8},{10,11... | collective-permute-start | bytes 5308424 | tf_op jit(solution)/shard_map/ppermute | solution.py:207
  125.8 21.7 %collective-permute-start.24 = (f16[128,3456]{1,0:T(8,128)(2,1)S(1)}, f16[128,3456]{1,0:T(8,128)(2,1)S(1)}, u32[]{:S(2)}, u32[]{:S(2)}) collective-permute-start(f16[128,3456]{1,0:T(8,128)(2,1)S(1)} %bitcast_convert_fusion), channel_id=1, source_target_pairs={{0,2},{1,3},{6,4},{7,5},{8,10},{9,11},{14,12},{15,13},{16,18},{17,... | collective-permute-start | bytes 2654216 | tf_op jit(solution)/shard_map/ppermute | solution.py:247
  131.1 16.5 %collective-permute-start.25 = (f16[128,3456]{1,0:T(8,128)(2,1)S(1)}, f16[128,3456]{1,0:T(8,128)(2,1)S(1)}, u32[]{:S(2)}, u32[]{:S(2)}) collective-permute-start(f16[128,3456]{1,0:T(8,128)(2,1)S(1)} %get-tuple-element.83), channel_id=1, source_target_pairs={{2,4},{3,5},{4,2},{5,3},{10,12},{11,13},{12,10},{13,11},{18,20},{1... | collective-permute-start | bytes 2654216 | tf_op jit(solution)/shard_map/ppermute | solution.py:248
  131.8 21.5 %collective-permute-start.27 = (f16[128,3456]{1,0:T(8,128)(2,1)S(1)}, f16[128,3456]{1,0:T(8,128)(2,1)S(1)}, u32[]{:S(2)}, u32[]{:S(2)}) collective-permute-start(f16[128,3456]{1,0:T(8,128)(2,1)S(1)} %get-tuple-element.84), channel_id=1, source_target_pairs={{4,6},{5,7},{2,0},{3,1},{12,14},{13,15},{10,8},{11,9},{20,22},{21,... | collective-permute-start | bytes 2654216 | tf_op jit(solution)/shard_map/ppermute | solution.py:249

commit v3 on v2

--- a/solution.py
+++ b/solution.py
@@ -94,7 +94,7 @@
 def product_kernel(place, own, gx, gy, dx, dy, c_ref, keep_ref, send_ref, scale_ref, rows, lhs, *, piece, bound):
     slots = own.shape[0]
 
-    @pl.when(pl.program_id(0) == 0)
+    @pl.when(place[2] >= 0)
     def _():
         for s in range(slots):
             for side in range(2):
@@ -103,10 +103,14 @@
                 top = jnp.zeros((TAIL, LANES), F32)
                 for q, part in parts:
                     at = pl.multiple_of((place[2] ^ q) * piece, TAIL)
-                    rows[pl.ds(at, piece), :] = part[:piece, :]
+                    rows[2 * s + side, pl.ds(at, piece), :] = part[:piece, :]
                     top = jnp.maximum(top, part[piece:, :].astype(F32))
-                lhs[(2 * s + side) * LANES : (2 * s + side + 1) * LANES, :] = rows[...].T
                 scale_ref[s, side] = bound / top[:8, :]
+
+    @pl.when(place[1] >= 0)
+    def _():
+        for k in range(2 * slots):
+            lhs[k * LANES : (k + 1) * LANES, :] = rows[k].T
 
     for s in range(slots):
         out = jnp.dot(lhs[2 * s * LANES : 2 * (s + 1) * LANES, :], c_ref[...], preferred_element_type=F32)
@@ -118,20 +122,15 @@
     slots = own.shape[0]
     piece = own.shape[2] - TAIL
     depth, columns = matrix.shape
-    block = columns // 3
-    whole = lambda a: pl.BlockSpec(a.shape, lambda n: (0,) * a.ndim)
     out = jax.ShapeDtypeStruct((slots, LANES, columns), F32)
-    out_spec = pl.BlockSpec((slots, LANES, block), lambda n: (0, 0, n))
+    vmem = pl.BlockSpec(memory_space=pltpu.VMEM)
     return pl.pallas_call(
         functools.partial(product_kernel, piece=piece, bound=HALF_MAX / (vels * columns * COLLISION_MAX)),
-        grid=(columns // block,),
         out_shape=(out, out, jax.ShapeDtypeStruct((slots, 2, 8, LANES), F32)),
-        in_specs=[pl.BlockSpec(memory_space=pltpu.SMEM)]
-        + [whole(a) for a in (own, gx, gy, dx, dy)]
-        + [pl.BlockSpec((depth, block), lambda n: (0, n))],
-        out_specs=(out_spec, out_spec, pl.BlockSpec((slots, 2, 8, LANES), lambda n: (0, 0, 0, 0))),
-        scratch_shapes=[pltpu.VMEM((depth, LANES), BF16), pltpu.VMEM((slots * 2 * LANES, depth), BF16)],
-        compiler_params=pltpu.CompilerParams(vmem_limit_bytes=18 << 20),
+        in_specs=[pl.BlockSpec(memory_space=pltpu.SMEM)] + [vmem] * 6,
+        out_specs=(vmem, vmem, vmem),
+        scratch_shapes=[pltpu.VMEM((2 * slots, depth, LANES), BF16), pltpu.VMEM((slots * 2 * LANES, depth), BF16)],
+        compiler_params=pltpu.CompilerParams(vmem_limit_bytes=8 << 20),
         cost_estimate=pl.CostEstimate(
             flops=2 * slots * 2 * LANES * depth * columns,
             bytes_accessed=depth * columns * 2 + slots * 2 * LANES * columns * 4,
@@ -139,6 +138,25 @@
         ),
         name="product",
     )(place, own, gx, gy, dx, dy, matrix)
+
+
+def load_kernel(c_ref, out_ref, sem):
+    copy = pltpu.make_async_copy(c_ref, out_ref, sem)
+    copy.start()
+    copy.wait()
+
+
+def loaded(matrix):
+    return pl.pallas_call(
+        load_kernel,
+        out_shape=jax.ShapeDtypeStruct(matrix.shape, matrix.dtype),
+        in_specs=[pl.BlockSpec(memory_space=pltpu.HBM)],
+        out_specs=pl.BlockSpec(memory_space=pltpu.VMEM),
+        scratch_shapes=[pltpu.SemaphoreType.DMA],
+        compiler_params=pltpu.CompilerParams(vmem_limit_bytes=1 << 20),
+        cost_estimate=pl.CostEstimate(flops=1, bytes_accessed=2 * matrix.size * 2, transcendentals=0),
+        name="load",
+    )(matrix)
 
 
 def edge_kernel(place, a_ref, c_ref, d_ref, out_ref, *, cells):
@@ -182,7 +200,7 @@
     place = jnp.stack([cell >> 1, cell & 1, vel])
     is_end = jnp.logical_or(cell < 2, cell >= cells - 2)
     distribution, place, is_end, offset = lax.optimization_barrier((distribution, place, is_end, vel * local_vel))
-    matrix = pltpu.with_memory_space_constraint(collision.reshape(-1, local_vel), pltpu.HBM)
+    matrix = collision.reshape(-1, local_vel)
 
     other_core = [(i, i ^ 1) for i in range(cells)]
     across = lambda q: [(i, 2 * ((i // 2) ^ q) + i % 2) for i in range(cells)]
@@ -212,35 +230,38 @@
 
     keep, send = split_pieces(distribution, place, cells)
     got = lax.ppermute(send, "cell", other_core)
+    matrix = loaded(pltpu.with_memory_space_constraint(after(matrix, got), pltpu.HBM))
     both = [jnp.stack([keep[q], got[q]])[None] for q in range(4)]
 
     from_end = lax.ppermute(both[3], "cell", chips((0, 3), (3, 0)))
-    slot_a = jnp.where(is_end, from_end, both[0])
-    ga = gather_x_y(slot_a)
-    slot_b = lax.ppermute(after(both[2], from_end), "cell", across(2))
-    z1 = lax.ppermute(after(both[1], from_end), "cell", across(1))
-    from_middle = lax.ppermute(after(both[3], from_end), "cell", middle)
-    ga = gather_diagonal(ga)
+    ga = gather_x_y(jnp.where(is_end, from_end, both[0]))
+    slot_a = ga[0]
     own_top = keep[0:1, keep.shape[1] - 1 :, 0:1].astype(F32)
-    edges = after(distribution, slot_b, z1, from_middle) * (HALF_MAX / own_top)
+    edges = after(distribution, from_end) * (HALF_MAX / own_top)
     from_below = lax.ppermute(edges[tile_len - 2 :].astype(F16), "cell", ring)
     from_above = lax.ppermute(edges[:2].astype(F16), "cell", [(j, i) for i, j in ring])
-
-    mine_a, theirs_a, scale_a = product(place, *behind(ga, slot_b), matrix, 4)
-    gb = gather_x_y(after(slot_b, theirs_a))
+    ga = gather_diagonal(ga)
+    mine_a, theirs_a, scale_a = product(place, *ga, matrix, 4)
+    theirs_a, both1, both2, both3, from_below, from_above = lax.optimization_barrier(
+        (theirs_a, both[1], both[2], both[3], from_below, from_above)
+    )
+    slot_b = lax.ppermute(both2, "cell", across(2))
+    z1 = lax.ppermute(both1, "cell", across(1))
+    from_middle = lax.ppermute(both3, "cell", middle)
     (pa,) = exchanged(mine_a, theirs_a)
-    ma = after(pa.astype(F16), from_below, from_above)
+    ma, slot_b, z1, from_middle = lax.optimization_barrier((pa.astype(F16), slot_b, z1, from_middle))
     a0 = lax.ppermute(ma, "cell", ends)
-    gb = gather_diagonal(gb, ma)
-    mine_b, theirs_b, _ = product(place, *behind(gb, ma), matrix, 4)
-    z1, from_middle, both0, _ = lax.optimization_barrier((z1, from_middle, both[0], theirs_b))
-    slot_c = jnp.where(is_end, z1, from_middle)
-    slot_d = jnp.where(is_end, both0, z1)
-    gcd = gather_x_y(jnp.concatenate([slot_c, slot_d]))
+    gb = gather_x_y(slot_b)
+    gb = gather_diagonal(gb)
+    mine_b, theirs_b, _ = product(place, *gb, matrix, 4)
     (pb,) = exchanged(mine_b, theirs_b)
     mb = pb.astype(F16)
     a1 = lax.ppermute(after(mb, a0), "cell", ends)
     b1 = lax.ppermute((pb + a0.astype(F32)).astype(F16), "cell", middle)
+    z1, from_middle, both0, _ = lax.optimization_barrier((z1, from_middle, both[0], a0))
+    slot_c = jnp.where(is_end, z1, from_middle)
+    slot_d = jnp.where(is_end, both0, z1)
+    gcd = gather_x_y(jnp.concatenate([slot_c, slot_d]))
     gcd = gather_diagonal(gcd, mb)
     mine_cd, theirs_cd, scale_cd = product(place, *behind(gcd, mb), matrix, 4)
     pc, pd = exchanged(mine_cd, theirs_cd)

time: 156 us -> 140 us (0.90)
  waiting for transfers between devices: 70.1 us -> 53.2 us
  starting transfers between devices: 41.8 us -> 47.5 us
  Pallas kernels: 28.2 us -> 23.8 us
    pallas_call x3, Pallas kernels: 26.6 us -> 17.6 us  [product(): pl.pallas_call(functools.partial(product_kernel, piece=piece, bound=HALF_...]
    ppermute x1, waiting for transfers between devices: 12 us -> 5.58 us  [chain_body(): a0 = lax.ppermute(ma, 'cell', ends)]
    ppermute x6, waiting for transfers between devices: 12.9 us -> 6.77 us  [gather_x_y(): return (own, lax.ppermute(own, 'vel', in_x), lax.ppermute(own, 'vel', in_y))]
    ppermute x1, waiting for transfers between devices: 5.84 us -> 0.07 us  [chain_body(): from_end = lax.ppermute(both[3], 'cell', chips((0, 3), (3, 0)))]
    ppermute x1, waiting for transfers between devices: 5.24 us -> 0.01 us  [chain_body(): from_below = lax.ppermute(edges[tile_len - 2:].astype(F16), 'cell', ring)]
    ppermute x3, waiting for transfers between devices: 4.51 us -> 9.72 us  [the longest x1 9.71 us: chain_body(): slot_b = lax.ppermute(both2, 'cell', across(2))]
    pallas_call x0 -> x1, Pallas kernels: none -> 4.53 us  [loaded(): pl.pallas_call(load_kernel, out_shape=jax.ShapeDtypeStruct(matrix.shape,...]
    ppermute x1, starting transfers between devices: 2.84 us -> 7.01 us  [chain_body(): a0 = lax.ppermute(ma, 'cell', ends)]
  transfers between devices with their start and end apart: 28 -> 28, of which waited for: 18 -> 16; matrix products, arithmetic and copies ran while one was open for 6% -> 6% of each run, Pallas kernels for 7% -> 16%
where the time goes in v3:
time: 140 us
  waiting for transfers between devices  53.2 us (38%)
  starting transfers between devices  47.5 us (34%)
  Pallas kernels  23.8 us (17%)
  other arithmetic  8.52 us (6%)
  local copies, waits for them, and re-layouts  4.44 us (3%)
  between operations  2.42 us (2%)
    pallas_call x3, Pallas kernels, product(): pl.pallas_call(functools.partial(product_kernel, piece=piece, bound=HALF_...  17.6 us
    ppermute x1, waiting for transfers between devices, chain_body(): a2 = lax.ppermute(after(pc.astype(F16), a1), 'cell', ends)  11.9 us
    ppermute x1, waiting for transfers between devices, chain_body(): slot_b = lax.ppermute(both2, 'cell', across(2))  9.71 us
    ppermute x6, starting transfers between devices, gather_x_y(): return (own, lax.ppermute(own, 'vel', in_x), lax.ppermute(own, 'vel', in_y))  7.19 us
    ppermute x1, starting transfers between devices, chain_body(): a0 = lax.ppermute(ma, 'cell', ends)  7.01 us
    ppermute x1, starting transfers between devices, chain_body(): from_end = lax.ppermute(both[3], 'cell', chips((0, 3), (3, 0)))  6.88 us
    ppermute x6, waiting for transfers between devices, gather_x_y(): return (own, lax.ppermute(own, 'vel', in_x), lax.ppermute(own, 'vel', in_y))  6.77 us
    ppermute x1, waiting for transfers between devices, chain_body(): c2 = lax.ppermute((pd + b1.astype(F32)).astype(F16), 'cell', outward)  5.72 us
  transfers between devices with their start and end apart: 28, of which 16 were waited for; matrix products, arithmetic and copies ran while one was open for 6% of the time, Pallas kernels for 16%

profile of v3, /device:TPU:0, one launch (start us, length us, event | category | flops | bytes accessed | tf_op | source)
XLA Modules:
  0.0 139.8 jit_solution(12272074999120038974)
XLA Ops:
  0.1 1.5 %copy-done = f32[4,32,3456]{2,1,0:T(8,128)S(1)} copy-done((f32[4,32,3456]{2,1,0:T(8,128)S(1)}, f32[4,32,3456]{2,1,0:T(8,128)}, u32[]{:S(2)}) %copy-start) | copy-done | bytes 1769496
  1.6 1.1 pieces.1
  2.6 0.5 collective-permute-start
  3.2 1.4 %collective-permute-done = bf16[4,448,128]{2,1,0:T(8,128)(2,1)S(1)} collective-permute-done((bf16[4,448,128]{2,1,0:T(8,128)(2,1)S(1)}, bf16[4,448,128]{2,1,0:T(8,128)(2,1)S(1)}, u32[]{:S(2)}, u32[]{:S(2)}) %collective-permute-start) | collective-permute-done | bytes 458784 | tf_op jit(solution)/shard_map/ppermute | solution.py:232
  4.7 6.9 %collective-permute-start.1 = (bf16[1,2,448,128]{3,2,0,1:T(8,128)(2,1)S(1)}, bf16[1,2,448,128]{3,2,0,1:T(8,128)(2,1)S(1)}, u32[]{:S(2)}, u32[]{:S(2)}) collective-permute-start(bf16[1,2,448,128]{3,2,0,1:T(8,128)(2,1)S(1)} %maximum_bitcast_fusion), channel_id=1, source_target_pairs={{0,6},{1,7},{6,0},{7,1},{8,14},{9,15},{14,8},{15,9},{16,22},{17,23... | collective-permute-start | bytes 688136 | tf_op jit(solution)/shard_map/ppermute | solution.py:236
  11.6 0.5 slice.115
  12.8 4.5 %load.1.c_ref = bf16[1728,3456]{1,0:T(8,128)(2,1)S(1)} custom-call(bf16[1728,3456]{1,0:T(8,128)(2,1)} %bitcast.72), custom_call_target="tpu_custom_call" | custom-call | flops 1 | bytes 23887872 | tf_op jit(solution)/shard_map/load/pallas_call | solution.py:150
  17.5 1.6 %collective-permute-start.3 = (bf16[1,2,448,128]{3,2,0,1:T(8,128)(2,1)S(1)}, bf16[1,2,448,128]{3,2,0,1:T(8,128)(2,1)S(1)}, u32[]{:S(2)}, u32[]{:S(2)}) collective-permute-start(bf16[1,2,448,128]{3,2,0,1:T(8,128)(2,1)S(1)} %broadcast_select_fusion.2), channel_id=1, source_target_pairs={{0,16},{8,24},{16,0},{24,8},{1,17},{9,25},{17,1},{25,9},{2,18},{10... | collective-permute-start | bytes 688136 | tf_op jit(solution)/shard_map/ppermute | solution.py:216
  19.1 1.5 %collective-permute-start.2 = (bf16[1,2,448,128]{3,2,0,1:T(8,128)(2,1)S(1)}, bf16[1,2,448,128]{3,2,0,1:T(8,128)(2,1)S(1)}, u32[]{:S(2)}, u32[]{:S(2)}) collective-permute-start(bf16[1,2,448,128]{3,2,0,1:T(8,128)(2,1)S(1)} %broadcast_select_fusion.2), channel_id=1, source_target_pairs={{0,8},{8,0},{16,24},{24,16},{1,9},{9,1},{17,25},{25,17},{2,10},{10... | collective-permute-start | bytes 688136 | tf_op jit(solution)/shard_map/ppermute | solution.py:216
  20.6 0.1 multiply_convert_fusion
  20.7 0.1 fusion.32
  20.9 1.9 %collective-permute-start.7 = (f16[2,32,3456]{2,1,0:T(8,128)(2,1)S(1)}, f16[2,32,3456]{2,1,0:T(8,128)(2,1)S(1)}, u32[]{:S(2)}, u32[]{:S(2)}) collective-permute-start(f16[2,32,3456]{2,1,0:T(8,128)(2,1)S(1)} %get-tuple-element.90), channel_id=1, source_target_pairs={{1,0},{2,1},{3,2},{4,3},{5,4},{6,5},{7,6},{0,7},{9,8},{10,9},{11,1... | collective-permute-start | bytes 1327112 | tf_op jit(solution)/shard_map/ppermute | solution.py:242
  22.8 2.0 %collective-permute-done.3 = bf16[1,2,448,128]{3,2,0,1:T(8,128)(2,1)S(1)} collective-permute-done((bf16[1,2,448,128]{3,2,0,1:T(8,128)(2,1)S(1)}, bf16[1,2,448,128]{3,2,0,1:T(8,128)(2,1)S(1)}, u32[]{:S(2)}, u32[]{:S(2)}) %collective-permute-start.3) | collective-permute-done | bytes 229408 | tf_op jit(solution)/shard_map/ppermute | solution.py:216
  24.9 1.6 %collective-permute-start.5 = (bf16[1,448,128]{2,1,0:T(8,128)(2,1)S(1)}, bf16[1,448,128]{2,1,0:T(8,128)(2,1)S(1)}, u32[]{:S(2)}, u32[]{:S(2)}) collective-permute-start(bf16[1,448,128]{2,1,0:T(8,128)(2,1)S(1)} %slice_bitcast_fusion.4), channel_id=1, source_target_pairs={{0,8},{8,0},{16,24},{24,16},{1,9},{9,1},{17,25},{25,17},{2,10},{10... | collective-permute-start | bytes 344072 | tf_op jit(solution)/shard_map/ppermute | solution.py:221
  26.4 1.6 %collective-permute-start.4 = (bf16[1,448,128]{2,1,0:T(8,128)(2,1)S(1)}, bf16[1,448,128]{2,1,0:T(8,128)(2,1)S(1)}, u32[]{:S(2)}, u32[]{:S(2)}) collective-permute-start(bf16[1,448,128]{2,1,0:T(8,128)(2,1)S(1)} %slice_bitcast_fusion.5), channel_id=1, source_target_pairs={{0,16},{8,24},{16,0},{24,8},{1,17},{9,25},{17,1},{25,9},{2,18},{10... | collective-permute-start | bytes 344072 | tf_op jit(solution)/shard_map/ppermute | solution.py:220
  28.1 1.7 %collective-permute-done.5.dy = bf16[1,448,128]{2,1,0:T(8,128)(2,1)S(1)} collective-permute-done((bf16[1,448,128]{2,1,0:T(8,128)(2,1)S(1)}, bf16[1,448,128]{2,1,0:T(8,128)(2,1)S(1)}, u32[]{:S(2)}, u32[]{:S(2)}) %collective-permute-start.5) | collective-permute-done | bytes 114720 | tf_op jit(solution)/shard_map/ppermute | solution.py:221
  29.7 1.6 %collective-permute-done.4.dx = bf16[1,448,128]{2,1,0:T(8,128)(2,1)S(1)} collective-permute-done((bf16[1,448,128]{2,1,0:T(8,128)(2,1)S(1)}, bf16[1,448,128]{2,1,0:T(8,128)(2,1)S(1)}, u32[]{:S(2)}, u32[]{:S(2)}) %collective-permute-start.4) | collective-permute-done | bytes 114720 | tf_op jit(solution)/shard_map/ppermute | solution.py:220
  31.3 4.4 %product.3 = (f32[1,128,3456]{2,1,0:T(8,128)S(1)}, f32[1,128,3456]{2,1,0:T(8,128)S(1)}, f32[1,2,8,128]{3,2,1,0:T(8,128)S(1)}) custom-call(s32[3]{0:T(128)S(1)} %pad_add_fusion.place, bf16[1,2,448,128]{3,2,1,0:T(8,128)(2,1)S(1)} %fusion.36.own, bf16[1,2,448,128]{3,2,1,0:T(8,128)(2,1)S(1)} %bitcast.71, bf16[1,2,448,128]{3,2,1,0:T(8,128)(2,1)S(1)} %bitcast.70, ...), custom_call_target="tpu_custom_call" | custom-call | flops 3057647616 | bytes 15482880 | tf_op jit(solution)/shard_map/product/pallas_call | solution.py:127
  35.8 0.1 convert_element_type.93
  36.0 3.6 %collective-permute-start.10 = (bf16[1,2,448,128]{3,2,0,1:T(8,128)(2,1)S(1)}, bf16[1,2,448,128]{3,2,0,1:T(8,128)(2,1)S(1)}, u32[]{:S(2)}, u32[]{:S(2)}) collective-permute-start(bf16[1,2,448,128]{3,2,0,1:T(8,128)(2,1)S(1)} %bitcast.74), channel_id=1, source_target_pairs={{0,2},{1,3},{2,0},{3,1},{4,6},{5,7},{6,4},{7,5},{8,10},{9,11},{10,... | collective-permute-start | bytes 688136 | tf_op jit(solution)/shard_map/ppermute | solution.py:249
  39.6 0.7 collective-permute-start.11
  40.3 0.2 bitcast_convert_fusion.2
  40.5 9.7 %collective-permute-done.9.own = bf16[1,2,448,128]{3,2,1,0:T(8,128)(2,1)S(1)} collective-permute-done((bf16[1,2,448,128]{3,2,1,0:T(8,128)(2,1)S(1)}, bf16[1,2,448,128]{3,2,1,0:T(8,128)(2,1)S(1)}, u32[]{:S(2)}, u32[]{:S(2)}) %collective-permute-start.9) | collective-permute-done | bytes 229408 | tf_op jit(solution)/shard_map/ppermute | solution.py:248
  50.2 1.5 %collective-permute-start.13 = (bf16[1,2,448,128]{3,2,1,0:T(8,128)(2,1)S(1)}, bf16[1,2,448,128]{3,2,1,0:T(8,128)(2,1)S(1)}, u32[]{:S(2)}, u32[]{:S(2)}) collective-permute-start(bf16[1,2,448,128]{3,2,1,0:T(8,128)(2,1)S(1)} %collective-permute-done.9.own), channel_id=1, source_target_pairs={{0,16},{8,24},{16,0},{24,8},{1,17},{9,25},{17,1},{25,9},{2,18},{10... | collective-permute-start | bytes 688136 | tf_op jit(solution)/shard_map/ppermute | solution.py:216
  51.8 0.5 collective-permute-start.12
  52.3 7.0 %collective-permute-start.17 = (f16[128,3456]{1,0:T(8,128)(2,1)S(1)}, f16[128,3456]{1,0:T(8,128)(2,1)S(1)}, u32[]{:S(2)}, u32[]{:S(2)}) collective-permute-start(f16[128,3456]{1,0:T(8,128)(2,1)S(1)} %bitcast_convert_fusion.2), channel_id=1, source_target_pairs={{0,2},{1,3},{6,4},{7,5},{8,10},{9,11},{14,12},{15,13},{16,18},{17,... | collective-permute-start | bytes 2654216 | tf_op jit(solution)/shard_map/ppermute | solution.py:253
  59.3 1.6 %collective-permute-start.15 = (bf16[1,448,128]{2,1,0:T(8,128)(2,1)S(1)}, bf16[1,448,128]{2,1,0:T(8,128)(2,1)S(1)}, u32[]{:S(2)}, u32[]{:S(2)}) collective-permute-start(bf16[1,448,128]{2,1,0:T(8,128)(2,1)S(1)} %slice_bitcast_fusion.2), channel_id=1, source_target_pairs={{0,8},{8,0},{16,24},{24,16},{1,9},{9,1},{17,25},{25,17},{2,10},{10... | collective-permute-start | bytes 344072 | tf_op jit(solution)/shard_map/ppermute | solution.py:221
  60.9 0.6 collective-permute-start.14
  61.5 2.7 %collective-permute-done.15.dy = bf16[1,448,128]{2,1,0:T(8,128)(2,1)S(1)} collective-permute-done((bf16[1,448,128]{2,1,0:T(8,128)(2,1)S(1)}, bf16[1,448,128]{2,1,0:T(8,128)(2,1)S(1)}, u32[]{:S(2)}, u32[]{:S(2)}) %collective-permute-start.15) | collective-permute-done | bytes 114720 | tf_op jit(solution)/shard_map/ppermute | solution.py:221
  64.2 1.6 %collective-permute-done.14.dx = bf16[1,448,128]{2,1,0:T(8,128)(2,1)S(1)} collective-permute-done((bf16[1,448,128]{2,1,0:T(8,128)(2,1)S(1)}, bf16[1,448,128]{2,1,0:T(8,128)(2,1)S(1)}, u32[]{:S(2)}, u32[]{:S(2)}) %collective-permute-start.14) | collective-permute-done | bytes 114720 | tf_op jit(solution)/shard_map/ppermute | solution.py:220
  65.8 4.8 %product.4 = (f32[1,128,3456]{2,1,0:T(8,128)S(1)}, f32[1,128,3456]{2,1,0:T(8,128)S(1)}, f32[1,2,8,128]{3,2,1,0:T(8,128)}) custom-call(s32[3]{0:T(128)S(1)} %pad_add_fusion.place, bf16[1,2,448,128]{3,2,1,0:T(8,128)(2,1)S(1)} %collective-permute-done.9.own, bf16[1,2,448,128]{3,2,1,0:T(8,128)(2,1)S(1)} %collective-permute-done.12.gx, ...), custom_call_target="tpu_custom_call" | custom-call | flops 3057647616 | bytes 15482880 | tf_op jit(solution)/shard_map/product/pallas_call | solution.py:127
  70.8 0.5 copy-done.2
  71.3 0.5 slice.133
  71.9 5.6 %collective-permute-done.17 = f16[128,3456]{1,0:T(8,128)(2,1)S(1)} collective-permute-done((f16[128,3456]{1,0:T(8,128)(2,1)S(1)}, f16[128,3456]{1,0:T(8,128)(2,1)S(1)}, u32[]{:S(2)}, u32[]{:S(2)}) %collective-permute-start.17) | collective-permute-done | bytes 884768 | tf_op jit(solution)/shard_map/ppermute | solution.py:253
  77.5 1.2 collective-permute-start.19
  78.7 0.9 collective-permute-start.18
  79.6 0.2 bitcast_convert_fusion.1
  79.9 4.4 %collective-permute-start.23 = (f16[128,3456]{1,0:T(8,128)(2,1)S(1)}, f16[128,3456]{1,0:T(8,128)(2,1)S(1)}, u32[]{:S(2)}, u32[]{:S(2)}) collective-permute-start(f16[128,3456]{1,0:T(8,128)(2,1)S(1)} %bitcast_convert_fusion.1), channel_id=1, source_target_pairs={{0,2},{1,3},{6,4},{7,5},{8,10},{9,11},{14,12},{15,13},{16,18},{17,... | collective-permute-start | bytes 2654216 | tf_op jit(solution)/shard_map/ppermute | solution.py:259
  84.3 3.9 %collective-permute-done.19 = bf16[2,2,448,128]{3,2,0,1:T(8,128)(2,1)S(1)} collective-permute-done((bf16[2,2,448,128]{3,2,0,1:T(8,128)(2,1)S(1)}, bf16[2,2,448,128]{3,2,0,1:T(8,128)(2,1)S(1)}, u32[]{:S(2)}, u32[]{:S(2)}) %collective-permute-start.19) | collective-permute-done | bytes 458784 | tf_op jit(solution)/shard_map/ppermute | solution.py:216
  88.3 0.8 collective-permute-done.18
  89.1 1.0 collective-permute-start.20
  90.1 1.5 %collective-permute-start.21 = (bf16[2,448,128]{2,1,0:T(8,128)(2,1)S(1)}, bf16[2,448,128]{2,1,0:T(8,128)(2,1)S(1)}, u32[]{:S(2)}, u32[]{:S(2)}) collective-permute-start(bf16[2,448,128]{2,1,0:T(8,128)(2,1)S(1)} %slice_bitcast_fusion), channel_id=1, source_target_pairs={{0,8},{8,0},{16,24},{24,16},{1,9},{9,1},{17,25},{25,17},{2,10},{10... | collective-permute-start | bytes 688136 | tf_op jit(solution)/shard_map/ppermute | solution.py:221
  91.6 0.3 fusion.21
  91.9 0.7 collective-permute-start.26
  92.6 0.6 edges.1
  93.2 0.6 fusion.35
  93.9 1.3 collective-permute-done.20.dx
  95.2 0.9 collective-permute-done.21.dy
  96.1 8.3 %product.5 = (f32[2,128,3456]{2,1,0:T(8,128)S(1)}, f32[2,128,3456]{2,1,0:T(8,128)S(1)}, f32[2,2,8,128]{3,2,1,0:T(8,128)S(1)}) custom-call(s32[3]{0:T(128)S(1)} %pad_add_fusion.place, bf16[2,2,448,128]{3,2,1,0:T(8,128)(2,1)S(1)} %copy.12.own, bf16[2,2,448,128]{3,2,1,0:T(8,128)(2,1)S(1)} %copy.13.gx, bf16[2,2,448,128]{3,2,1,0:T(8,128)(2,1)S(1)} %copy.14.gy, ...), custom_call_target="tpu_custom_call" | custom-call | flops 6115295232 | bytes 19021824 | tf_op jit(solution)/shard_map/product/pallas_call | solution.py:127
  104.4 0.2 convert_element_type.103
  104.7 0.7 convert_multiply_fusion.1
  105.4 0.7 convert_multiply_fusion
  106.1 2.2 %collective-permute-done.22 = f16[2,128,3456]{2,1,0:T(8,128)(2,1)S(1)} collective-permute-done((f16[2,128,3456]{2,1,0:T(8,128)(2,1)S(1)}, f16[2,128,3456]{2,1,0:T(8,128)(2,1)S(1)}, u32[]{:S(2)}, u32[]{:S(2)}) %collective-permute-start.22) | collective-permute-done | bytes 1769504 | tf_op jit(solution)/shard_map/ppermute | solution.py:225
  108.4 0.2 bitcast_convert_fusion
  108.6 4.4 %collective-permute-start.24 = (f16[128,3456]{1,0:T(8,128)(2,1)S(1)}, f16[128,3456]{1,0:T(8,128)(2,1)S(1)}, u32[]{:S(2)}, u32[]{:S(2)}) collective-permute-start(f16[128,3456]{1,0:T(8,128)(2,1)S(1)} %bitcast_convert_fusion), channel_id=1, source_target_pairs={{0,2},{1,3},{6,4},{7,5},{8,10},{9,11},{14,12},{15,13},{16,18},{17,... | collective-permute-start | bytes 2654216 | tf_op jit(solution)/shard_map/ppermute | solution.py:268
  113.0 0.8 fusion.19
  113.9 0.7 collective-permute-start.25
  114.6 1.3 collective-permute-start.27
  115.9 2.5 %fusion.6 = f32[4,32,3456]{2,1,0:T(8,128)S(1)} fusion(f32[4,32,3456]{2,1,0:T(8,128)S(1)} %copy-done.1, f32[2,32,3456]{2,1,0:T(8,128)S(1)} %convert_multiply_fusion, f32[2,32,3456]{2,1,0:T(8,128)S(1)} %convert_multiply_fusion.1, f32[3456]{0:T(1024)S(1)} %get-tuple-element.105, f32[3456]{0:T(1024)S(1)} %get-tuple-element.104, ...), kind=kLoop, calls=%fused_computation.14 | loop fusion | flops 9732096 | bytes 5343488 | tf_op jit(solution)/shard_map/mul | solution.py:57
  118.4 0.5 slice.132
  120.2 11.9 %collective-permute-done.24 = f16[128,3456]{1,0:T(8,128)(2,1)S(1)} collective-permute-done((f16[128,3456]{1,0:T(8,128)(2,1)S(1)}, f16[128,3456]{1,0:T(8,128)(2,1)S(1)}, u32[]{:S(2)}, u32[]{:S(2)}) %collective-permute-start.24) | collective-permute-done | bytes 884768 | tf_op jit(solution)/shard_map/ppermute | solution.py:268
  132.2 5.7 %collective-permute-done.27 = f16[128,3456]{1,0:T(8,128)(2,1)S(1)} collective-permute-done((f16[128,3456]{1,0:T(8,128)(2,1)S(1)}, f16[128,3456]{1,0:T(8,128)(2,1)S(1)}, u32[]{:S(2)}, u32[]{:S(2)}) %collective-permute-start.27) | collective-permute-done | bytes 884768 | tf_op jit(solution)/shard_map/ppermute | solution.py:270
  137.9 0.4 add_add_fusion
  138.3 1.5 %multiply_add_fusion = f32[4,32,3456]{2,1,0:T(8,128)} fusion(f32[4,32,3456]{2,1,0:T(8,128)S(1)} %fusion.6, f32[4,32,3456]{2,1,0:T(8,128)S(1)} %bitcast.73, f32[4,32]{1,0:T(4,128)S(1)} %bitcast.75), kind=kLoop, calls=%fused_computation.39 | loop fusion | flops 884736 | bytes 5308928 | tf_op jit(solution)/shard_map/add | solution.py:281
  (49 shorter events, 1.1 us)
Async XLA Ops:
  0.1 1.5 %copy-start = (f32[4,32,3456]{2,1,0:T(8,128)S(1)}, f32[4,32,3456]{2,1,0:T(8,128)}, u32[]{:S(2)}) copy-start(f32[4,32,3456]{2,1,0:T(8,128)} %param.4) | copy-start | bytes 5308420
  2.6 2.0 %collective-permute-start = (bf16[4,448,128]{2,1,0:T(8,128)(2,1)S(1)}, bf16[4,448,128]{2,1,0:T(8,128)(2,1)S(1)}, u32[]{:S(2)}, u32[]{:S(2)}) collective-permute-start(bf16[4,448,128]{2,1,0:T(8,128)(2,1)S(1)} %get-tuple-element.50), channel_id=1, source_target_pairs={{0,1},{1,0},{2,3},{3,2},{4,5},{5,4},{6,7},{7,6},{8,9},{9,8},{10,11... | collective-permute-start | bytes 1376264 | tf_op jit(solution)/shard_map/ppermute | solution.py:232
  4.7 12.8 %collective-permute-start.1 = (bf16[1,2,448,128]{3,2,0,1:T(8,128)(2,1)S(1)}, bf16[1,2,448,128]{3,2,0,1:T(8,128)(2,1)S(1)}, u32[]{:S(2)}, u32[]{:S(2)}) collective-permute-start(bf16[1,2,448,128]{3,2,0,1:T(8,128)(2,1)S(1)} %maximum_bitcast_fusion), channel_id=1, source_target_pairs={{0,6},{1,7},{6,0},{7,1},{8,14},{9,15},{14,8},{15,9},{16,22},{17,23... | collective-permute-start | bytes 688136 | tf_op jit(solution)/shard_map/ppermute | solution.py:236
  12.8 7.8 %copy-start.1 = (f32[4,32,3456]{2,1,0:T(8,128)S(1)}, f32[4,32,3456]{2,1,0:T(8,128)}, u32[]{:S(2)}) copy-start(f32[4,32,3456]{2,1,0:T(8,128)} %param.4) | copy-start | bytes 5308420
  17.5 7.4 %collective-permute-start.3 = (bf16[1,2,448,128]{3,2,0,1:T(8,128)(2,1)S(1)}, bf16[1,2,448,128]{3,2,0,1:T(8,128)(2,1)S(1)}, u32[]{:S(2)}, u32[]{:S(2)}) collective-permute-start(bf16[1,2,448,128]{3,2,0,1:T(8,128)(2,1)S(1)} %broadcast_select_fusion.2), channel_id=1, source_target_pairs={{0,16},{8,24},{16,0},{24,8},{1,17},{9,25},{17,1},{25,9},{2,18},{10... | collective-permute-start | bytes 688136 | tf_op jit(solution)/shard_map/ppermute | solution.py:216
  19.1 7.4 %collective-permute-start.2 = (bf16[1,2,448,128]{3,2,0,1:T(8,128)(2,1)S(1)}, bf16[1,2,448,128]{3,2,0,1:T(8,128)(2,1)S(1)}, u32[]{:S(2)}, u32[]{:S(2)}) collective-permute-start(bf16[1,2,448,128]{3,2,0,1:T(8,128)(2,1)S(1)} %broadcast_select_fusion.2), channel_id=1, source_target_pairs={{0,8},{8,0},{16,24},{24,16},{1,9},{9,1},{17,25},{25,17},{2,10},{10... | collective-permute-start | bytes 688136 | tf_op jit(solution)/shard_map/ppermute | solution.py:216
  20.9 14.9 %collective-permute-start.7 = (f16[2,32,3456]{2,1,0:T(8,128)(2,1)S(1)}, f16[2,32,3456]{2,1,0:T(8,128)(2,1)S(1)}, u32[]{:S(2)}, u32[]{:S(2)}) collective-permute-start(f16[2,32,3456]{2,1,0:T(8,128)(2,1)S(1)} %get-tuple-element.90), channel_id=1, source_target_pairs={{1,0},{2,1},{3,2},{4,3},{5,4},{6,5},{7,6},{0,7},{9,8},{10,9},{11,1... | collective-permute-start | bytes 1327112 | tf_op jit(solution)/shard_map/ppermute | solution.py:242
  22.8 13.0 %collective-permute-start.6 = (f16[2,32,3456]{2,1,0:T(8,128)(2,1)S(1)}, f16[2,32,3456]{2,1,0:T(8,128)(2,1)S(1)}, u32[]{:S(2)}, u32[]{:S(2)}) collective-permute-start(f16[2,32,3456]{2,1,0:T(8,128)(2,1)S(1)} %get-tuple-element.91), channel_id=1, source_target_pairs={{0,1},{1,2},{2,3},{3,4},{4,5},{5,6},{6,7},{7,0},{8,9},{9,10},{10,1... | collective-permute-start | bytes 1327112 | tf_op jit(solution)/shard_map/ppermute | solution.py:241
  24.9 4.9 %collective-permute-start.5 = (bf16[1,448,128]{2,1,0:T(8,128)(2,1)S(1)}, bf16[1,448,128]{2,1,0:T(8,128)(2,1)S(1)}, u32[]{:S(2)}, u32[]{:S(2)}) collective-permute-start(bf16[1,448,128]{2,1,0:T(8,128)(2,1)S(1)} %slice_bitcast_fusion.4), channel_id=1, source_target_pairs={{0,8},{8,0},{16,24},{24,16},{1,9},{9,1},{17,25},{25,17},{2,10},{10... | collective-permute-start | bytes 344072 | tf_op jit(solution)/shard_map/ppermute | solution.py:221
  26.4 4.9 %collective-permute-start.4 = (bf16[1,448,128]{2,1,0:T(8,128)(2,1)S(1)}, bf16[1,448,128]{2,1,0:T(8,128)(2,1)S(1)}, u32[]{:S(2)}, u32[]{:S(2)}) collective-permute-start(bf16[1,448,128]{2,1,0:T(8,128)(2,1)S(1)} %slice_bitcast_fusion.5), channel_id=1, source_target_pairs={{0,16},{8,24},{16,0},{24,8},{1,17},{9,25},{17,1},{25,9},{2,18},{10... | collective-permute-start | bytes 344072 | tf_op jit(solution)/shard_map/ppermute | solution.py:220
  35.9 4.4 %collective-permute-start.8 = (f16[1,128,3456]{2,1,0:T(8,128)(2,1)S(1)}, f16[1,128,3456]{2,1,0:T(8,128)(2,1)S(1)}, u32[]{:S(2)}, u32[]{:S(2)}) collective-permute-start(f16[1,128,3456]{2,1,0:T(8,128)(2,1)S(1)} %convert_element_type.93), channel_id=1, source_target_pairs={{0,1},{1,0},{2,3},{3,2},{4,5},{5,4},{6,7},{7,6},{8,9},{9,8},{10,11... | collective-permute-start | bytes 2654216 | tf_op jit(solution)/shard_map/ppermute | solution.py:225
  35.9 14.3 %collective-permute-start.9 = (bf16[1,2,448,128]{3,2,1,0:T(8,128)(2,1)S(1)}, bf16[1,2,448,128]{3,2,1,0:T(8,128)(2,1)S(1)}, u32[]{:S(2)}, u32[]{:S(2)}) collective-permute-start(bf16[1,2,448,128]{3,2,1,0:T(8,128)(2,1)S(1)} %get-tuple-element.56), channel_id=1, source_target_pairs={{0,4},{1,5},{2,6},{3,7},{4,0},{5,1},{6,2},{7,3},{8,12},{9,13},{10,... | collective-permute-start | bytes 688136 | tf_op jit(solution)/shard_map/ppermute | solution.py:248
  36.0 14.2 %collective-permute-start.10 = (bf16[1,2,448,128]{3,2,0,1:T(8,128)(2,1)S(1)}, bf16[1,2,448,128]{3,2,0,1:T(8,128)(2,1)S(1)}, u32[]{:S(2)}, u32[]{:S(2)}) collective-permute-start(bf16[1,2,448,128]{3,2,0,1:T(8,128)(2,1)S(1)} %bitcast.74), channel_id=1, source_target_pairs={{0,2},{1,3},{2,0},{3,1},{4,6},{5,7},{6,4},{7,5},{8,10},{9,11},{10,... | collective-permute-start | bytes 688136 | tf_op jit(solution)/shard_map/ppermute | solution.py:249
  39.6 10.6 %collective-permute-start.11 = (bf16[1,2,448,128]{3,2,0,1:T(8,128)(2,1)S(1)}, bf16[1,2,448,128]{3,2,0,1:T(8,128)(2,1)S(1)}, u32[]{:S(2)}, u32[]{:S(2)}) collective-permute-start(bf16[1,2,448,128]{3,2,0,1:T(8,128)(2,1)S(1)} %maximum_bitcast_fusion), channel_id=1, source_target_pairs={{2,4},{3,5},{4,2},{5,3},{10,12},{11,13},{12,10},{13,11},{18,20},{1... | collective-permute-start | bytes 688136 | tf_op jit(solution)/shard_map/ppermute | solution.py:250
  40.3 21.2 %copy-start.3 = (s32[4,32]{1,0:T(4,128)S(1)}, s32[4,32]{1,0:T(4,128)}, u32[]{:S(2)}) copy-start(s32[4,32]{1,0:T(4,128)} %param.7) | copy-start | bytes 1540
  50.2 9.1 %collective-permute-start.13 = (bf16[1,2,448,128]{3,2,1,0:T(8,128)(2,1)S(1)}, bf16[1,2,448,128]{3,2,1,0:T(8,128)(2,1)S(1)}, u32[]{:S(2)}, u32[]{:S(2)}) collective-permute-start(bf16[1,2,448,128]{3,2,1,0:T(8,128)(2,1)S(1)} %collective-permute-done.9.own), channel_id=1, source_target_pairs={{0,16},{8,24},{16,0},{24,8},{1,17},{9,25},{17,1},{25,9},{2,18},{10... | collective-permute-start | bytes 688136 | tf_op jit(solution)/shard_map/ppermute | solution.py:216
  51.8 9.1 %collective-permute-start.12 = (bf16[1,2,448,128]{3,2,1,0:T(8,128)(2,1)S(1)}, bf16[1,2,448,128]{3,2,1,0:T(8,128)(2,1)S(1)}, u32[]{:S(2)}, u32[]{:S(2)}) collective-permute-start(bf16[1,2,448,128]{3,2,1,0:T(8,128)(2,1)S(1)} %collective-permute-done.9.own), channel_id=1, source_target_pairs={{0,8},{8,0},{16,24},{24,16},{1,9},{9,1},{17,25},{25,17},{2,10},{10... | collective-permute-start | bytes 688136 | tf_op jit(solution)/shard_map/ppermute | solution.py:216
  52.3 25.2 %collective-permute-start.17 = (f16[128,3456]{1,0:T(8,128)(2,1)S(1)}, f16[128,3456]{1,0:T(8,128)(2,1)S(1)}, u32[]{:S(2)}, u32[]{:S(2)}) collective-permute-start(f16[128,3456]{1,0:T(8,128)(2,1)S(1)} %bitcast_convert_fusion.2), channel_id=1, source_target_pairs={{0,2},{1,3},{6,4},{7,5},{8,10},{9,11},{14,12},{15,13},{16,18},{17,... | collective-permute-start | bytes 2654216 | tf_op jit(solution)/shard_map/ppermute | solution.py:253
  59.3 4.9 %collective-permute-start.15 = (bf16[1,448,128]{2,1,0:T(8,128)(2,1)S(1)}, bf16[1,448,128]{2,1,0:T(8,128)(2,1)S(1)}, u32[]{:S(2)}, u32[]{:S(2)}) collective-permute-start(bf16[1,448,128]{2,1,0:T(8,128)(2,1)S(1)} %slice_bitcast_fusion.2), channel_id=1, source_target_pairs={{0,8},{8,0},{16,24},{24,16},{1,9},{9,1},{17,25},{25,17},{2,10},{10... | collective-permute-start | bytes 344072 | tf_op jit(solution)/shard_map/ppermute | solution.py:221
  60.9 4.9 %collective-permute-start.14 = (bf16[1,448,128]{2,1,0:T(8,128)(2,1)S(1)}, bf16[1,448,128]{2,1,0:T(8,128)(2,1)S(1)}, u32[]{:S(2)}, u32[]{:S(2)}) collective-permute-start(bf16[1,448,128]{2,1,0:T(8,128)(2,1)S(1)} %slice_bitcast_fusion.3), channel_id=1, source_target_pairs={{0,16},{8,24},{16,0},{24,8},{1,17},{9,25},{17,1},{25,9},{2,18},{10... | collective-permute-start | bytes 344072 | tf_op jit(solution)/shard_map/ppermute | solution.py:220
  70.6 0.7 copy-start.2
  70.7 8.9 %collective-permute-start.16 = (f16[1,128,3456]{2,1,0:T(8,128)(2,1)S(1)}, f16[1,128,3456]{2,1,0:T(8,128)(2,1)S(1)}, u32[]{:S(2)}, u32[]{:S(2)}) collective-permute-start(f16[1,128,3456]{2,1,0:T(8,128)(2,1)S(1)} %convert_element_type.96), channel_id=1, source_target_pairs={{0,1},{1,0},{2,3},{3,2},{4,5},{5,4},{6,7},{7,6},{8,9},{9,8},{10,11... | collective-permute-start | bytes 2654216 | tf_op jit(solution)/shard_map/ppermute | solution.py:225
  77.5 10.7 %collective-permute-start.19 = (bf16[2,2,448,128]{3,2,0,1:T(8,128)(2,1)S(1)}, bf16[2,2,448,128]{3,2,0,1:T(8,128)(2,1)S(1)}, u32[]{:S(2)}, u32[]{:S(2)}) collective-permute-start(bf16[2,2,448,128]{3,2,0,1:T(8,128)(2,1)S(1)} %pad_maximum_fusion.2), channel_id=1, source_target_pairs={{0,16},{8,24},{16,0},{24,8},{1,17},{9,25},{17,1},{25,9},{2,18},{10... | collective-permute-start | bytes 1376264 | tf_op jit(solution)/shard_map/ppermute | solution.py:216
  78.7 10.3 %collective-permute-start.18 = (bf16[2,2,448,128]{3,2,0,1:T(8,128)(2,1)S(1)}, bf16[2,2,448,128]{3,2,0,1:T(8,128)(2,1)S(1)}, u32[]{:S(2)}, u32[]{:S(2)}) collective-permute-start(bf16[2,2,448,128]{3,2,0,1:T(8,128)(2,1)S(1)} %pad_maximum_fusion.2), channel_id=1, source_target_pairs={{0,8},{8,0},{16,24},{24,16},{1,9},{9,1},{17,25},{25,17},{2,10},{10... | collective-permute-start | bytes 1376264 | tf_op jit(solution)/shard_map/ppermute | solution.py:216
  79.9 28.7 %collective-permute-start.23 = (f16[128,3456]{1,0:T(8,128)(2,1)S(1)}, f16[128,3456]{1,0:T(8,128)(2,1)S(1)}, u32[]{:S(2)}, u32[]{:S(2)}) collective-permute-start(f16[128,3456]{1,0:T(8,128)(2,1)S(1)} %bitcast_convert_fusion.1), channel_id=1, source_target_pairs={{0,2},{1,3},{6,4},{7,5},{8,10},{9,11},{14,12},{15,13},{16,18},{17,... | collective-permute-start | bytes 2654216 | tf_op jit(solution)/shard_map/ppermute | solution.py:259
  89.1 6.1 %collective-permute-start.20 = (bf16[2,448,128]{2,1,0:T(8,128)(2,1)S(1)}, bf16[2,448,128]{2,1,0:T(8,128)(2,1)S(1)}, u32[]{:S(2)}, u32[]{:S(2)}) collective-permute-start(bf16[2,448,128]{2,1,0:T(8,128)(2,1)S(1)} %slice_bitcast_fusion.1), channel_id=1, source_target_pairs={{0,16},{8,24},{16,0},{24,8},{1,17},{9,25},{17,1},{25,9},{2,18},{10... | collective-permute-start | bytes 688136 | tf_op jit(solution)/shard_map/ppermute | solution.py:220
  90.1 6.0 %collective-permute-start.21 = (bf16[2,448,128]{2,1,0:T(8,128)(2,1)S(1)}, bf16[2,448,128]{2,1,0:T(8,128)(2,1)S(1)}, u32[]{:S(2)}, u32[]{:S(2)}) collective-permute-start(bf16[2,448,128]{2,1,0:T(8,128)(2,1)S(1)} %slice_bitcast_fusion), channel_id=1, source_target_pairs={{0,8},{8,0},{16,24},{24,16},{1,9},{9,1},{17,25},{25,17},{2,10},{10... | collective-permute-start | bytes 688136 | tf_op jit(solution)/shard_map/ppermute | solution.py:221
  91.9 21.1 %collective-permute-start.26 = (f16[128,3456]{1,0:T(8,128)(2,1)S(1)}, f16[128,3456]{1,0:T(8,128)(2,1)S(1)}, u32[]{:S(2)}, u32[]{:S(2)}) collective-permute-start(f16[128,3456]{1,0:T(8,128)(2,1)S(1)} %fusion.21), channel_id=1, source_target_pairs={{2,4},{3,5},{4,2},{5,3},{10,12},{11,13},{12,10},{13,11},{18,20},{1... | collective-permute-start | bytes 2654216 | tf_op jit(solution)/shard_map/ppermute | solution.py:260
  104.6 3.8 %collective-permute-start.22 = (f16[2,128,3456]{2,1,0:T(8,128)(2,1)S(1)}, f16[2,128,3456]{2,1,0:T(8,128)(2,1)S(1)}, u32[]{:S(2)}, u32[]{:S(2)}) collective-permute-start(f16[2,128,3456]{2,1,0:T(8,128)(2,1)S(1)} %convert_element_type.103), channel_id=1, source_target_pairs={{0,1},{1,0},{2,3},{3,2},{4,5},{5,4},{6,7},{7,6},{8,9},{9,8},{10,11... | collective-permute-start | bytes 5308424 | tf_op jit(solution)/shard_map/ppermute | solution.py:225
  108.6 23.6 %collective-permute-start.24 = (f16[128,3456]{1,0:T(8,128)(2,1)S(1)}, f16[128,3456]{1,0:T(8,128)(2,1)S(1)}, u32[]{:S(2)}, u32[]{:S(2)}) collective-permute-start(f16[128,3456]{1,0:T(8,128)(2,1)S(1)} %bitcast_convert_fusion), channel_id=1, source_target_pairs={{0,2},{1,3},{6,4},{7,5},{8,10},{9,11},{14,12},{15,13},{16,18},{17,... | collective-permute-start | bytes 2654216 | tf_op jit(solution)/shard_map/ppermute | solution.py:268
  113.9 18.3 %collective-permute-start.25 = (f16[128,3456]{1,0:T(8,128)(2,1)S(1)}, f16[128,3456]{1,0:T(8,128)(2,1)S(1)}, u32[]{:S(2)}, u32[]{:S(2)}) collective-permute-start(f16[128,3456]{1,0:T(8,128)(2,1)S(1)} %get-tuple-element.87), channel_id=1, source_target_pairs={{2,4},{3,5},{4,2},{5,3},{10,12},{11,13},{12,10},{13,11},{18,20},{1... | collective-permute-start | bytes 2654216 | tf_op jit(solution)/shard_map/ppermute | solution.py:269
  114.6 23.3 %collective-permute-start.27 = (f16[128,3456]{1,0:T(8,128)(2,1)S(1)}, f16[128,3456]{1,0:T(8,128)(2,1)S(1)}, u32[]{:S(2)}, u32[]{:S(2)}) collective-permute-start(f16[128,3456]{1,0:T(8,128)(2,1)S(1)} %get-tuple-element.88), channel_id=1, source_target_pairs={{4,6},{5,7},{2,0},{3,1},{12,14},{13,15},{10,8},{11,9},{20,22},{21,... | collective-permute-start | bytes 2654216 | tf_op jit(solution)/shard_map/ppermute | solution.py:270

commit v4 on v3

--- a/solution.py
+++ b/solution.py
@@ -234,36 +234,36 @@
     both = [jnp.stack([keep[q], got[q]])[None] for q in range(4)]
 
     from_end = lax.ppermute(both[3], "cell", chips((0, 3), (3, 0)))
+    both1, both2, both3, from_end, matrix = lax.optimization_barrier((both[1], both[2], both[3], from_end, matrix))
     ga = gather_x_y(jnp.where(is_end, from_end, both[0]))
     slot_a = ga[0]
-    own_top = keep[0:1, keep.shape[1] - 1 :, 0:1].astype(F32)
-    edges = after(distribution, from_end) * (HALF_MAX / own_top)
-    from_below = lax.ppermute(edges[tile_len - 2 :].astype(F16), "cell", ring)
-    from_above = lax.ppermute(edges[:2].astype(F16), "cell", [(j, i) for i, j in ring])
-    ga = gather_diagonal(ga)
-    mine_a, theirs_a, scale_a = product(place, *ga, matrix, 4)
-    theirs_a, both1, both2, both3, from_below, from_above = lax.optimization_barrier(
-        (theirs_a, both[1], both[2], both[3], from_below, from_above)
-    )
     slot_b = lax.ppermute(both2, "cell", across(2))
     z1 = lax.ppermute(both1, "cell", across(1))
     from_middle = lax.ppermute(both3, "cell", middle)
+    ga = gather_diagonal(ga)
+    mine_a, theirs_a, scale_a = product(place, *ga, matrix, 4)
+    theirs_a, slot_b, z1, from_middle = lax.optimization_barrier((theirs_a, slot_b, z1, from_middle))
     (pa,) = exchanged(mine_a, theirs_a)
-    ma, slot_b, z1, from_middle = lax.optimization_barrier((pa.astype(F16), slot_b, z1, from_middle))
+    ma = pa.astype(F16)
     a0 = lax.ppermute(ma, "cell", ends)
-    gb = gather_x_y(slot_b)
-    gb = gather_diagonal(gb)
+    gb = gather_x_y(after(slot_b, ma))
+    gb = gather_diagonal(gb, ma)
     mine_b, theirs_b, _ = product(place, *gb, matrix, 4)
     (pb,) = exchanged(mine_b, theirs_b)
     mb = pb.astype(F16)
     a1 = lax.ppermute(after(mb, a0), "cell", ends)
     b1 = lax.ppermute((pb + a0.astype(F32)).astype(F16), "cell", middle)
-    z1, from_middle, both0, _ = lax.optimization_barrier((z1, from_middle, both[0], a0))
+    own_top = keep[0:1, keep.shape[1] - 1 :, 0:1].astype(F32)
+    edges = after(distribution, a0) * (HALF_MAX / own_top)
+    from_below = lax.ppermute(edges[tile_len - 2 :].astype(F16), "cell", ring)
+    from_above = lax.ppermute(edges[:2].astype(F16), "cell", [(j, i) for i, j in ring])
+    z1, from_middle, both0, _ = lax.optimization_barrier((z1, from_middle, both[0], gb[1]))
     slot_c = jnp.where(is_end, z1, from_middle)
     slot_d = jnp.where(is_end, both0, z1)
     gcd = gather_x_y(jnp.concatenate([slot_c, slot_d]))
     gcd = gather_diagonal(gcd, mb)
     mine_cd, theirs_cd, scale_cd = product(place, *behind(gcd, mb), matrix, 4)
+    theirs_cd, from_below, from_above = lax.optimization_barrier((theirs_cd, from_below, from_above))
     pc, pd = exchanged(mine_cd, theirs_cd)
     a2 = lax.ppermute(after(pc.astype(F16), a1), "cell", ends)
     b2 = lax.ppermute((pc + a1.astype(F32)).astype(F16), "cell", middle)

time: 140 us -> 130 us (0.929)
  waiting for transfers between devices: 53.2 us -> 45.1 us
  starting transfers between devices: 47.5 us -> 45.9 us
    ppermute x1, waiting for transfers between devices: 9.71 us -> 2.95 us  [chain_body(): slot_b = lax.ppermute(both2, 'cell', across(2))]
    ppermute x3, waiting for transfers between devices: 5.32 us -> 0.01 us  [gather_diagonal(): dy = lax.ppermute(after(gy[:, 1], *earlier), 'vel', in_x)]
    ppermute x3, waiting for transfers between devices: 4.43 us -> 0.74 us  [gather_diagonal(): dx = lax.ppermute(after(gx[:, 0], *earlier), 'vel', in_y)]
    ppermute x1, waiting for transfers between devices: 0.01 us -> 3.5 us  [chain_body(): a1 = lax.ppermute(after(mb, a0), 'cell', ends)]
    ppermute x1, waiting for transfers between devices: 5.58 us -> 2.39 us  [chain_body(): a0 = lax.ppermute(ma, 'cell', ends)]
    ppermute x3, waiting for transfers between devices: 2.23 us -> 4.31 us  [exchanged(): theirs = lax.ppermute(theirs.astype(F16), 'cell', other_core)]
    ppermute x1, starting transfers between devices: 1.94 us -> 0.06 us  [chain_body(): lax.ppermute(edges[:2].astype(F16), 'cell', [(j, i) for i, j in ring])]
    ppermute x1, waiting for transfers between devices: 11.9 us -> 13.6 us  [chain_body(): a2 = lax.ppermute(after(pc.astype(F16), a1), 'cell', ends)]
  transfers between devices with their start and end apart: 28 -> 28, of which waited for: 16 -> 13; matrix products, arithmetic and copies ran while one was open for 6% -> 7% of each run, Pallas kernels for 16% -> 17%
where the time goes in v4:
time: 130 us; the launch traced here: 129 us
  starting transfers between devices  45.9 us (35%)
  waiting for transfers between devices  45.1 us (35%)
  Pallas kernels  23.6 us (18%)
  other arithmetic  8.45 us (6%)
  local copies, waits for them, and re-layouts  3.87 us (3%)
  between operations  2.34 us (2%)
    pallas_call x3, Pallas kernels, product(): pl.pallas_call(functools.partial(product_kernel, piece=piece, bound=HALF_...  17.6 us
    ppermute x1, waiting for transfers between devices, chain_body(): a2 = lax.ppermute(after(pc.astype(F16), a1), 'cell', ends)  13.6 us
    ppermute x6, waiting for transfers between devices, gather_x_y(): return (own, lax.ppermute(own, 'vel', in_x), lax.ppermute(own, 'vel', in_y))  8.29 us
    ppermute x1, starting transfers between devices, chain_body(): from_end = lax.ppermute(both[3], 'cell', chips((0, 3), (3, 0)))  6.88 us
    ppermute x6, starting transfers between devices, gather_x_y(): return (own, lax.ppermute(own, 'vel', in_x), lax.ppermute(own, 'vel', in_y))  6.6 us
    ppermute x1, waiting for transfers between devices, chain_body(): c2 = lax.ppermute((pd + b1.astype(F32)).astype(F16), 'cell', outward)  6.55 us
    ppermute x1, starting transfers between devices, chain_body(): a0 = lax.ppermute(ma, 'cell', ends)  6.51 us
    ppermute x1, starting transfers between devices, chain_body(): a1 = lax.ppermute(after(mb, a0), 'cell', ends)  4.43 us
  transfers between devices with their start and end apart: 28, of which 13 were waited for; matrix products, arithmetic and copies ran while one was open for 7% of the time, Pallas kernels for 17%

profile of v4, /device:TPU:0, one launch (start us, length us, event | category | flops | bytes accessed | tf_op | source)
XLA Modules:
  0.0 129.3 jit_solution(14259399528310338329)
XLA Ops:
  0.0 0.1 pad_add_fusion.place
  0.1 1.5 %copy-done = f32[4,32,3456]{2,1,0:T(8,128)S(1)} copy-done((f32[4,32,3456]{2,1,0:T(8,128)S(1)}, f32[4,32,3456]{2,1,0:T(8,128)}, u32[]{:S(2)}) %copy-start) | copy-done | bytes 1769496
  1.6 1.1 pieces.1
  2.6 0.5 collective-permute-start
  3.2 1.4 %collective-permute-done = bf16[4,448,128]{2,1,0:T(8,128)(2,1)S(1)} collective-permute-done((bf16[4,448,128]{2,1,0:T(8,128)(2,1)S(1)}, bf16[4,448,128]{2,1,0:T(8,128)(2,1)S(1)}, u32[]{:S(2)}, u32[]{:S(2)}) %collective-permute-start) | collective-permute-done | bytes 458784 | tf_op jit(solution)/shard_map/ppermute | solution.py:232
  4.7 6.9 %collective-permute-start.1 = (bf16[1,2,448,128]{3,2,1,0:T(8,128)(2,1)S(1)}, bf16[1,2,448,128]{3,2,1,0:T(8,128)(2,1)S(1)}, u32[]{:S(2)}, u32[]{:S(2)}) collective-permute-start(bf16[1,2,448,128]{3,2,1,0:T(8,128)(2,1)S(1)} %maximum_bitcast_fusion.2), channel_id=1, source_target_pairs={{0,6},{1,7},{6,0},{7,1},{8,14},{9,15},{14,8},{15,9},{16,22},{17,23... | collective-permute-start | bytes 688136 | tf_op jit(solution)/shard_map/ppermute | solution.py:236
  11.5 4.4 %load.1.c_ref = bf16[1728,3456]{1,0:T(8,128)(2,1)S(1)} custom-call(bf16[1728,3456]{1,0:T(8,128)(2,1)} %bitcast.57), custom_call_target="tpu_custom_call" | custom-call | flops 1 | bytes 23887872 | tf_op jit(solution)/shard_map/load/pallas_call | solution.py:150
  16.0 1.4 %collective-permute-done.1 = bf16[1,2,448,128]{3,2,1,0:T(8,128)(2,1)S(1)} collective-permute-done((bf16[1,2,448,128]{3,2,1,0:T(8,128)(2,1)S(1)}, bf16[1,2,448,128]{3,2,1,0:T(8,128)(2,1)S(1)}, u32[]{:S(2)}, u32[]{:S(2)}) %collective-permute-start.1) | collective-permute-done | bytes 229408 | tf_op jit(solution)/shard_map/ppermute | solution.py:236
  17.5 1.6 %collective-permute-start.3 = (bf16[1,2,448,128]{3,2,1,0:T(8,128)(2,1)S(1)}, bf16[1,2,448,128]{3,2,1,0:T(8,128)(2,1)S(1)}, u32[]{:S(2)}, u32[]{:S(2)}) collective-permute-start(bf16[1,2,448,128]{3,2,1,0:T(8,128)(2,1)S(1)} %broadcast_select_fusion.2.own.a_ref), channel_id=1, source_target_pairs={{0,16},{8,24},{16,0},{24,8},{1,17},{9,25},{17,1},{25,9},{2,18},{10... | collective-permute-start | bytes 688136 | tf_op jit(solution)/shard_map/ppermute | solution.py:216
  19.1 1.5 %collective-permute-start.2 = (bf16[1,2,448,128]{3,2,1,0:T(8,128)(2,1)S(1)}, bf16[1,2,448,128]{3,2,1,0:T(8,128)(2,1)S(1)}, u32[]{:S(2)}, u32[]{:S(2)}) collective-permute-start(bf16[1,2,448,128]{3,2,1,0:T(8,128)(2,1)S(1)} %broadcast_select_fusion.2.own.a_ref), channel_id=1, source_target_pairs={{0,8},{8,0},{16,24},{24,16},{1,9},{9,1},{17,25},{25,17},{2,10},{10... | collective-permute-start | bytes 688136 | tf_op jit(solution)/shard_map/ppermute | solution.py:216
  20.5 4.1 %collective-permute-done.3.gy = bf16[1,2,448,128]{3,2,1,0:T(8,128)(2,1)S(1)} collective-permute-done((bf16[1,2,448,128]{3,2,1,0:T(8,128)(2,1)S(1)}, bf16[1,2,448,128]{3,2,1,0:T(8,128)(2,1)S(1)}, u32[]{:S(2)}, u32[]{:S(2)}) %collective-permute-start.3) | collective-permute-done | bytes 229408 | tf_op jit(solution)/shard_map/ppermute | solution.py:216
  24.7 1.3 %collective-permute-start.5 = (bf16[1,448,128]{2,1,0:T(8,128)(2,1)S(1)}, bf16[1,448,128]{2,1,0:T(8,128)(2,1)S(1)}, u32[]{:S(2)}, u32[]{:S(2)}) collective-permute-start(bf16[1,448,128]{2,1,0:T(8,128)(2,1)S(1)} %slice_bitcast_fusion.4), channel_id=1, source_target_pairs={{0,8},{8,0},{16,24},{24,16},{1,9},{9,1},{17,25},{25,17},{2,10},{10... | collective-permute-start | bytes 344072 | tf_op jit(solution)/shard_map/ppermute | solution.py:221
  26.0 1.6 %collective-permute-start.4 = (bf16[1,448,128]{2,1,0:T(8,128)(2,1)S(1)}, bf16[1,448,128]{2,1,0:T(8,128)(2,1)S(1)}, u32[]{:S(2)}, u32[]{:S(2)}) collective-permute-start(bf16[1,448,128]{2,1,0:T(8,128)(2,1)S(1)} %slice_bitcast_fusion.5), channel_id=1, source_target_pairs={{0,16},{8,24},{16,0},{24,8},{1,17},{9,25},{17,1},{25,9},{2,18},{10... | collective-permute-start | bytes 344072 | tf_op jit(solution)/shard_map/ppermute | solution.py:220
  27.6 4.0 %collective-permute-start.7 = (bf16[1,2,448,128]{3,2,1,0:T(8,128)(2,1)S(1)}, bf16[1,2,448,128]{3,2,1,0:T(8,128)(2,1)S(1)}, u32[]{:S(2)}, u32[]{:S(2)}) collective-permute-start(bf16[1,2,448,128]{3,2,1,0:T(8,128)(2,1)S(1)} %get-tuple-element.61), channel_id=1, source_target_pairs={{0,2},{1,3},{2,0},{3,1},{4,6},{5,7},{6,4},{7,5},{8,10},{9,11},{10,... | collective-permute-start | bytes 688136 | tf_op jit(solution)/shard_map/ppermute | solution.py:241
  31.6 0.7 collective-permute-start.8
  32.3 4.4 %product.3 = (f32[1,128,3456]{2,1,0:T(8,128)S(1)}, f32[1,128,3456]{2,1,0:T(8,128)S(1)}, f32[1,2,8,128]{3,2,1,0:T(8,128)S(1)}) custom-call(s32[3]{0:T(128)S(1)} %pad_add_fusion.place, bf16[1,2,448,128]{3,2,1,0:T(8,128)(2,1)S(1)} %broadcast_select_fusion.2.own.a_ref, bf16[1,2,448,128]{3,2,1,0:T(8,128)(2,1)S(1)} %collective-permute-done.2.gx, ...), custom_call_target="tpu_custom_call" | custom-call | flops 3057647616 | bytes 15482880 | tf_op jit(solution)/shard_map/product/pallas_call | solution.py:127
  36.8 3.0 %collective-permute-done.6.own = bf16[1,2,448,128]{3,2,1,0:T(8,128)(2,1)S(1)} collective-permute-done((bf16[1,2,448,128]{3,2,1,0:T(8,128)(2,1)S(1)}, bf16[1,2,448,128]{3,2,1,0:T(8,128)(2,1)S(1)}, u32[]{:S(2)}, u32[]{:S(2)}) %collective-permute-start.6) | collective-permute-done | bytes 229408 | tf_op jit(solution)/shard_map/ppermute | solution.py:240
  39.7 0.1 convert_element_type.92
  39.9 2.4 %collective-permute-done.9 = f16[1,128,3456]{2,1,0:T(8,128)(2,1)S(1)} collective-permute-done((f16[1,128,3456]{2,1,0:T(8,128)(2,1)S(1)}, f16[1,128,3456]{2,1,0:T(8,128)(2,1)S(1)}, u32[]{:S(2)}, u32[]{:S(2)}) %collective-permute-start.9) | collective-permute-done | bytes 884768 | tf_op jit(solution)/shard_map/ppermute | solution.py:225
  42.3 0.2 bitcast_convert_fusion.2
  42.5 0.6 collective-permute-start.11
  43.1 1.2 collective-permute-start.10
  44.4 6.5 %collective-permute-start.19 = (f16[128,3456]{1,0:T(8,128)(2,1)S(1)}, f16[128,3456]{1,0:T(8,128)(2,1)S(1)}, u32[]{:S(2)}, u32[]{:S(2)}) collective-permute-start(f16[128,3456]{1,0:T(8,128)(2,1)S(1)} %bitcast_convert_fusion.2), channel_id=1, source_target_pairs={{0,2},{1,3},{6,4},{7,5},{8,10},{9,11},{14,12},{15,13},{16,18},{17,... | collective-permute-start | bytes 2654216 | tf_op jit(solution)/shard_map/ppermute | solution.py:248
  50.9 0.9 collective-permute-start.13
  51.9 1.6 %collective-permute-start.12 = (bf16[1,448,128]{2,1,0:T(8,128)(2,1)S(1)}, bf16[1,448,128]{2,1,0:T(8,128)(2,1)S(1)}, u32[]{:S(2)}, u32[]{:S(2)}) collective-permute-start(bf16[1,448,128]{2,1,0:T(8,128)(2,1)S(1)} %slice_bitcast_fusion.3), channel_id=1, source_target_pairs={{0,16},{8,24},{16,0},{24,8},{1,17},{9,25},{17,1},{25,9},{2,18},{10... | collective-permute-start | bytes 344072 | tf_op jit(solution)/shard_map/ppermute | solution.py:220
  53.5 0.6 collective-permute-start.16
  54.1 0.5 slice.119
  55.4 0.6 slice.133
  56.0 1.2 collective-permute-start.15
  57.1 0.7 collective-permute-done.12.dx
  57.9 4.8 %product.4 = (f32[1,128,3456]{2,1,0:T(8,128)S(1)}, f32[1,128,3456]{2,1,0:T(8,128)S(1)}, f32[1,2,8,128]{3,2,1,0:T(8,128)}) custom-call(s32[3]{0:T(128)S(1)} %pad_add_fusion.place, bf16[1,2,448,128]{3,2,1,0:T(8,128)(2,1)S(1)} %collective-permute-done.6.own, bf16[1,2,448,128]{3,2,1,0:T(8,128)(2,1)S(1)} %collective-permute-done.10.gx, ...), custom_call_target="tpu_custom_call" | custom-call | flops 3057647616 | bytes 15482880 | tf_op jit(solution)/shard_map/product/pallas_call | solution.py:127
  62.7 0.1 convert_element_type.95
  62.9 3.1 %collective-permute-done.16.gy = bf16[2,2,448,128]{3,2,1,0:T(8,128)(2,1)S(1)} collective-permute-done((bf16[2,2,448,128]{3,2,1,0:T(8,128)(2,1)S(1)}, bf16[2,2,448,128]{3,2,1,0:T(8,128)(2,1)S(1)}, u32[]{:S(2)}, u32[]{:S(2)}) %collective-permute-start.16) | collective-permute-done | bytes 458784 | tf_op jit(solution)/shard_map/ppermute | solution.py:216
  66.0 1.0 collective-permute-done.15.gx
  67.1 2.4 %collective-permute-done.19 = f16[128,3456]{1,0:T(8,128)(2,1)S(1)} collective-permute-done((f16[128,3456]{1,0:T(8,128)(2,1)S(1)}, f16[128,3456]{1,0:T(8,128)(2,1)S(1)}, u32[]{:S(2)}, u32[]{:S(2)}) %collective-permute-start.19) | collective-permute-done | bytes 884768 | tf_op jit(solution)/shard_map/ppermute | solution.py:248
  69.5 0.1 multiply_convert_fusion
  69.6 0.1 fusion.32
  69.8 0.5 collective-permute-start.20
  70.3 0.2 bitcast_convert_fusion.1
  70.5 1.0 collective-permute-start.17
  71.5 1.5 %collective-permute-start.18 = (bf16[2,448,128]{2,1,0:T(8,128)(2,1)S(1)}, bf16[2,448,128]{2,1,0:T(8,128)(2,1)S(1)}, u32[]{:S(2)}, u32[]{:S(2)}) collective-permute-start(bf16[2,448,128]{2,1,0:T(8,128)(2,1)S(1)} %slice_bitcast_fusion), channel_id=1, source_target_pairs={{0,8},{8,0},{16,24},{24,16},{1,9},{9,1},{17,25},{25,17},{2,10},{10... | collective-permute-start | bytes 688136 | tf_op jit(solution)/shard_map/ppermute | solution.py:221
  73.0 4.4 %collective-permute-start.23 = (f16[128,3456]{1,0:T(8,128)(2,1)S(1)}, f16[128,3456]{1,0:T(8,128)(2,1)S(1)}, u32[]{:S(2)}, u32[]{:S(2)}) collective-permute-start(f16[128,3456]{1,0:T(8,128)(2,1)S(1)} %bitcast_convert_fusion.1), channel_id=1, source_target_pairs={{0,2},{1,3},{6,4},{7,5},{8,10},{9,11},{14,12},{15,13},{16,18},{17,... | collective-permute-start | bytes 2654216 | tf_op jit(solution)/shard_map/ppermute | solution.py:254
  77.4 0.3 fusion.21
  77.8 0.6 edges.1
  78.3 0.5 fusion.35
  78.9 0.7 collective-permute-start.26
  79.6 8.3 %product.5 = (f32[2,128,3456]{2,1,0:T(8,128)S(1)}, f32[2,128,3456]{2,1,0:T(8,128)S(1)}, f32[2,2,8,128]{3,2,1,0:T(8,128)S(1)}) custom-call(s32[3]{0:T(128)S(1)} %pad_add_fusion.place, bf16[2,2,448,128]{3,2,1,0:T(8,128)(2,1)S(1)} %pad_maximum_fusion.2.own, bf16[2,2,448,128]{3,2,1,0:T(8,128)(2,1)S(1)} %collective-permute-done.15.gx, ...), custom_call_target="tpu_custom_call" | custom-call | flops 6115295232 | bytes 19021824 | tf_op jit(solution)/shard_map/product/pallas_call | solution.py:127
  87.9 0.5 slice.132
  89.7 0.2 convert_element_type.103
  89.9 0.6 collective-permute-start.22
  90.4 0.7 convert_multiply_fusion.1
  91.1 0.7 convert_multiply_fusion
  91.8 1.9 %collective-permute-done.22 = f16[2,128,3456]{2,1,0:T(8,128)(2,1)S(1)} collective-permute-done((f16[2,128,3456]{2,1,0:T(8,128)(2,1)S(1)}, f16[2,128,3456]{2,1,0:T(8,128)(2,1)S(1)}, u32[]{:S(2)}, u32[]{:S(2)}) %collective-permute-start.22) | collective-permute-done | bytes 1769504 | tf_op jit(solution)/shard_map/ppermute | solution.py:225
  93.8 0.2 bitcast_convert_fusion
  94.0 3.5 %collective-permute-done.23 = f16[128,3456]{1,0:T(8,128)(2,1)S(1)} collective-permute-done((f16[128,3456]{1,0:T(8,128)(2,1)S(1)}, f16[128,3456]{1,0:T(8,128)(2,1)S(1)}, u32[]{:S(2)}, u32[]{:S(2)}) %collective-permute-start.23) | collective-permute-done | bytes 884768 | tf_op jit(solution)/shard_map/ppermute | solution.py:254
  97.5 4.4 %collective-permute-start.24 = (f16[128,3456]{1,0:T(8,128)(2,1)S(1)}, f16[128,3456]{1,0:T(8,128)(2,1)S(1)}, u32[]{:S(2)}, u32[]{:S(2)}) collective-permute-start(f16[128,3456]{1,0:T(8,128)(2,1)S(1)} %bitcast_convert_fusion), channel_id=1, source_target_pairs={{0,2},{1,3},{6,4},{7,5},{8,10},{9,11},{14,12},{15,13},{16,18},{17,... | collective-permute-start | bytes 2654216 | tf_op jit(solution)/shard_map/ppermute | solution.py:268
  101.9 0.8 fusion.19
  102.7 0.7 collective-permute-start.25
  103.5 1.3 collective-permute-start.27
  104.8 2.5 %fusion.6 = f32[4,32,3456]{2,1,0:T(8,128)S(1)} fusion(f32[4,32,3456]{2,1,0:T(8,128)S(1)} %copy-done.1, f32[2,32,3456]{2,1,0:T(8,128)S(1)} %convert_multiply_fusion, f32[2,32,3456]{2,1,0:T(8,128)S(1)} %convert_multiply_fusion.1, f32[3456]{0:T(1024)S(1)} %get-tuple-element.115, f32[3456]{0:T(1024)S(1)} %get-tuple-element.114, ...), kind=kLoop, calls=%fused_computation.14 | loop fusion | flops 9732096 | bytes 5343488 | tf_op jit(solution)/shard_map/mul | solution.py:57
  107.3 13.6 %collective-permute-done.24 = f16[128,3456]{1,0:T(8,128)(2,1)S(1)} collective-permute-done((f16[128,3456]{1,0:T(8,128)(2,1)S(1)}, f16[128,3456]{1,0:T(8,128)(2,1)S(1)}, u32[]{:S(2)}, u32[]{:S(2)}) %collective-permute-start.24) | collective-permute-done | bytes 884768 | tf_op jit(solution)/shard_map/ppermute | solution.py:268
  120.8 6.5 %collective-permute-done.27 = f16[128,3456]{1,0:T(8,128)(2,1)S(1)} collective-permute-done((f16[128,3456]{1,0:T(8,128)(2,1)S(1)}, f16[128,3456]{1,0:T(8,128)(2,1)S(1)}, u32[]{:S(2)}, u32[]{:S(2)}) %collective-permute-start.27) | collective-permute-done | bytes 884768 | tf_op jit(solution)/shard_map/ppermute | solution.py:270
  127.4 0.4 add_add_fusion
  127.8 1.5 %multiply_add_fusion = f32[4,32,3456]{2,1,0:T(8,128)} fusion(f32[4,32,3456]{2,1,0:T(8,128)S(1)} %fusion.6, f32[4,32,3456]{2,1,0:T(8,128)S(1)} %bitcast.58, f32[4,32]{1,0:T(4,128)S(1)} %bitcast.59), kind=kLoop, calls=%fused_computation.39 | loop fusion | flops 884736 | bytes 5308928 | tf_op jit(solution)/shard_map/add | solution.py:281
  (45 shorter events, 0.7 us)
Async XLA Ops:
  0.1 1.5 %copy-start = (f32[4,32,3456]{2,1,0:T(8,128)S(1)}, f32[4,32,3456]{2,1,0:T(8,128)}, u32[]{:S(2)}) copy-start(f32[4,32,3456]{2,1,0:T(8,128)} %param.4) | copy-start | bytes 5308420
  2.6 2.0 %collective-permute-start = (bf16[4,448,128]{2,1,0:T(8,128)(2,1)S(1)}, bf16[4,448,128]{2,1,0:T(8,128)(2,1)S(1)}, u32[]{:S(2)}, u32[]{:S(2)}) collective-permute-start(bf16[4,448,128]{2,1,0:T(8,128)(2,1)S(1)} %get-tuple-element.55), channel_id=1, source_target_pairs={{0,1},{1,0},{2,3},{3,2},{4,5},{5,4},{6,7},{7,6},{8,9},{9,8},{10,11... | collective-permute-start | bytes 1376264 | tf_op jit(solution)/shard_map/ppermute | solution.py:232
  4.7 12.8 %collective-permute-start.1 = (bf16[1,2,448,128]{3,2,1,0:T(8,128)(2,1)S(1)}, bf16[1,2,448,128]{3,2,1,0:T(8,128)(2,1)S(1)}, u32[]{:S(2)}, u32[]{:S(2)}) collective-permute-start(bf16[1,2,448,128]{3,2,1,0:T(8,128)(2,1)S(1)} %maximum_bitcast_fusion.2), channel_id=1, source_target_pairs={{0,6},{1,7},{6,0},{7,1},{8,14},{9,15},{14,8},{15,9},{16,22},{17,23... | collective-permute-start | bytes 688136 | tf_op jit(solution)/shard_map/ppermute | solution.py:236
  17.5 7.2 %collective-permute-start.3 = (bf16[1,2,448,128]{3,2,1,0:T(8,128)(2,1)S(1)}, bf16[1,2,448,128]{3,2,1,0:T(8,128)(2,1)S(1)}, u32[]{:S(2)}, u32[]{:S(2)}) collective-permute-start(bf16[1,2,448,128]{3,2,1,0:T(8,128)(2,1)S(1)} %broadcast_select_fusion.2.own.a_ref), channel_id=1, source_target_pairs={{0,16},{8,24},{16,0},{24,8},{1,17},{9,25},{17,1},{25,9},{2,18},{10... | collective-permute-start | bytes 688136 | tf_op jit(solution)/shard_map/ppermute | solution.py:216
  19.1 6.9 %collective-permute-start.2 = (bf16[1,2,448,128]{3,2,1,0:T(8,128)(2,1)S(1)}, bf16[1,2,448,128]{3,2,1,0:T(8,128)(2,1)S(1)}, u32[]{:S(2)}, u32[]{:S(2)}) collective-permute-start(bf16[1,2,448,128]{3,2,1,0:T(8,128)(2,1)S(1)} %broadcast_select_fusion.2.own.a_ref), channel_id=1, source_target_pairs={{0,8},{8,0},{16,24},{24,16},{1,9},{9,1},{17,25},{25,17},{2,10},{10... | collective-permute-start | bytes 688136 | tf_op jit(solution)/shard_map/ppermute | solution.py:216
  24.7 7.6 %collective-permute-start.5 = (bf16[1,448,128]{2,1,0:T(8,128)(2,1)S(1)}, bf16[1,448,128]{2,1,0:T(8,128)(2,1)S(1)}, u32[]{:S(2)}, u32[]{:S(2)}) collective-permute-start(bf16[1,448,128]{2,1,0:T(8,128)(2,1)S(1)} %slice_bitcast_fusion.4), channel_id=1, source_target_pairs={{0,8},{8,0},{16,24},{24,16},{1,9},{9,1},{17,25},{25,17},{2,10},{10... | collective-permute-start | bytes 344072 | tf_op jit(solution)/shard_map/ppermute | solution.py:221
  26.0 6.3 %collective-permute-start.4 = (bf16[1,448,128]{2,1,0:T(8,128)(2,1)S(1)}, bf16[1,448,128]{2,1,0:T(8,128)(2,1)S(1)}, u32[]{:S(2)}, u32[]{:S(2)}) collective-permute-start(bf16[1,448,128]{2,1,0:T(8,128)(2,1)S(1)} %slice_bitcast_fusion.5), channel_id=1, source_target_pairs={{0,16},{8,24},{16,0},{24,8},{1,17},{9,25},{17,1},{25,9},{2,18},{10... | collective-permute-start | bytes 344072 | tf_op jit(solution)/shard_map/ppermute | solution.py:220
  27.6 12.1 %collective-permute-start.6 = (bf16[1,2,448,128]{3,2,1,0:T(8,128)(2,1)S(1)}, bf16[1,2,448,128]{3,2,1,0:T(8,128)(2,1)S(1)}, u32[]{:S(2)}, u32[]{:S(2)}) collective-permute-start(bf16[1,2,448,128]{3,2,1,0:T(8,128)(2,1)S(1)} %get-tuple-element.60), channel_id=1, source_target_pairs={{0,4},{1,5},{2,6},{3,7},{4,0},{5,1},{6,2},{7,3},{8,12},{9,13},{10,... | collective-permute-start | bytes 688136 | tf_op jit(solution)/shard_map/ppermute | solution.py:240
  27.6 12.1 %collective-permute-start.7 = (bf16[1,2,448,128]{3,2,1,0:T(8,128)(2,1)S(1)}, bf16[1,2,448,128]{3,2,1,0:T(8,128)(2,1)S(1)}, u32[]{:S(2)}, u32[]{:S(2)}) collective-permute-start(bf16[1,2,448,128]{3,2,1,0:T(8,128)(2,1)S(1)} %get-tuple-element.61), channel_id=1, source_target_pairs={{0,2},{1,3},{2,0},{3,1},{4,6},{5,7},{6,4},{7,5},{8,10},{9,11},{10,... | collective-permute-start | bytes 688136 | tf_op jit(solution)/shard_map/ppermute | solution.py:241
  31.6 8.1 %collective-permute-start.8 = (bf16[1,2,448,128]{3,2,1,0:T(8,128)(2,1)S(1)}, bf16[1,2,448,128]{3,2,1,0:T(8,128)(2,1)S(1)}, u32[]{:S(2)}, u32[]{:S(2)}) collective-permute-start(bf16[1,2,448,128]{3,2,1,0:T(8,128)(2,1)S(1)} %maximum_bitcast_fusion.2), channel_id=1, source_target_pairs={{2,4},{3,5},{4,2},{5,3},{10,12},{11,13},{12,10},{13,11},{18,20},{1... | collective-permute-start | bytes 688136 | tf_op jit(solution)/shard_map/ppermute | solution.py:242
  36.8 3.1 %copy-start.2 = (s32[3456]{0:T(1024)S(1)}, s32[3456]{0:T(1024)}, u32[]{:S(2)}) copy-start(s32[3456]{0:T(1024)} %param.6) | copy-start | bytes 41476
  39.8 2.5 %collective-permute-start.9 = (f16[1,128,3456]{2,1,0:T(8,128)(2,1)S(1)}, f16[1,128,3456]{2,1,0:T(8,128)(2,1)S(1)}, u32[]{:S(2)}, u32[]{:S(2)}) collective-permute-start(f16[1,128,3456]{2,1,0:T(8,128)(2,1)S(1)} %convert_element_type.92), channel_id=1, source_target_pairs={{0,1},{1,0},{2,3},{3,2},{4,5},{5,4},{6,7},{7,6},{8,9},{9,8},{10,11... | collective-permute-start | bytes 2654216 | tf_op jit(solution)/shard_map/ppermute | solution.py:225
  42.3 0.8 copy-start.3
  42.5 8.3 %collective-permute-start.11 = (bf16[1,2,448,128]{3,2,1,0:T(8,128)(2,1)S(1)}, bf16[1,2,448,128]{3,2,1,0:T(8,128)(2,1)S(1)}, u32[]{:S(2)}, u32[]{:S(2)}) collective-permute-start(bf16[1,2,448,128]{3,2,1,0:T(8,128)(2,1)S(1)} %collective-permute-done.6.own), channel_id=1, source_target_pairs={{0,16},{8,24},{16,0},{24,8},{1,17},{9,25},{17,1},{25,9},{2,18},{10... | collective-permute-start | bytes 688136 | tf_op jit(solution)/shard_map/ppermute | solution.py:216
  43.1 8.7 %collective-permute-start.10 = (bf16[1,2,448,128]{3,2,1,0:T(8,128)(2,1)S(1)}, bf16[1,2,448,128]{3,2,1,0:T(8,128)(2,1)S(1)}, u32[]{:S(2)}, u32[]{:S(2)}) collective-permute-start(bf16[1,2,448,128]{3,2,1,0:T(8,128)(2,1)S(1)} %collective-permute-done.6.own), channel_id=1, source_target_pairs={{0,8},{8,0},{16,24},{24,16},{1,9},{9,1},{17,25},{25,17},{2,10},{10... | collective-permute-start | bytes 688136 | tf_op jit(solution)/shard_map/ppermute | solution.py:216
  44.4 25.1 %collective-permute-start.19 = (f16[128,3456]{1,0:T(8,128)(2,1)S(1)}, f16[128,3456]{1,0:T(8,128)(2,1)S(1)}, u32[]{:S(2)}, u32[]{:S(2)}) collective-permute-start(f16[128,3456]{1,0:T(8,128)(2,1)S(1)} %bitcast_convert_fusion.2), channel_id=1, source_target_pairs={{0,2},{1,3},{6,4},{7,5},{8,10},{9,11},{14,12},{15,13},{16,18},{17,... | collective-permute-start | bytes 2654216 | tf_op jit(solution)/shard_map/ppermute | solution.py:248
  50.9 6.2 %collective-permute-start.13 = (bf16[1,448,128]{2,1,0:T(8,128)(2,1)S(1)}, bf16[1,448,128]{2,1,0:T(8,128)(2,1)S(1)}, u32[]{:S(2)}, u32[]{:S(2)}) collective-permute-start(bf16[1,448,128]{2,1,0:T(8,128)(2,1)S(1)} %slice_bitcast_fusion.2), channel_id=1, source_target_pairs={{0,8},{8,0},{16,24},{24,16},{1,9},{9,1},{17,25},{25,17},{2,10},{10... | collective-permute-start | bytes 344072 | tf_op jit(solution)/shard_map/ppermute | solution.py:221
  51.9 6.0 %collective-permute-start.12 = (bf16[1,448,128]{2,1,0:T(8,128)(2,1)S(1)}, bf16[1,448,128]{2,1,0:T(8,128)(2,1)S(1)}, u32[]{:S(2)}, u32[]{:S(2)}) collective-permute-start(bf16[1,448,128]{2,1,0:T(8,128)(2,1)S(1)} %slice_bitcast_fusion.3), channel_id=1, source_target_pairs={{0,16},{8,24},{16,0},{24,8},{1,17},{9,25},{17,1},{25,9},{2,18},{10... | collective-permute-start | bytes 344072 | tf_op jit(solution)/shard_map/ppermute | solution.py:220
  53.5 12.5 %collective-permute-start.16 = (bf16[2,2,448,128]{3,2,1,0:T(8,128)(2,1)S(1)}, bf16[2,2,448,128]{3,2,1,0:T(8,128)(2,1)S(1)}, u32[]{:S(2)}, u32[]{:S(2)}) collective-permute-start(bf16[2,2,448,128]{3,2,1,0:T(8,128)(2,1)S(1)} %pad_maximum_fusion.2.own), channel_id=1, source_target_pairs={{0,16},{8,24},{16,0},{24,8},{1,17},{9,25},{17,1},{25,9},{2,18},{10... | collective-permute-start | bytes 1376264 | tf_op jit(solution)/shard_map/ppermute | solution.py:216
  56.0 11.1 %collective-permute-start.15 = (bf16[2,2,448,128]{3,2,1,0:T(8,128)(2,1)S(1)}, bf16[2,2,448,128]{3,2,1,0:T(8,128)(2,1)S(1)}, u32[]{:S(2)}, u32[]{:S(2)}) collective-permute-start(bf16[2,2,448,128]{3,2,1,0:T(8,128)(2,1)S(1)} %pad_maximum_fusion.2.own), channel_id=1, source_target_pairs={{0,8},{8,0},{16,24},{24,16},{1,9},{9,1},{17,25},{25,17},{2,10},{10... | collective-permute-start | bytes 1376264 | tf_op jit(solution)/shard_map/ppermute | solution.py:216
  62.7 6.8 %copy-start.1 = (f32[4,32,3456]{2,1,0:T(8,128)S(1)}, f32[4,32,3456]{2,1,0:T(8,128)}, u32[]{:S(2)}) copy-start(f32[4,32,3456]{2,1,0:T(8,128)} %param.4) | copy-start | bytes 5308420
  62.8 7.5 %collective-permute-start.14 = (f16[1,128,3456]{2,1,0:T(8,128)(2,1)S(1)}, f16[1,128,3456]{2,1,0:T(8,128)(2,1)S(1)}, u32[]{:S(2)}, u32[]{:S(2)}) collective-permute-start(f16[1,128,3456]{2,1,0:T(8,128)(2,1)S(1)} %convert_element_type.95), channel_id=1, source_target_pairs={{0,1},{1,0},{2,3},{3,2},{4,5},{5,4},{6,7},{7,6},{8,9},{9,8},{10,11... | collective-permute-start | bytes 2654216 | tf_op jit(solution)/shard_map/ppermute | solution.py:225
  69.8 18.6 %collective-permute-start.21 = (f16[2,32,3456]{2,1,0:T(8,128)(2,1)S(1)}, f16[2,32,3456]{2,1,0:T(8,128)(2,1)S(1)}, u32[]{:S(2)}, u32[]{:S(2)}) collective-permute-start(f16[2,32,3456]{2,1,0:T(8,128)(2,1)S(1)} %get-tuple-element.100), channel_id=1, source_target_pairs={{1,0},{2,1},{3,2},{4,3},{5,4},{6,5},{7,6},{0,7},{9,8},{10,9},{11,1... | collective-permute-start | bytes 1327112 | tf_op jit(solution)/shard_map/ppermute | solution.py:259
  69.8 18.6 %collective-permute-start.20 = (f16[2,32,3456]{2,1,0:T(8,128)(2,1)S(1)}, f16[2,32,3456]{2,1,0:T(8,128)(2,1)S(1)}, u32[]{:S(2)}, u32[]{:S(2)}) collective-permute-start(f16[2,32,3456]{2,1,0:T(8,128)(2,1)S(1)} %get-tuple-element.101), channel_id=1, source_target_pairs={{0,1},{1,2},{2,3},{3,4},{4,5},{5,6},{6,7},{7,0},{8,9},{9,10},{10,1... | collective-permute-start | bytes 1327112 | tf_op jit(solution)/shard_map/ppermute | solution.py:258
  70.5 8.3 %collective-permute-start.17 = (bf16[2,448,128]{2,1,0:T(8,128)(2,1)S(1)}, bf16[2,448,128]{2,1,0:T(8,128)(2,1)S(1)}, u32[]{:S(2)}, u32[]{:S(2)}) collective-permute-start(bf16[2,448,128]{2,1,0:T(8,128)(2,1)S(1)} %slice_bitcast_fusion.1), channel_id=1, source_target_pairs={{0,16},{8,24},{16,0},{24,8},{1,17},{9,25},{17,1},{25,9},{2,18},{10... | collective-permute-start | bytes 688136 | tf_op jit(solution)/shard_map/ppermute | solution.py:220
  71.5 8.1 %collective-permute-start.18 = (bf16[2,448,128]{2,1,0:T(8,128)(2,1)S(1)}, bf16[2,448,128]{2,1,0:T(8,128)(2,1)S(1)}, u32[]{:S(2)}, u32[]{:S(2)}) collective-permute-start(bf16[2,448,128]{2,1,0:T(8,128)(2,1)S(1)} %slice_bitcast_fusion), channel_id=1, source_target_pairs={{0,8},{8,0},{16,24},{24,16},{1,9},{9,1},{17,25},{25,17},{2,10},{10... | collective-permute-start | bytes 688136 | tf_op jit(solution)/shard_map/ppermute | solution.py:221
  73.0 24.5 %collective-permute-start.23 = (f16[128,3456]{1,0:T(8,128)(2,1)S(1)}, f16[128,3456]{1,0:T(8,128)(2,1)S(1)}, u32[]{:S(2)}, u32[]{:S(2)}) collective-permute-start(f16[128,3456]{1,0:T(8,128)(2,1)S(1)} %bitcast_convert_fusion.1), channel_id=1, source_target_pairs={{0,2},{1,3},{6,4},{7,5},{8,10},{9,11},{14,12},{15,13},{16,18},{17,... | collective-permute-start | bytes 2654216 | tf_op jit(solution)/shard_map/ppermute | solution.py:254
  78.9 23.0 %collective-permute-start.26 = (f16[128,3456]{1,0:T(8,128)(2,1)S(1)}, f16[128,3456]{1,0:T(8,128)(2,1)S(1)}, u32[]{:S(2)}, u32[]{:S(2)}) collective-permute-start(f16[128,3456]{1,0:T(8,128)(2,1)S(1)} %fusion.21), channel_id=1, source_target_pairs={{2,4},{3,5},{4,2},{5,3},{10,12},{11,13},{12,10},{13,11},{18,20},{1... | collective-permute-start | bytes 2654216 | tf_op jit(solution)/shard_map/ppermute | solution.py:255
  89.9 3.9 %collective-permute-start.22 = (f16[2,128,3456]{2,1,0:T(8,128)(2,1)S(1)}, f16[2,128,3456]{2,1,0:T(8,128)(2,1)S(1)}, u32[]{:S(2)}, u32[]{:S(2)}) collective-permute-start(f16[2,128,3456]{2,1,0:T(8,128)(2,1)S(1)} %convert_element_type.103), channel_id=1, source_target_pairs={{0,1},{1,0},{2,3},{3,2},{4,5},{5,4},{6,7},{7,6},{8,9},{9,8},{10,11... | collective-permute-start | bytes 5308424 | tf_op jit(solution)/shard_map/ppermute | solution.py:225
  97.5 23.4 %collective-permute-start.24 = (f16[128,3456]{1,0:T(8,128)(2,1)S(1)}, f16[128,3456]{1,0:T(8,128)(2,1)S(1)}, u32[]{:S(2)}, u32[]{:S(2)}) collective-permute-start(f16[128,3456]{1,0:T(8,128)(2,1)S(1)} %bitcast_convert_fusion), channel_id=1, source_target_pairs={{0,2},{1,3},{6,4},{7,5},{8,10},{9,11},{14,12},{15,13},{16,18},{17,... | collective-permute-start | bytes 2654216 | tf_op jit(solution)/shard_map/ppermute | solution.py:268
  102.7 18.1 %collective-permute-start.25 = (f16[128,3456]{1,0:T(8,128)(2,1)S(1)}, f16[128,3456]{1,0:T(8,128)(2,1)S(1)}, u32[]{:S(2)}, u32[]{:S(2)}) collective-permute-start(f16[128,3456]{1,0:T(8,128)(2,1)S(1)} %get-tuple-element.97), channel_id=1, source_target_pairs={{2,4},{3,5},{4,2},{5,3},{10,12},{11,13},{12,10},{13,11},{18,20},{1... | collective-permute-start | bytes 2654216 | tf_op jit(solution)/shard_map/ppermute | solution.py:269
  103.5 23.9 %collective-permute-start.27 = (f16[128,3456]{1,0:T(8,128)(2,1)S(1)}, f16[128,3456]{1,0:T(8,128)(2,1)S(1)}, u32[]{:S(2)}, u32[]{:S(2)}) collective-permute-start(f16[128,3456]{1,0:T(8,128)(2,1)S(1)} %get-tuple-element.98), channel_id=1, source_target_pairs={{4,6},{5,7},{2,0},{3,1},{12,14},{13,15},{10,8},{11,9},{20,22},{21,... | collective-permute-start | bytes 2654216 | tf_op jit(solution)/shard_map/ppermute | solution.py:270

commit v5 on v4

--- a/solution.py
+++ b/solution.py
@@ -233,16 +233,15 @@
     matrix = loaded(pltpu.with_memory_space_constraint(after(matrix, got), pltpu.HBM))
     both = [jnp.stack([keep[q], got[q]])[None] for q in range(4)]
 
-    from_end = lax.ppermute(both[3], "cell", chips((0, 3), (3, 0)))
-    both1, both2, both3, from_end, matrix = lax.optimization_barrier((both[1], both[2], both[3], from_end, matrix))
-    ga = gather_x_y(jnp.where(is_end, from_end, both[0]))
+    z3 = lax.ppermute(both[3], "cell", across(3))
+    both1, both2, z3, matrix = lax.optimization_barrier((both[1], both[2], z3, matrix))
+    ga = gather_x_y(jnp.where(is_end, z3, both[0]))
     slot_a = ga[0]
     slot_b = lax.ppermute(both2, "cell", across(2))
     z1 = lax.ppermute(both1, "cell", across(1))
-    from_middle = lax.ppermute(both3, "cell", middle)
     ga = gather_diagonal(ga)
     mine_a, theirs_a, scale_a = product(place, *ga, matrix, 4)
-    theirs_a, slot_b, z1, from_middle = lax.optimization_barrier((theirs_a, slot_b, z1, from_middle))
+    theirs_a, slot_b, z1 = lax.optimization_barrier((theirs_a, slot_b, z1))
     (pa,) = exchanged(mine_a, theirs_a)
     ma = pa.astype(F16)
     a0 = lax.ppermute(ma, "cell", ends)
@@ -257,17 +256,18 @@
     edges = after(distribution, a0) * (HALF_MAX / own_top)
     from_below = lax.ppermute(edges[tile_len - 2 :].astype(F16), "cell", ring)
     from_above = lax.ppermute(edges[:2].astype(F16), "cell", [(j, i) for i, j in ring])
-    z1, from_middle, both0, _ = lax.optimization_barrier((z1, from_middle, both[0], gb[1]))
-    slot_c = jnp.where(is_end, z1, from_middle)
+    z1, z3, both0, _ = lax.optimization_barrier((z1, z3, both[0], gb[1]))
+    slot_c = jnp.where(is_end, z1, z3)
     slot_d = jnp.where(is_end, both0, z1)
     gcd = gather_x_y(jnp.concatenate([slot_c, slot_d]))
     gcd = gather_diagonal(gcd, mb)
     mine_cd, theirs_cd, scale_cd = product(place, *behind(gcd, mb), matrix, 4)
     theirs_cd, from_below, from_above = lax.optimization_barrier((theirs_cd, from_below, from_above))
     pc, pd = exchanged(mine_cd, theirs_cd)
-    a2 = lax.ppermute(after(pc.astype(F16), a1), "cell", ends)
+    mc2 = (pd + b1.astype(F32)).astype(F16)
+    c2 = lax.ppermute(mc2, "cell", outward)
+    a2 = lax.ppermute(after(pc.astype(F16), a1, mc2), "cell", ends)
     b2 = lax.ppermute((pc + a1.astype(F32)).astype(F16), "cell", middle)
-    c2 = lax.ppermute((pd + b1.astype(F32)).astype(F16), "cell", outward)
 
     edge = edge_scales(place, *lax.optimization_barrier((slot_a, slot_c, slot_d, mb))[:3], cells)
     below = from_below.astype(F32) * edge[0:1, :1, :1]

time: 130 us -> 126 us (0.969)
  waiting for transfers between devices: 45.1 us -> 40.8 us
    ppermute x4 -> x3, waiting for transfers between devices: 21.5 us -> 15.8 us  [the longest x1 14.2 us: chain_body(): a2 = lax.ppermute(after(pc.astype(F16), a1, mc2), 'cell', ends)]
    ppermute x1, starting transfers between devices: 0.01 us -> 5.53 us  [chain_body(): slot_b = lax.ppermute(both2, 'cell', across(2))]
    ppermute x1, starting transfers between devices: 4.02 us -> 0.01 us  [chain_body(): z1 = lax.ppermute(both1, 'cell', across(1))]
    ppermute x1, starting transfers between devices: 6.51 us -> 3.43 us  [chain_body(): a0 = lax.ppermute(ma, 'cell', ends)]
    ppermute x6, waiting for transfers between devices: 8.29 us -> 10.4 us  [gather_x_y(): return (own, lax.ppermute(own, 'vel', in_x), lax.ppermute(own, 'vel', in_y))]
    ppermute x1, waiting for transfers between devices: 3.5 us -> 5.44 us  [chain_body(): a1 = lax.ppermute(after(mb, a0), 'cell', ends)]
    ppermute x1, waiting for transfers between devices: 2.39 us -> 0.47 us  [chain_body(): a0 = lax.ppermute(ma, 'cell', ends)]
    ppermute x3, waiting for transfers between devices: 4.31 us -> 2.39 us  [exchanged(): theirs = lax.ppermute(theirs.astype(F16), 'cell', other_core)]
  transfers between devices with their start and end apart: 28 -> 27, of which waited for: 13 -> 13; matrix products, arithmetic and copies ran while one was open for 7% -> 6% of each run, Pallas kernels for 17% -> 18%
where the time goes in v5:
time: 126 us; the launch traced here: 125 us
  starting transfers between devices  45.5 us (36%)
  waiting for transfers between devices  40.8 us (32%)
  Pallas kernels  23.6 us (19%)
  other arithmetic  8.41 us (7%)
  local copies, waits for them, and re-layouts  3.93 us (3%)
  between operations  2.36 us (2%)
    pallas_call x3, Pallas kernels, product(): pl.pallas_call(functools.partial(product_kernel, piece=piece, bound=HALF_...  17.6 us
    ppermute x1, waiting for transfers between devices, chain_body(): a2 = lax.ppermute(after(pc.astype(F16), a1, mc2), 'cell', ends)  14.2 us
    ppermute x6, waiting for transfers between devices, gather_x_y(): return (own, lax.ppermute(own, 'vel', in_x), lax.ppermute(own, 'vel', in_y))  10.4 us
    ppermute x1, starting transfers between devices, chain_body(): a2 = lax.ppermute(after(pc.astype(F16), a1, mc2), 'cell', ends)  8.14 us
    ppermute x6, starting transfers between devices, gather_x_y(): return (own, lax.ppermute(own, 'vel', in_x), lax.ppermute(own, 'vel', in_y))  7.22 us
    ppermute x1, starting transfers between devices, chain_body(): slot_b = lax.ppermute(both2, 'cell', across(2))  5.53 us
    ppermute x1, waiting for transfers between devices, chain_body(): a1 = lax.ppermute(after(mb, a0), 'cell', ends)  5.44 us
    ppermute x1, starting transfers between devices, chain_body(): z3 = lax.ppermute(both[3], 'cell', across(3))  5.04 us
  transfers between devices with their start and end apart: 27, of which 13 were waited for; matrix products, arithmetic and copies ran while one was open for 6% of the time, Pallas kernels for 18%

profile of v5, /device:TPU:0, one launch (start us, length us, event | category | flops | bytes accessed | tf_op | source)
XLA Modules:
  0.0 124.6 jit_solution(3729662060419295436)
XLA Ops:
  0.0 0.1 pad_add_fusion.place
  0.1 1.5 %copy-done = f32[4,32,3456]{2,1,0:T(8,128)S(1)} copy-done((f32[4,32,3456]{2,1,0:T(8,128)S(1)}, f32[4,32,3456]{2,1,0:T(8,128)}, u32[]{:S(2)}) %copy-start) | copy-done | bytes 1769496
  1.6 1.1 pieces.1
  2.6 0.5 collective-permute-start
  3.2 1.4 %collective-permute-done = bf16[4,448,128]{2,1,0:T(8,128)(2,1)S(1)} collective-permute-done((bf16[4,448,128]{2,1,0:T(8,128)(2,1)S(1)}, bf16[4,448,128]{2,1,0:T(8,128)(2,1)S(1)}, u32[]{:S(2)}, u32[]{:S(2)}) %collective-permute-start) | collective-permute-done | bytes 458784 | tf_op jit(solution)/shard_map/ppermute | solution.py:232
  4.7 5.0 %collective-permute-start.1 = (bf16[1,2,448,128]{3,2,1,0:T(8,128)(2,1)S(1)}, bf16[1,2,448,128]{3,2,1,0:T(8,128)(2,1)S(1)}, u32[]{:S(2)}, u32[]{:S(2)}) collective-permute-start(bf16[1,2,448,128]{3,2,1,0:T(8,128)(2,1)S(1)} %maximum_bitcast_fusion.2), channel_id=1, source_target_pairs={{0,6},{1,7},{2,4},{3,5},{4,2},{5,3},{6,0},{7,1},{8,14},{9,15},{10,... | collective-permute-start | bytes 688136 | tf_op jit(solution)/shard_map/ppermute | solution.py:236
  9.7 4.4 %load.1.c_ref = bf16[1728,3456]{1,0:T(8,128)(2,1)S(1)} custom-call(bf16[1728,3456]{1,0:T(8,128)(2,1)} %bitcast.57), custom_call_target="tpu_custom_call" | custom-call | flops 1 | bytes 23887872 | tf_op jit(solution)/shard_map/load/pallas_call | solution.py:150
  14.2 1.6 %collective-permute-done.1 = bf16[1,2,448,128]{3,2,1,0:T(8,128)(2,1)S(1)} collective-permute-done((bf16[1,2,448,128]{3,2,1,0:T(8,128)(2,1)S(1)}, bf16[1,2,448,128]{3,2,1,0:T(8,128)(2,1)S(1)}, u32[]{:S(2)}, u32[]{:S(2)}) %collective-permute-start.1) | collective-permute-done | bytes 229408 | tf_op jit(solution)/shard_map/ppermute | solution.py:236
  15.7 1.6 %collective-permute-start.3 = (bf16[1,2,448,128]{3,2,1,0:T(8,128)(2,1)S(1)}, bf16[1,2,448,128]{3,2,1,0:T(8,128)(2,1)S(1)}, u32[]{:S(2)}, u32[]{:S(2)}) collective-permute-start(bf16[1,2,448,128]{3,2,1,0:T(8,128)(2,1)S(1)} %broadcast_select_fusion.2.own.a_ref), channel_id=1, source_target_pairs={{0,16},{8,24},{16,0},{24,8},{1,17},{9,25},{17,1},{25,9},{2,18},{10... | collective-permute-start | bytes 688136 | tf_op jit(solution)/shard_map/ppermute | solution.py:216
  17.3 1.5 %collective-permute-start.2 = (bf16[1,2,448,128]{3,2,1,0:T(8,128)(2,1)S(1)}, bf16[1,2,448,128]{3,2,1,0:T(8,128)(2,1)S(1)}, u32[]{:S(2)}, u32[]{:S(2)}) collective-permute-start(bf16[1,2,448,128]{3,2,1,0:T(8,128)(2,1)S(1)} %broadcast_select_fusion.2.own.a_ref), channel_id=1, source_target_pairs={{0,8},{8,0},{16,24},{24,16},{1,9},{9,1},{17,25},{25,17},{2,10},{10... | collective-permute-start | bytes 688136 | tf_op jit(solution)/shard_map/ppermute | solution.py:216
  18.8 4.1 %collective-permute-done.3.gy = bf16[1,2,448,128]{3,2,1,0:T(8,128)(2,1)S(1)} collective-permute-done((bf16[1,2,448,128]{3,2,1,0:T(8,128)(2,1)S(1)}, bf16[1,2,448,128]{3,2,1,0:T(8,128)(2,1)S(1)}, u32[]{:S(2)}, u32[]{:S(2)}) %collective-permute-start.3) | collective-permute-done | bytes 229408 | tf_op jit(solution)/shard_map/ppermute | solution.py:216
  22.9 1.3 %collective-permute-start.5 = (bf16[1,448,128]{2,1,0:T(8,128)(2,1)S(1)}, bf16[1,448,128]{2,1,0:T(8,128)(2,1)S(1)}, u32[]{:S(2)}, u32[]{:S(2)}) collective-permute-start(bf16[1,448,128]{2,1,0:T(8,128)(2,1)S(1)} %slice_bitcast_fusion.4), channel_id=1, source_target_pairs={{0,8},{8,0},{16,24},{24,16},{1,9},{9,1},{17,25},{25,17},{2,10},{10... | collective-permute-start | bytes 344072 | tf_op jit(solution)/shard_map/ppermute | solution.py:221
  24.2 1.6 %collective-permute-start.4 = (bf16[1,448,128]{2,1,0:T(8,128)(2,1)S(1)}, bf16[1,448,128]{2,1,0:T(8,128)(2,1)S(1)}, u32[]{:S(2)}, u32[]{:S(2)}) collective-permute-start(bf16[1,448,128]{2,1,0:T(8,128)(2,1)S(1)} %slice_bitcast_fusion.5), channel_id=1, source_target_pairs={{0,16},{8,24},{16,0},{24,8},{1,17},{9,25},{17,1},{25,9},{2,18},{10... | collective-permute-start | bytes 344072 | tf_op jit(solution)/shard_map/ppermute | solution.py:220
  25.8 5.5 %collective-permute-start.6 = (bf16[1,2,448,128]{3,2,1,0:T(8,128)(2,1)S(1)}, bf16[1,2,448,128]{3,2,1,0:T(8,128)(2,1)S(1)}, u32[]{:S(2)}, u32[]{:S(2)}) collective-permute-start(bf16[1,2,448,128]{3,2,1,0:T(8,128)(2,1)S(1)} %get-tuple-element.58), channel_id=1, source_target_pairs={{0,4},{1,5},{2,6},{3,7},{4,0},{5,1},{6,2},{7,3},{8,12},{9,13},{10,... | collective-permute-start | bytes 688136 | tf_op jit(solution)/shard_map/ppermute | solution.py:240
  31.3 4.4 %product.3 = (f32[1,128,3456]{2,1,0:T(8,128)S(1)}, f32[1,128,3456]{2,1,0:T(8,128)S(1)}, f32[1,2,8,128]{3,2,1,0:T(8,128)S(1)}) custom-call(s32[3]{0:T(128)S(1)} %pad_add_fusion.place, bf16[1,2,448,128]{3,2,1,0:T(8,128)(2,1)S(1)} %broadcast_select_fusion.2.own.a_ref, bf16[1,2,448,128]{3,2,1,0:T(8,128)(2,1)S(1)} %collective-permute-done.2.gx, ...), custom_call_target="tpu_custom_call" | custom-call | flops 3057647616 | bytes 15482880 | tf_op jit(solution)/shard_map/product/pallas_call | solution.py:127
  35.8 4.1 %collective-permute-done.6.own = bf16[1,2,448,128]{3,2,1,0:T(8,128)(2,1)S(1)} collective-permute-done((bf16[1,2,448,128]{3,2,1,0:T(8,128)(2,1)S(1)}, bf16[1,2,448,128]{3,2,1,0:T(8,128)(2,1)S(1)}, u32[]{:S(2)}, u32[]{:S(2)}) %collective-permute-start.6) | collective-permute-done | bytes 229408 | tf_op jit(solution)/shard_map/ppermute | solution.py:240
  40.0 0.2 collective-permute-done.7
  40.1 0.1 convert_element_type.92
  40.2 0.1 collective-permute-start.8
  40.3 2.4 %collective-permute-done.8 = f16[1,128,3456]{2,1,0:T(8,128)(2,1)S(1)} collective-permute-done((f16[1,128,3456]{2,1,0:T(8,128)(2,1)S(1)}, f16[1,128,3456]{2,1,0:T(8,128)(2,1)S(1)}, u32[]{:S(2)}, u32[]{:S(2)}) %collective-permute-start.8) | collective-permute-done | bytes 884768 | tf_op jit(solution)/shard_map/ppermute | solution.py:225
  42.7 0.2 bitcast_convert_fusion.2
  42.9 0.6 collective-permute-start.10
  43.6 1.2 collective-permute-start.9
  44.8 3.4 %collective-permute-start.18 = (f16[128,3456]{1,0:T(8,128)(2,1)S(1)}, f16[128,3456]{1,0:T(8,128)(2,1)S(1)}, u32[]{:S(2)}, u32[]{:S(2)}) collective-permute-start(f16[128,3456]{1,0:T(8,128)(2,1)S(1)} %bitcast_convert_fusion.2), channel_id=1, source_target_pairs={{0,2},{1,3},{6,4},{7,5},{8,10},{9,11},{14,12},{15,13},{16,18},{17,... | collective-permute-start | bytes 2654216 | tf_op jit(solution)/shard_map/ppermute | solution.py:247
  48.2 2.4 %collective-permute-done.10.gy = bf16[1,2,448,128]{3,2,1,0:T(8,128)(2,1)S(1)} collective-permute-done((bf16[1,2,448,128]{3,2,1,0:T(8,128)(2,1)S(1)}, bf16[1,2,448,128]{3,2,1,0:T(8,128)(2,1)S(1)}, u32[]{:S(2)}, u32[]{:S(2)}) %collective-permute-start.10) | collective-permute-done | bytes 229408 | tf_op jit(solution)/shard_map/ppermute | solution.py:216
  50.7 0.6 collective-permute-start.12
  51.3 1.3 %collective-permute-start.11 = (bf16[1,448,128]{2,1,0:T(8,128)(2,1)S(1)}, bf16[1,448,128]{2,1,0:T(8,128)(2,1)S(1)}, u32[]{:S(2)}, u32[]{:S(2)}) collective-permute-start(bf16[1,448,128]{2,1,0:T(8,128)(2,1)S(1)} %slice_bitcast_fusion.3), channel_id=1, source_target_pairs={{0,16},{8,24},{16,0},{24,8},{1,17},{9,25},{17,1},{25,9},{2,18},{10... | collective-permute-start | bytes 344072 | tf_op jit(solution)/shard_map/ppermute | solution.py:220
  52.7 0.9 collective-permute-start.15
  53.6 0.5 slice.119
  54.8 0.5 slice.133
  55.4 1.5 %collective-permute-start.14 = (bf16[2,2,448,128]{3,2,1,0:T(8,128)(2,1)S(1)}, bf16[2,2,448,128]{3,2,1,0:T(8,128)(2,1)S(1)}, u32[]{:S(2)}, u32[]{:S(2)}) collective-permute-start(bf16[2,2,448,128]{3,2,1,0:T(8,128)(2,1)S(1)} %pad_maximum_fusion.2.own), channel_id=1, source_target_pairs={{0,8},{8,0},{16,24},{24,16},{1,9},{9,1},{17,25},{25,17},{2,10},{10... | collective-permute-start | bytes 1376264 | tf_op jit(solution)/shard_map/ppermute | solution.py:216
  56.9 0.6 collective-permute-done.11.dx
  57.4 4.8 %product.4 = (f32[1,128,3456]{2,1,0:T(8,128)S(1)}, f32[1,128,3456]{2,1,0:T(8,128)S(1)}, f32[1,2,8,128]{3,2,1,0:T(8,128)}) custom-call(s32[3]{0:T(128)S(1)} %pad_add_fusion.place, bf16[1,2,448,128]{3,2,1,0:T(8,128)(2,1)S(1)} %collective-permute-done.6.own, bf16[1,2,448,128]{3,2,1,0:T(8,128)(2,1)S(1)} %collective-permute-done.9.gx, ...), custom_call_target="tpu_custom_call" | custom-call | flops 3057647616 | bytes 15482880 | tf_op jit(solution)/shard_map/product/pallas_call | solution.py:127
  62.3 0.1 convert_element_type.95
  62.4 2.9 %collective-permute-done.15.gy = bf16[2,2,448,128]{3,2,1,0:T(8,128)(2,1)S(1)} collective-permute-done((bf16[2,2,448,128]{3,2,1,0:T(8,128)(2,1)S(1)}, bf16[2,2,448,128]{3,2,1,0:T(8,128)(2,1)S(1)}, u32[]{:S(2)}, u32[]{:S(2)}) %collective-permute-start.15) | collective-permute-done | bytes 458784 | tf_op jit(solution)/shard_map/ppermute | solution.py:216
  65.3 1.0 collective-permute-done.14.gx
  66.3 0.5 collective-permute-done.18
  66.8 0.1 multiply_convert_fusion
  66.9 0.1 fusion.32
  67.2 0.5 collective-permute-start.19
  67.7 0.2 bitcast_convert_fusion.1
  67.9 1.0 collective-permute-start.16
  68.8 1.5 %collective-permute-start.17 = (bf16[2,448,128]{2,1,0:T(8,128)(2,1)S(1)}, bf16[2,448,128]{2,1,0:T(8,128)(2,1)S(1)}, u32[]{:S(2)}, u32[]{:S(2)}) collective-permute-start(bf16[2,448,128]{2,1,0:T(8,128)(2,1)S(1)} %slice_bitcast_fusion), channel_id=1, source_target_pairs={{0,8},{8,0},{16,24},{24,16},{1,9},{9,1},{17,25},{25,17},{2,10},{10... | collective-permute-start | bytes 688136 | tf_op jit(solution)/shard_map/ppermute | solution.py:221
  70.3 4.4 %collective-permute-start.22 = (f16[128,3456]{1,0:T(8,128)(2,1)S(1)}, f16[128,3456]{1,0:T(8,128)(2,1)S(1)}, u32[]{:S(2)}, u32[]{:S(2)}) collective-permute-start(f16[128,3456]{1,0:T(8,128)(2,1)S(1)} %bitcast_convert_fusion.1), channel_id=1, source_target_pairs={{0,2},{1,3},{6,4},{7,5},{8,10},{9,11},{14,12},{15,13},{16,18},{17,... | collective-permute-start | bytes 2654216 | tf_op jit(solution)/shard_map/ppermute | solution.py:253
  74.8 0.3 fusion.21
  75.1 0.6 edges.1
  75.7 0.6 fusion.35
  76.2 0.7 collective-permute-start.23
  77.0 8.3 %product.5 = (f32[2,128,3456]{2,1,0:T(8,128)S(1)}, f32[2,128,3456]{2,1,0:T(8,128)S(1)}, f32[2,2,8,128]{3,2,1,0:T(8,128)S(1)}) custom-call(s32[3]{0:T(128)S(1)} %pad_add_fusion.place, bf16[2,2,448,128]{3,2,1,0:T(8,128)(2,1)S(1)} %pad_maximum_fusion.2.own, bf16[2,2,448,128]{3,2,1,0:T(8,128)(2,1)S(1)} %collective-permute-done.14.gx, ...), custom_call_target="tpu_custom_call" | custom-call | flops 6115295232 | bytes 19021824 | tf_op jit(solution)/shard_map/product/pallas_call | solution.py:127
  85.3 0.6 slice.132
  87.2 0.2 convert_element_type.103
  87.4 0.5 collective-permute-start.21
  87.9 0.7 convert_multiply_fusion.1
  88.6 0.7 convert_multiply_fusion
  89.3 5.4 %collective-permute-done.22 = f16[128,3456]{1,0:T(8,128)(2,1)S(1)} collective-permute-done((f16[128,3456]{1,0:T(8,128)(2,1)S(1)}, f16[128,3456]{1,0:T(8,128)(2,1)S(1)}, u32[]{:S(2)}, u32[]{:S(2)}) %collective-permute-start.22) | collective-permute-done | bytes 884768 | tf_op jit(solution)/shard_map/ppermute | solution.py:253
  94.8 0.8 fusion.19
  95.6 1.3 %collective-permute-start.26 = (f16[128,3456]{1,0:T(8,128)(2,1)S(1)}, f16[128,3456]{1,0:T(8,128)(2,1)S(1)}, u32[]{:S(2)}, u32[]{:S(2)}) collective-permute-start(f16[128,3456]{1,0:T(8,128)(2,1)S(1)} %get-tuple-element.94), channel_id=1, source_target_pairs={{4,6},{5,7},{2,0},{3,1},{12,14},{13,15},{10,8},{11,9},{20,22},{21,... | collective-permute-start | bytes 2654216 | tf_op jit(solution)/shard_map/ppermute | solution.py:268
  96.9 0.2 bitcast_convert_fusion
  97.1 8.1 %collective-permute-start.24 = (f16[128,3456]{1,0:T(8,128)(2,1)S(1)}, f16[128,3456]{1,0:T(8,128)(2,1)S(1)}, u32[]{:S(2)}, u32[]{:S(2)}) collective-permute-start(f16[128,3456]{1,0:T(8,128)(2,1)S(1)} %bitcast_convert_fusion), channel_id=1, source_target_pairs={{0,2},{1,3},{6,4},{7,5},{8,10},{9,11},{14,12},{15,13},{16,18},{17,... | collective-permute-start | bytes 2654216 | tf_op jit(solution)/shard_map/ppermute | solution.py:269
  105.3 0.7 collective-permute-start.25
  106.0 2.5 %fusion.6 = f32[4,32,3456]{2,1,0:T(8,128)S(1)} fusion(f32[4,32,3456]{2,1,0:T(8,128)S(1)} %copy-done.1, f32[2,32,3456]{2,1,0:T(8,128)S(1)} %convert_multiply_fusion, f32[2,32,3456]{2,1,0:T(8,128)S(1)} %convert_multiply_fusion.1, f32[3456]{0:T(1024)S(1)} %get-tuple-element.111, f32[3456]{0:T(1024)S(1)} %get-tuple-element.110, ...), kind=kLoop, calls=%fused_computation.14 | loop fusion | flops 9732096 | bytes 5343488 | tf_op jit(solution)/shard_map/mul | solution.py:57
  108.5 14.2 %collective-permute-done.24 = f16[128,3456]{1,0:T(8,128)(2,1)S(1)} collective-permute-done((f16[128,3456]{1,0:T(8,128)(2,1)S(1)}, f16[128,3456]{1,0:T(8,128)(2,1)S(1)}, u32[]{:S(2)}, u32[]{:S(2)}) %collective-permute-start.24) | collective-permute-done | bytes 884768 | tf_op jit(solution)/shard_map/ppermute | solution.py:269
  122.7 0.3 add_add_fusion
  123.1 1.5 %multiply_add_fusion = f32[4,32,3456]{2,1,0:T(8,128)} fusion(f32[4,32,3456]{2,1,0:T(8,128)S(1)} %fusion.6, f32[4,32,3456]{2,1,0:T(8,128)S(1)} %bitcast.58, f32[4,32]{1,0:T(4,128)S(1)} %bitcast.59), kind=kLoop, calls=%fused_computation.39 | loop fusion | flops 884736 | bytes 5308928 | tf_op jit(solution)/shard_map/add | solution.py:281
  (43 shorter events, 0.6 us)
Async XLA Ops:
  0.1 1.5 %copy-start = (f32[4,32,3456]{2,1,0:T(8,128)S(1)}, f32[4,32,3456]{2,1,0:T(8,128)}, u32[]{:S(2)}) copy-start(f32[4,32,3456]{2,1,0:T(8,128)} %param.4) | copy-start | bytes 5308420
  2.6 2.0 %collective-permute-start = (bf16[4,448,128]{2,1,0:T(8,128)(2,1)S(1)}, bf16[4,448,128]{2,1,0:T(8,128)(2,1)S(1)}, u32[]{:S(2)}, u32[]{:S(2)}) collective-permute-start(bf16[4,448,128]{2,1,0:T(8,128)(2,1)S(1)} %get-tuple-element.53), channel_id=1, source_target_pairs={{0,1},{1,0},{2,3},{3,2},{4,5},{5,4},{6,7},{7,6},{8,9},{9,8},{10,11... | collective-permute-start | bytes 1376264 | tf_op jit(solution)/shard_map/ppermute | solution.py:232
  4.7 11.0 %collective-permute-start.1 = (bf16[1,2,448,128]{3,2,1,0:T(8,128)(2,1)S(1)}, bf16[1,2,448,128]{3,2,1,0:T(8,128)(2,1)S(1)}, u32[]{:S(2)}, u32[]{:S(2)}) collective-permute-start(bf16[1,2,448,128]{3,2,1,0:T(8,128)(2,1)S(1)} %maximum_bitcast_fusion.2), channel_id=1, source_target_pairs={{0,6},{1,7},{2,4},{3,5},{4,2},{5,3},{6,0},{7,1},{8,14},{9,15},{10,... | collective-permute-start | bytes 688136 | tf_op jit(solution)/shard_map/ppermute | solution.py:236
  15.7 7.1 %collective-permute-start.3 = (bf16[1,2,448,128]{3,2,1,0:T(8,128)(2,1)S(1)}, bf16[1,2,448,128]{3,2,1,0:T(8,128)(2,1)S(1)}, u32[]{:S(2)}, u32[]{:S(2)}) collective-permute-start(bf16[1,2,448,128]{3,2,1,0:T(8,128)(2,1)S(1)} %broadcast_select_fusion.2.own.a_ref), channel_id=1, source_target_pairs={{0,16},{8,24},{16,0},{24,8},{1,17},{9,25},{17,1},{25,9},{2,18},{10... | collective-permute-start | bytes 688136 | tf_op jit(solution)/shard_map/ppermute | solution.py:216
  17.3 6.9 %collective-permute-start.2 = (bf16[1,2,448,128]{3,2,1,0:T(8,128)(2,1)S(1)}, bf16[1,2,448,128]{3,2,1,0:T(8,128)(2,1)S(1)}, u32[]{:S(2)}, u32[]{:S(2)}) collective-permute-start(bf16[1,2,448,128]{3,2,1,0:T(8,128)(2,1)S(1)} %broadcast_select_fusion.2.own.a_ref), channel_id=1, source_target_pairs={{0,8},{8,0},{16,24},{24,16},{1,9},{9,1},{17,25},{25,17},{2,10},{10... | collective-permute-start | bytes 688136 | tf_op jit(solution)/shard_map/ppermute | solution.py:216
  22.9 8.4 %collective-permute-start.5 = (bf16[1,448,128]{2,1,0:T(8,128)(2,1)S(1)}, bf16[1,448,128]{2,1,0:T(8,128)(2,1)S(1)}, u32[]{:S(2)}, u32[]{:S(2)}) collective-permute-start(bf16[1,448,128]{2,1,0:T(8,128)(2,1)S(1)} %slice_bitcast_fusion.4), channel_id=1, source_target_pairs={{0,8},{8,0},{16,24},{24,16},{1,9},{9,1},{17,25},{25,17},{2,10},{10... | collective-permute-start | bytes 344072 | tf_op jit(solution)/shard_map/ppermute | solution.py:221
  24.2 7.1 %collective-permute-start.4 = (bf16[1,448,128]{2,1,0:T(8,128)(2,1)S(1)}, bf16[1,448,128]{2,1,0:T(8,128)(2,1)S(1)}, u32[]{:S(2)}, u32[]{:S(2)}) collective-permute-start(bf16[1,448,128]{2,1,0:T(8,128)(2,1)S(1)} %slice_bitcast_fusion.5), channel_id=1, source_target_pairs={{0,16},{8,24},{16,0},{24,8},{1,17},{9,25},{17,1},{25,9},{2,18},{10... | collective-permute-start | bytes 344072 | tf_op jit(solution)/shard_map/ppermute | solution.py:220
  25.8 14.1 %collective-permute-start.6 = (bf16[1,2,448,128]{3,2,1,0:T(8,128)(2,1)S(1)}, bf16[1,2,448,128]{3,2,1,0:T(8,128)(2,1)S(1)}, u32[]{:S(2)}, u32[]{:S(2)}) collective-permute-start(bf16[1,2,448,128]{3,2,1,0:T(8,128)(2,1)S(1)} %get-tuple-element.58), channel_id=1, source_target_pairs={{0,4},{1,5},{2,6},{3,7},{4,0},{5,1},{6,2},{7,3},{8,12},{9,13},{10,... | collective-permute-start | bytes 688136 | tf_op jit(solution)/shard_map/ppermute | solution.py:240
  31.3 8.8 %collective-permute-start.7 = (bf16[1,2,448,128]{3,2,1,0:T(8,128)(2,1)S(1)}, bf16[1,2,448,128]{3,2,1,0:T(8,128)(2,1)S(1)}, u32[]{:S(2)}, u32[]{:S(2)}) collective-permute-start(bf16[1,2,448,128]{3,2,1,0:T(8,128)(2,1)S(1)} %get-tuple-element.59), channel_id=1, source_target_pairs={{0,2},{1,3},{2,0},{3,1},{4,6},{5,7},{6,4},{7,5},{8,10},{9,11},{10,... | collective-permute-start | bytes 688136 | tf_op jit(solution)/shard_map/ppermute | solution.py:241
  35.8 4.5 %copy-start.2 = (s32[3456]{0:T(1024)S(1)}, s32[3456]{0:T(1024)}, u32[]{:S(2)}) copy-start(s32[3456]{0:T(1024)} %param.6) | copy-start | bytes 41476
  40.2 2.5 %collective-permute-start.8 = (f16[1,128,3456]{2,1,0:T(8,128)(2,1)S(1)}, f16[1,128,3456]{2,1,0:T(8,128)(2,1)S(1)}, u32[]{:S(2)}, u32[]{:S(2)}) collective-permute-start(f16[1,128,3456]{2,1,0:T(8,128)(2,1)S(1)} %convert_element_type.92), channel_id=1, source_target_pairs={{0,1},{1,0},{2,3},{3,2},{4,5},{5,4},{6,7},{7,6},{8,9},{9,8},{10,11... | collective-permute-start | bytes 2654216 | tf_op jit(solution)/shard_map/ppermute | solution.py:225
  42.7 0.8 copy-start.3
  42.9 7.7 %collective-permute-start.10 = (bf16[1,2,448,128]{3,2,1,0:T(8,128)(2,1)S(1)}, bf16[1,2,448,128]{3,2,1,0:T(8,128)(2,1)S(1)}, u32[]{:S(2)}, u32[]{:S(2)}) collective-permute-start(bf16[1,2,448,128]{3,2,1,0:T(8,128)(2,1)S(1)} %collective-permute-done.6.own), channel_id=1, source_target_pairs={{0,16},{8,24},{16,0},{24,8},{1,17},{9,25},{17,1},{25,9},{2,18},{10... | collective-permute-start | bytes 688136 | tf_op jit(solution)/shard_map/ppermute | solution.py:216
  43.6 7.7 %collective-permute-start.9 = (bf16[1,2,448,128]{3,2,1,0:T(8,128)(2,1)S(1)}, bf16[1,2,448,128]{3,2,1,0:T(8,128)(2,1)S(1)}, u32[]{:S(2)}, u32[]{:S(2)}) collective-permute-start(bf16[1,2,448,128]{3,2,1,0:T(8,128)(2,1)S(1)} %collective-permute-done.6.own), channel_id=1, source_target_pairs={{0,8},{8,0},{16,24},{24,16},{1,9},{9,1},{17,25},{25,17},{2,10},{10... | collective-permute-start | bytes 688136 | tf_op jit(solution)/shard_map/ppermute | solution.py:216
  44.8 22.0 %collective-permute-start.18 = (f16[128,3456]{1,0:T(8,128)(2,1)S(1)}, f16[128,3456]{1,0:T(8,128)(2,1)S(1)}, u32[]{:S(2)}, u32[]{:S(2)}) collective-permute-start(f16[128,3456]{1,0:T(8,128)(2,1)S(1)} %bitcast_convert_fusion.2), channel_id=1, source_target_pairs={{0,2},{1,3},{6,4},{7,5},{8,10},{9,11},{14,12},{15,13},{16,18},{17,... | collective-permute-start | bytes 2654216 | tf_op jit(solution)/shard_map/ppermute | solution.py:247
  50.7 6.2 %collective-permute-start.12 = (bf16[1,448,128]{2,1,0:T(8,128)(2,1)S(1)}, bf16[1,448,128]{2,1,0:T(8,128)(2,1)S(1)}, u32[]{:S(2)}, u32[]{:S(2)}) collective-permute-start(bf16[1,448,128]{2,1,0:T(8,128)(2,1)S(1)} %slice_bitcast_fusion.2), channel_id=1, source_target_pairs={{0,8},{8,0},{16,24},{24,16},{1,9},{9,1},{17,25},{25,17},{2,10},{10... | collective-permute-start | bytes 344072 | tf_op jit(solution)/shard_map/ppermute | solution.py:221
  51.3 6.1 %collective-permute-start.11 = (bf16[1,448,128]{2,1,0:T(8,128)(2,1)S(1)}, bf16[1,448,128]{2,1,0:T(8,128)(2,1)S(1)}, u32[]{:S(2)}, u32[]{:S(2)}) collective-permute-start(bf16[1,448,128]{2,1,0:T(8,128)(2,1)S(1)} %slice_bitcast_fusion.3), channel_id=1, source_target_pairs={{0,16},{8,24},{16,0},{24,8},{1,17},{9,25},{17,1},{25,9},{2,18},{10... | collective-permute-start | bytes 344072 | tf_op jit(solution)/shard_map/ppermute | solution.py:220
  52.7 12.6 %collective-permute-start.15 = (bf16[2,2,448,128]{3,2,1,0:T(8,128)(2,1)S(1)}, bf16[2,2,448,128]{3,2,1,0:T(8,128)(2,1)S(1)}, u32[]{:S(2)}, u32[]{:S(2)}) collective-permute-start(bf16[2,2,448,128]{3,2,1,0:T(8,128)(2,1)S(1)} %pad_maximum_fusion.2.own), channel_id=1, source_target_pairs={{0,16},{8,24},{16,0},{24,8},{1,17},{9,25},{17,1},{25,9},{2,18},{10... | collective-permute-start | bytes 1376264 | tf_op jit(solution)/shard_map/ppermute | solution.py:216
  55.4 10.9 %collective-permute-start.14 = (bf16[2,2,448,128]{3,2,1,0:T(8,128)(2,1)S(1)}, bf16[2,2,448,128]{3,2,1,0:T(8,128)(2,1)S(1)}, u32[]{:S(2)}, u32[]{:S(2)}) collective-permute-start(bf16[2,2,448,128]{3,2,1,0:T(8,128)(2,1)S(1)} %pad_maximum_fusion.2.own), channel_id=1, source_target_pairs={{0,8},{8,0},{16,24},{24,16},{1,9},{9,1},{17,25},{25,17},{2,10},{10... | collective-permute-start | bytes 1376264 | tf_op jit(solution)/shard_map/ppermute | solution.py:216
  62.2 4.5 %copy-start.1 = (f32[4,32,3456]{2,1,0:T(8,128)S(1)}, f32[4,32,3456]{2,1,0:T(8,128)}, u32[]{:S(2)}) copy-start(f32[4,32,3456]{2,1,0:T(8,128)} %param.4) | copy-start | bytes 5308420
  62.3 5.3 %collective-permute-start.13 = (f16[1,128,3456]{2,1,0:T(8,128)(2,1)S(1)}, f16[1,128,3456]{2,1,0:T(8,128)(2,1)S(1)}, u32[]{:S(2)}, u32[]{:S(2)}) collective-permute-start(f16[1,128,3456]{2,1,0:T(8,128)(2,1)S(1)} %convert_element_type.95), channel_id=1, source_target_pairs={{0,1},{1,0},{2,3},{3,2},{4,5},{5,4},{6,7},{7,6},{8,9},{9,8},{10,11... | collective-permute-start | bytes 2654216 | tf_op jit(solution)/shard_map/ppermute | solution.py:225
  67.1 18.8 %collective-permute-start.20 = (f16[2,32,3456]{2,1,0:T(8,128)(2,1)S(1)}, f16[2,32,3456]{2,1,0:T(8,128)(2,1)S(1)}, u32[]{:S(2)}, u32[]{:S(2)}) collective-permute-start(f16[2,32,3456]{2,1,0:T(8,128)(2,1)S(1)} %get-tuple-element.96), channel_id=1, source_target_pairs={{1,0},{2,1},{3,2},{4,3},{5,4},{6,5},{7,6},{0,7},{9,8},{10,9},{11,1... | collective-permute-start | bytes 1327112 | tf_op jit(solution)/shard_map/ppermute | solution.py:258
  67.2 18.7 %collective-permute-start.19 = (f16[2,32,3456]{2,1,0:T(8,128)(2,1)S(1)}, f16[2,32,3456]{2,1,0:T(8,128)(2,1)S(1)}, u32[]{:S(2)}, u32[]{:S(2)}) collective-permute-start(f16[2,32,3456]{2,1,0:T(8,128)(2,1)S(1)} %get-tuple-element.97), channel_id=1, source_target_pairs={{0,1},{1,2},{2,3},{3,4},{4,5},{5,6},{6,7},{7,0},{8,9},{9,10},{10,1... | collective-permute-start | bytes 1327112 | tf_op jit(solution)/shard_map/ppermute | solution.py:257
  67.9 8.4 %collective-permute-start.16 = (bf16[2,448,128]{2,1,0:T(8,128)(2,1)S(1)}, bf16[2,448,128]{2,1,0:T(8,128)(2,1)S(1)}, u32[]{:S(2)}, u32[]{:S(2)}) collective-permute-start(bf16[2,448,128]{2,1,0:T(8,128)(2,1)S(1)} %slice_bitcast_fusion.1), channel_id=1, source_target_pairs={{0,16},{8,24},{16,0},{24,8},{1,17},{9,25},{17,1},{25,9},{2,18},{10... | collective-permute-start | bytes 688136 | tf_op jit(solution)/shard_map/ppermute | solution.py:220
  68.8 8.1 %collective-permute-start.17 = (bf16[2,448,128]{2,1,0:T(8,128)(2,1)S(1)}, bf16[2,448,128]{2,1,0:T(8,128)(2,1)S(1)}, u32[]{:S(2)}, u32[]{:S(2)}) collective-permute-start(bf16[2,448,128]{2,1,0:T(8,128)(2,1)S(1)} %slice_bitcast_fusion), channel_id=1, source_target_pairs={{0,8},{8,0},{16,24},{24,16},{1,9},{9,1},{17,25},{25,17},{2,10},{10... | collective-permute-start | bytes 688136 | tf_op jit(solution)/shard_map/ppermute | solution.py:221
  70.3 24.4 %collective-permute-start.22 = (f16[128,3456]{1,0:T(8,128)(2,1)S(1)}, f16[128,3456]{1,0:T(8,128)(2,1)S(1)}, u32[]{:S(2)}, u32[]{:S(2)}) collective-permute-start(f16[128,3456]{1,0:T(8,128)(2,1)S(1)} %bitcast_convert_fusion.1), channel_id=1, source_target_pairs={{0,2},{1,3},{6,4},{7,5},{8,10},{9,11},{14,12},{15,13},{16,18},{17,... | collective-permute-start | bytes 2654216 | tf_op jit(solution)/shard_map/ppermute | solution.py:253
  76.2 18.5 %collective-permute-start.23 = (f16[128,3456]{1,0:T(8,128)(2,1)S(1)}, f16[128,3456]{1,0:T(8,128)(2,1)S(1)}, u32[]{:S(2)}, u32[]{:S(2)}) collective-permute-start(f16[128,3456]{1,0:T(8,128)(2,1)S(1)} %fusion.21), channel_id=1, source_target_pairs={{2,4},{3,5},{4,2},{5,3},{10,12},{11,13},{12,10},{13,11},{18,20},{1... | collective-permute-start | bytes 2654216 | tf_op jit(solution)/shard_map/ppermute | solution.py:254
  87.4 7.4 %collective-permute-start.21 = (f16[2,128,3456]{2,1,0:T(8,128)(2,1)S(1)}, f16[2,128,3456]{2,1,0:T(8,128)(2,1)S(1)}, u32[]{:S(2)}, u32[]{:S(2)}) collective-permute-start(f16[2,128,3456]{2,1,0:T(8,128)(2,1)S(1)} %convert_element_type.103), channel_id=1, source_target_pairs={{0,1},{1,0},{2,3},{3,2},{4,5},{5,4},{6,7},{7,6},{8,9},{9,8},{10,11... | collective-permute-start | bytes 5308424 | tf_op jit(solution)/shard_map/ppermute | solution.py:225
  95.6 27.2 %collective-permute-start.26 = (f16[128,3456]{1,0:T(8,128)(2,1)S(1)}, f16[128,3456]{1,0:T(8,128)(2,1)S(1)}, u32[]{:S(2)}, u32[]{:S(2)}) collective-permute-start(f16[128,3456]{1,0:T(8,128)(2,1)S(1)} %get-tuple-element.94), channel_id=1, source_target_pairs={{4,6},{5,7},{2,0},{3,1},{12,14},{13,15},{10,8},{11,9},{20,22},{21,... | collective-permute-start | bytes 2654216 | tf_op jit(solution)/shard_map/ppermute | solution.py:268
  97.1 25.6 %collective-permute-start.24 = (f16[128,3456]{1,0:T(8,128)(2,1)S(1)}, f16[128,3456]{1,0:T(8,128)(2,1)S(1)}, u32[]{:S(2)}, u32[]{:S(2)}) collective-permute-start(f16[128,3456]{1,0:T(8,128)(2,1)S(1)} %bitcast_convert_fusion), channel_id=1, source_target_pairs={{0,2},{1,3},{6,4},{7,5},{8,10},{9,11},{14,12},{15,13},{16,18},{17,... | collective-permute-start | bytes 2654216 | tf_op jit(solution)/shard_map/ppermute | solution.py:269
  105.3 17.5 %collective-permute-start.25 = (f16[128,3456]{1,0:T(8,128)(2,1)S(1)}, f16[128,3456]{1,0:T(8,128)(2,1)S(1)}, u32[]{:S(2)}, u32[]{:S(2)}) collective-permute-start(f16[128,3456]{1,0:T(8,128)(2,1)S(1)} %get-tuple-element.93), channel_id=1, source_target_pairs={{2,4},{3,5},{4,2},{5,3},{10,12},{11,13},{12,10},{13,11},{18,20},{1... | collective-permute-start | bytes 2654216 | tf_op jit(solution)/shard_map/ppermute | solution.py:270

commit v6 on v5

--- a/solution.py
+++ b/solution.py
@@ -250,13 +250,14 @@
     mine_b, theirs_b, _ = product(place, *gb, matrix, 4)
     (pb,) = exchanged(mine_b, theirs_b)
     mb = pb.astype(F16)
-    a1 = lax.ppermute(after(mb, a0), "cell", ends)
-    b1 = lax.ppermute((pb + a0.astype(F32)).astype(F16), "cell", middle)
+    mb1 = (pb + a0.astype(F32)).astype(F16)
+    b1 = lax.ppermute(mb1, "cell", middle)
+    a1 = lax.ppermute(after(mb, a0, mb1), "cell", ends)
     own_top = keep[0:1, keep.shape[1] - 1 :, 0:1].astype(F32)
     edges = after(distribution, a0) * (HALF_MAX / own_top)
     from_below = lax.ppermute(edges[tile_len - 2 :].astype(F16), "cell", ring)
     from_above = lax.ppermute(edges[:2].astype(F16), "cell", [(j, i) for i, j in ring])
-    z1, z3, both0, _ = lax.optimization_barrier((z1, z3, both[0], gb[1]))
+    z1, z3, both0, _ = lax.optimization_barrier((z1, z3, both[0], gb[2]))
     slot_c = jnp.where(is_end, z1, z3)
     slot_d = jnp.where(is_end, both0, z1)
     gcd = gather_x_y(jnp.concatenate([slot_c, slot_d]))

time: 126 us -> 125 us (level)
  starting transfers between devices: 45.5 us -> 41.9 us
  waiting for transfers between devices: 40.8 us -> 44.1 us
    ppermute x1, starting transfers between devices: 8.14 us -> 4.65 us  [chain_body(): a2 = lax.ppermute(after(pc.astype(F16), a1, mc2), 'cell', ends)]
    ppermute x3, waiting for transfers between devices: 0.59 us -> 3.22 us  [gather_diagonal(): dx = lax.ppermute(after(gx[:, 0], *earlier), 'vel', in_y)]
  transfers between devices with their start and end apart: 27 -> 27, of which waited for: 13 -> 14; matrix products, arithmetic and copies ran while one was open for 6% -> 6% of each run, Pallas kernels for 18% -> 18%
where the time goes in v6:
time: 125 us; the launch traced here: 124 us
  waiting for transfers between devices  44.1 us (35%)
  starting transfers between devices  41.9 us (34%)
  Pallas kernels  23.6 us (19%)
  other arithmetic  8.47 us (7%)
  local copies, waits for them, and re-layouts  3.93 us (3%)
  between operations  2.37 us (2%)
    pallas_call x3, Pallas kernels, product(): pl.pallas_call(functools.partial(product_kernel, piece=piece, bound=HALF_...  17.6 us
    ppermute x1, waiting for transfers between devices, chain_body(): a2 = lax.ppermute(after(pc.astype(F16), a1, mc2), 'cell', ends)  14 us
    ppermute x6, waiting for transfers between devices, gather_x_y(): return (own, lax.ppermute(own, 'vel', in_x), lax.ppermute(own, 'vel', in_y))  10.4 us
    ppermute x6, starting transfers between devices, gather_x_y(): return (own, lax.ppermute(own, 'vel', in_x), lax.ppermute(own, 'vel', in_y))  7.22 us
    ppermute x1, waiting for transfers between devices, chain_body(): a1 = lax.ppermute(after(mb, a0, mb1), 'cell', ends)  6.35 us
    ppermute x1, starting transfers between devices, chain_body(): slot_b = lax.ppermute(both2, 'cell', across(2))  5.53 us
    ppermute x1, starting transfers between devices, chain_body(): z3 = lax.ppermute(both[3], 'cell', across(3))  5.04 us
    ppermute x1, starting transfers between devices, chain_body(): a1 = lax.ppermute(after(mb, a0, mb1), 'cell', ends)  4.79 us
  transfers between devices with their start and end apart: 27, of which 14 were waited for; matrix products, arithmetic and copies ran while one was open for 6% of the time, Pallas kernels for 18%

profile of v6, /device:TPU:0, one launch (start us, length us, event | category | flops | bytes accessed | tf_op | source)
XLA Modules:
  0.0 124.4 jit_solution(16699221915124033884)
XLA Ops:
  0.0 0.1 pad_add_fusion.place
  0.1 1.5 %copy-done = f32[4,32,3456]{2,1,0:T(8,128)S(1)} copy-done((f32[4,32,3456]{2,1,0:T(8,128)S(1)}, f32[4,32,3456]{2,1,0:T(8,128)}, u32[]{:S(2)}) %copy-start) | copy-done | bytes 1769496
  1.6 1.1 pieces.1
  2.6 0.5 collective-permute-start
  3.2 1.4 %collective-permute-done = bf16[4,448,128]{2,1,0:T(8,128)(2,1)S(1)} collective-permute-done((bf16[4,448,128]{2,1,0:T(8,128)(2,1)S(1)}, bf16[4,448,128]{2,1,0:T(8,128)(2,1)S(1)}, u32[]{:S(2)}, u32[]{:S(2)}) %collective-permute-start) | collective-permute-done | bytes 458784 | tf_op jit(solution)/shard_map/ppermute | solution.py:232
  4.7 5.0 %collective-permute-start.1 = (bf16[1,2,448,128]{3,2,1,0:T(8,128)(2,1)S(1)}, bf16[1,2,448,128]{3,2,1,0:T(8,128)(2,1)S(1)}, u32[]{:S(2)}, u32[]{:S(2)}) collective-permute-start(bf16[1,2,448,128]{3,2,1,0:T(8,128)(2,1)S(1)} %maximum_bitcast_fusion.2), channel_id=1, source_target_pairs={{0,6},{1,7},{2,4},{3,5},{4,2},{5,3},{6,0},{7,1},{8,14},{9,15},{10,... | collective-permute-start | bytes 688136 | tf_op jit(solution)/shard_map/ppermute | solution.py:236
  9.7 4.4 %load.1.c_ref = bf16[1728,3456]{1,0:T(8,128)(2,1)S(1)} custom-call(bf16[1728,3456]{1,0:T(8,128)(2,1)} %bitcast.57), custom_call_target="tpu_custom_call" | custom-call | flops 1 | bytes 23887872 | tf_op jit(solution)/shard_map/load/pallas_call | solution.py:150
  14.2 1.6 %collective-permute-done.1 = bf16[1,2,448,128]{3,2,1,0:T(8,128)(2,1)S(1)} collective-permute-done((bf16[1,2,448,128]{3,2,1,0:T(8,128)(2,1)S(1)}, bf16[1,2,448,128]{3,2,1,0:T(8,128)(2,1)S(1)}, u32[]{:S(2)}, u32[]{:S(2)}) %collective-permute-start.1) | collective-permute-done | bytes 229408 | tf_op jit(solution)/shard_map/ppermute | solution.py:236
  15.7 1.6 %collective-permute-start.3 = (bf16[1,2,448,128]{3,2,1,0:T(8,128)(2,1)S(1)}, bf16[1,2,448,128]{3,2,1,0:T(8,128)(2,1)S(1)}, u32[]{:S(2)}, u32[]{:S(2)}) collective-permute-start(bf16[1,2,448,128]{3,2,1,0:T(8,128)(2,1)S(1)} %broadcast_select_fusion.2.own.a_ref), channel_id=1, source_target_pairs={{0,16},{8,24},{16,0},{24,8},{1,17},{9,25},{17,1},{25,9},{2,18},{10... | collective-permute-start | bytes 688136 | tf_op jit(solution)/shard_map/ppermute | solution.py:216
  17.3 1.5 %collective-permute-start.2 = (bf16[1,2,448,128]{3,2,1,0:T(8,128)(2,1)S(1)}, bf16[1,2,448,128]{3,2,1,0:T(8,128)(2,1)S(1)}, u32[]{:S(2)}, u32[]{:S(2)}) collective-permute-start(bf16[1,2,448,128]{3,2,1,0:T(8,128)(2,1)S(1)} %broadcast_select_fusion.2.own.a_ref), channel_id=1, source_target_pairs={{0,8},{8,0},{16,24},{24,16},{1,9},{9,1},{17,25},{25,17},{2,10},{10... | collective-permute-start | bytes 688136 | tf_op jit(solution)/shard_map/ppermute | solution.py:216
  18.8 4.1 %collective-permute-done.3.gy = bf16[1,2,448,128]{3,2,1,0:T(8,128)(2,1)S(1)} collective-permute-done((bf16[1,2,448,128]{3,2,1,0:T(8,128)(2,1)S(1)}, bf16[1,2,448,128]{3,2,1,0:T(8,128)(2,1)S(1)}, u32[]{:S(2)}, u32[]{:S(2)}) %collective-permute-start.3) | collective-permute-done | bytes 229408 | tf_op jit(solution)/shard_map/ppermute | solution.py:216
  22.9 1.3 %collective-permute-start.5 = (bf16[1,448,128]{2,1,0:T(8,128)(2,1)S(1)}, bf16[1,448,128]{2,1,0:T(8,128)(2,1)S(1)}, u32[]{:S(2)}, u32[]{:S(2)}) collective-permute-start(bf16[1,448,128]{2,1,0:T(8,128)(2,1)S(1)} %slice_bitcast_fusion.4), channel_id=1, source_target_pairs={{0,8},{8,0},{16,24},{24,16},{1,9},{9,1},{17,25},{25,17},{2,10},{10... | collective-permute-start | bytes 344072 | tf_op jit(solution)/shard_map/ppermute | solution.py:221
  24.2 1.6 %collective-permute-start.4 = (bf16[1,448,128]{2,1,0:T(8,128)(2,1)S(1)}, bf16[1,448,128]{2,1,0:T(8,128)(2,1)S(1)}, u32[]{:S(2)}, u32[]{:S(2)}) collective-permute-start(bf16[1,448,128]{2,1,0:T(8,128)(2,1)S(1)} %slice_bitcast_fusion.5), channel_id=1, source_target_pairs={{0,16},{8,24},{16,0},{24,8},{1,17},{9,25},{17,1},{25,9},{2,18},{10... | collective-permute-start | bytes 344072 | tf_op jit(solution)/shard_map/ppermute | solution.py:220
  25.8 5.5 %collective-permute-start.6 = (bf16[1,2,448,128]{3,2,1,0:T(8,128)(2,1)S(1)}, bf16[1,2,448,128]{3,2,1,0:T(8,128)(2,1)S(1)}, u32[]{:S(2)}, u32[]{:S(2)}) collective-permute-start(bf16[1,2,448,128]{3,2,1,0:T(8,128)(2,1)S(1)} %get-tuple-element.58), channel_id=1, source_target_pairs={{0,4},{1,5},{2,6},{3,7},{4,0},{5,1},{6,2},{7,3},{8,12},{9,13},{10,... | collective-permute-start | bytes 688136 | tf_op jit(solution)/shard_map/ppermute | solution.py:240
  31.3 4.4 %product.3 = (f32[1,128,3456]{2,1,0:T(8,128)S(1)}, f32[1,128,3456]{2,1,0:T(8,128)S(1)}, f32[1,2,8,128]{3,2,1,0:T(8,128)S(1)}) custom-call(s32[3]{0:T(128)S(1)} %pad_add_fusion.place, bf16[1,2,448,128]{3,2,1,0:T(8,128)(2,1)S(1)} %broadcast_select_fusion.2.own.a_ref, bf16[1,2,448,128]{3,2,1,0:T(8,128)(2,1)S(1)} %collective-permute-done.2.gx, ...), custom_call_target="tpu_custom_call" | custom-call | flops 3057647616 | bytes 15482880 | tf_op jit(solution)/shard_map/product/pallas_call | solution.py:127
  35.8 4.1 %collective-permute-done.6.own = bf16[1,2,448,128]{3,2,1,0:T(8,128)(2,1)S(1)} collective-permute-done((bf16[1,2,448,128]{3,2,1,0:T(8,128)(2,1)S(1)}, bf16[1,2,448,128]{3,2,1,0:T(8,128)(2,1)S(1)}, u32[]{:S(2)}, u32[]{:S(2)}) %collective-permute-start.6) | collective-permute-done | bytes 229408 | tf_op jit(solution)/shard_map/ppermute | solution.py:240
  40.0 0.2 collective-permute-done.7
  40.1 0.1 convert_element_type.92
  40.2 0.1 collective-permute-start.8
  40.3 2.4 %collective-permute-done.8 = f16[1,128,3456]{2,1,0:T(8,128)(2,1)S(1)} collective-permute-done((f16[1,128,3456]{2,1,0:T(8,128)(2,1)S(1)}, f16[1,128,3456]{2,1,0:T(8,128)(2,1)S(1)}, u32[]{:S(2)}, u32[]{:S(2)}) %collective-permute-start.8) | collective-permute-done | bytes 884768 | tf_op jit(solution)/shard_map/ppermute | solution.py:225
  42.7 0.2 bitcast_convert_fusion.2
  42.9 0.6 collective-permute-start.10
  43.6 1.2 collective-permute-start.9
  44.8 3.4 %collective-permute-start.18 = (f16[128,3456]{1,0:T(8,128)(2,1)S(1)}, f16[128,3456]{1,0:T(8,128)(2,1)S(1)}, u32[]{:S(2)}, u32[]{:S(2)}) collective-permute-start(f16[128,3456]{1,0:T(8,128)(2,1)S(1)} %bitcast_convert_fusion.2), channel_id=1, source_target_pairs={{0,2},{1,3},{6,4},{7,5},{8,10},{9,11},{14,12},{15,13},{16,18},{17,... | collective-permute-start | bytes 2654216 | tf_op jit(solution)/shard_map/ppermute | solution.py:247
  48.2 2.4 %collective-permute-done.10.gy = bf16[1,2,448,128]{3,2,1,0:T(8,128)(2,1)S(1)} collective-permute-done((bf16[1,2,448,128]{3,2,1,0:T(8,128)(2,1)S(1)}, bf16[1,2,448,128]{3,2,1,0:T(8,128)(2,1)S(1)}, u32[]{:S(2)}, u32[]{:S(2)}) %collective-permute-start.10) | collective-permute-done | bytes 229408 | tf_op jit(solution)/shard_map/ppermute | solution.py:216
  50.7 0.6 collective-permute-start.12
  51.3 1.3 %collective-permute-start.11 = (bf16[1,448,128]{2,1,0:T(8,128)(2,1)S(1)}, bf16[1,448,128]{2,1,0:T(8,128)(2,1)S(1)}, u32[]{:S(2)}, u32[]{:S(2)}) collective-permute-start(bf16[1,448,128]{2,1,0:T(8,128)(2,1)S(1)} %slice_bitcast_fusion.3), channel_id=1, source_target_pairs={{0,16},{8,24},{16,0},{24,8},{1,17},{9,25},{17,1},{25,9},{2,18},{10... | collective-permute-start | bytes 344072 | tf_op jit(solution)/shard_map/ppermute | solution.py:220
  52.7 0.9 collective-permute-start.15
  53.6 0.5 slice.119
  54.8 0.5 slice.133
  55.4 1.5 %collective-permute-start.14 = (bf16[2,2,448,128]{3,2,1,0:T(8,128)(2,1)S(1)}, bf16[2,2,448,128]{3,2,1,0:T(8,128)(2,1)S(1)}, u32[]{:S(2)}, u32[]{:S(2)}) collective-permute-start(bf16[2,2,448,128]{3,2,1,0:T(8,128)(2,1)S(1)} %pad_maximum_fusion.2.own), channel_id=1, source_target_pairs={{0,8},{8,0},{16,24},{24,16},{1,9},{9,1},{17,25},{25,17},{2,10},{10... | collective-permute-start | bytes 1376264 | tf_op jit(solution)/shard_map/ppermute | solution.py:216
  56.9 0.6 collective-permute-done.11.dx
  57.4 4.8 %product.4 = (f32[1,128,3456]{2,1,0:T(8,128)S(1)}, f32[1,128,3456]{2,1,0:T(8,128)S(1)}, f32[1,2,8,128]{3,2,1,0:T(8,128)}) custom-call(s32[3]{0:T(128)S(1)} %pad_add_fusion.place, bf16[1,2,448,128]{3,2,1,0:T(8,128)(2,1)S(1)} %collective-permute-done.6.own, bf16[1,2,448,128]{3,2,1,0:T(8,128)(2,1)S(1)} %collective-permute-done.9.gx, ...), custom_call_target="tpu_custom_call" | custom-call | flops 3057647616 | bytes 15482880 | tf_op jit(solution)/shard_map/product/pallas_call | solution.py:127
  62.3 0.1 convert_element_type.95
  62.4 2.9 %collective-permute-done.15.gy = bf16[2,2,448,128]{3,2,1,0:T(8,128)(2,1)S(1)} collective-permute-done((bf16[2,2,448,128]{3,2,1,0:T(8,128)(2,1)S(1)}, bf16[2,2,448,128]{3,2,1,0:T(8,128)(2,1)S(1)}, u32[]{:S(2)}, u32[]{:S(2)}) %collective-permute-start.15) | collective-permute-done | bytes 458784 | tf_op jit(solution)/shard_map/ppermute | solution.py:216
  65.3 1.0 collective-permute-done.14.gx
  66.3 0.5 collective-permute-done.18
  66.8 0.1 multiply_convert_fusion
  66.9 0.1 fusion.32
  67.2 0.5 collective-permute-start.19
  67.7 0.2 bitcast_convert_fusion.1
  67.9 1.0 collective-permute-start.16
  68.8 1.5 %collective-permute-start.17 = (bf16[2,448,128]{2,1,0:T(8,128)(2,1)S(1)}, bf16[2,448,128]{2,1,0:T(8,128)(2,1)S(1)}, u32[]{:S(2)}, u32[]{:S(2)}) collective-permute-start(bf16[2,448,128]{2,1,0:T(8,128)(2,1)S(1)} %slice_bitcast_fusion), channel_id=1, source_target_pairs={{0,8},{8,0},{16,24},{24,16},{1,9},{9,1},{17,25},{25,17},{2,10},{10... | collective-permute-start | bytes 688136 | tf_op jit(solution)/shard_map/ppermute | solution.py:221
  70.3 0.4 fusion.21
  70.7 0.7 collective-permute-start.23
  71.4 0.6 edges.1
  72.0 0.6 fusion.35
  72.6 2.6 %collective-permute-done.16.dx = bf16[2,448,128]{2,1,0:T(8,128)(2,1)S(1)} collective-permute-done((bf16[2,448,128]{2,1,0:T(8,128)(2,1)S(1)}, bf16[2,448,128]{2,1,0:T(8,128)(2,1)S(1)}, u32[]{:S(2)}, u32[]{:S(2)}) %collective-permute-start.16) | collective-permute-done | bytes 229408 | tf_op jit(solution)/shard_map/ppermute | solution.py:220
  75.2 4.8 %collective-permute-start.22 = (f16[128,3456]{1,0:T(8,128)(2,1)S(1)}, f16[128,3456]{1,0:T(8,128)(2,1)S(1)}, u32[]{:S(2)}, u32[]{:S(2)}) collective-permute-start(f16[128,3456]{1,0:T(8,128)(2,1)S(1)} %bitcast_convert_fusion.1), channel_id=1, source_target_pairs={{0,2},{1,3},{6,4},{7,5},{8,10},{9,11},{14,12},{15,13},{16,18},{17,... | collective-permute-start | bytes 2654216 | tf_op jit(solution)/shard_map/ppermute | solution.py:255
  80.0 8.3 %product.5 = (f32[2,128,3456]{2,1,0:T(8,128)S(1)}, f32[2,128,3456]{2,1,0:T(8,128)S(1)}, f32[2,2,8,128]{3,2,1,0:T(8,128)S(1)}) custom-call(s32[3]{0:T(128)S(1)} %pad_add_fusion.place, bf16[2,2,448,128]{3,2,1,0:T(8,128)(2,1)S(1)} %pad_maximum_fusion.2.own, bf16[2,2,448,128]{3,2,1,0:T(8,128)(2,1)S(1)} %collective-permute-done.14.gx, ...), custom_call_target="tpu_custom_call" | custom-call | flops 6115295232 | bytes 19021824 | tf_op jit(solution)/shard_map/product/pallas_call | solution.py:127
  88.3 0.6 slice.132
  90.3 0.2 convert_element_type.103
  90.5 0.7 convert_multiply_fusion.1
  91.3 0.7 convert_multiply_fusion
  91.9 6.3 %collective-permute-done.22 = f16[128,3456]{1,0:T(8,128)(2,1)S(1)} collective-permute-done((f16[128,3456]{1,0:T(8,128)(2,1)S(1)}, f16[128,3456]{1,0:T(8,128)(2,1)S(1)}, u32[]{:S(2)}, u32[]{:S(2)}) %collective-permute-start.22) | collective-permute-done | bytes 884768 | tf_op jit(solution)/shard_map/ppermute | solution.py:255
  98.3 0.8 fusion.19
  99.1 1.3 %collective-permute-start.26 = (f16[128,3456]{1,0:T(8,128)(2,1)S(1)}, f16[128,3456]{1,0:T(8,128)(2,1)S(1)}, u32[]{:S(2)}, u32[]{:S(2)}) collective-permute-start(f16[128,3456]{1,0:T(8,128)(2,1)S(1)} %get-tuple-element.94), channel_id=1, source_target_pairs={{4,6},{5,7},{2,0},{3,1},{12,14},{13,15},{10,8},{11,9},{20,22},{21,... | collective-permute-start | bytes 2654216 | tf_op jit(solution)/shard_map/ppermute | solution.py:269
  100.4 0.2 bitcast_convert_fusion
  100.6 4.7 %collective-permute-start.24 = (f16[128,3456]{1,0:T(8,128)(2,1)S(1)}, f16[128,3456]{1,0:T(8,128)(2,1)S(1)}, u32[]{:S(2)}, u32[]{:S(2)}) collective-permute-start(f16[128,3456]{1,0:T(8,128)(2,1)S(1)} %bitcast_convert_fusion), channel_id=1, source_target_pairs={{0,2},{1,3},{6,4},{7,5},{8,10},{9,11},{14,12},{15,13},{16,18},{17,... | collective-permute-start | bytes 2654216 | tf_op jit(solution)/shard_map/ppermute | solution.py:270
  105.3 0.7 collective-permute-start.25
  106.0 2.5 %fusion.6 = f32[4,32,3456]{2,1,0:T(8,128)S(1)} fusion(f32[4,32,3456]{2,1,0:T(8,128)S(1)} %copy-done.1, f32[2,32,3456]{2,1,0:T(8,128)S(1)} %convert_multiply_fusion, f32[2,32,3456]{2,1,0:T(8,128)S(1)} %convert_multiply_fusion.1, f32[3456]{0:T(1024)S(1)} %get-tuple-element.111, f32[3456]{0:T(1024)S(1)} %get-tuple-element.110, ...), kind=kLoop, calls=%fused_computation.14 | loop fusion | flops 9732096 | bytes 5343488 | tf_op jit(solution)/shard_map/mul | solution.py:57
  108.5 14.0 %collective-permute-done.24 = f16[128,3456]{1,0:T(8,128)(2,1)S(1)} collective-permute-done((f16[128,3456]{1,0:T(8,128)(2,1)S(1)}, f16[128,3456]{1,0:T(8,128)(2,1)S(1)}, u32[]{:S(2)}, u32[]{:S(2)}) %collective-permute-start.24) | collective-permute-done | bytes 884768 | tf_op jit(solution)/shard_map/ppermute | solution.py:270
  122.5 0.3 add_add_fusion
  122.8 1.5 %multiply_add_fusion = f32[4,32,3456]{2,1,0:T(8,128)} fusion(f32[4,32,3456]{2,1,0:T(8,128)S(1)} %fusion.6, f32[4,32,3456]{2,1,0:T(8,128)S(1)} %bitcast.58, f32[4,32]{1,0:T(4,128)S(1)} %bitcast.59), kind=kLoop, calls=%fused_computation.39 | loop fusion | flops 884736 | bytes 5308928 | tf_op jit(solution)/shard_map/add | solution.py:282
  (43 shorter events, 0.7 us)
Async XLA Ops:
  0.1 1.5 %copy-start = (f32[4,32,3456]{2,1,0:T(8,128)S(1)}, f32[4,32,3456]{2,1,0:T(8,128)}, u32[]{:S(2)}) copy-start(f32[4,32,3456]{2,1,0:T(8,128)} %param.4) | copy-start | bytes 5308420
  2.6 2.0 %collective-permute-start = (bf16[4,448,128]{2,1,0:T(8,128)(2,1)S(1)}, bf16[4,448,128]{2,1,0:T(8,128)(2,1)S(1)}, u32[]{:S(2)}, u32[]{:S(2)}) collective-permute-start(bf16[4,448,128]{2,1,0:T(8,128)(2,1)S(1)} %get-tuple-element.53), channel_id=1, source_target_pairs={{0,1},{1,0},{2,3},{3,2},{4,5},{5,4},{6,7},{7,6},{8,9},{9,8},{10,11... | collective-permute-start | bytes 1376264 | tf_op jit(solution)/shard_map/ppermute | solution.py:232
  4.7 11.0 %collective-permute-start.1 = (bf16[1,2,448,128]{3,2,1,0:T(8,128)(2,1)S(1)}, bf16[1,2,448,128]{3,2,1,0:T(8,128)(2,1)S(1)}, u32[]{:S(2)}, u32[]{:S(2)}) collective-permute-start(bf16[1,2,448,128]{3,2,1,0:T(8,128)(2,1)S(1)} %maximum_bitcast_fusion.2), channel_id=1, source_target_pairs={{0,6},{1,7},{2,4},{3,5},{4,2},{5,3},{6,0},{7,1},{8,14},{9,15},{10,... | collective-permute-start | bytes 688136 | tf_op jit(solution)/shard_map/ppermute | solution.py:236
  15.7 7.1 %collective-permute-start.3 = (bf16[1,2,448,128]{3,2,1,0:T(8,128)(2,1)S(1)}, bf16[1,2,448,128]{3,2,1,0:T(8,128)(2,1)S(1)}, u32[]{:S(2)}, u32[]{:S(2)}) collective-permute-start(bf16[1,2,448,128]{3,2,1,0:T(8,128)(2,1)S(1)} %broadcast_select_fusion.2.own.a_ref), channel_id=1, source_target_pairs={{0,16},{8,24},{16,0},{24,8},{1,17},{9,25},{17,1},{25,9},{2,18},{10... | collective-permute-start | bytes 688136 | tf_op jit(solution)/shard_map/ppermute | solution.py:216
  17.3 6.9 %collective-permute-start.2 = (bf16[1,2,448,128]{3,2,1,0:T(8,128)(2,1)S(1)}, bf16[1,2,448,128]{3,2,1,0:T(8,128)(2,1)S(1)}, u32[]{:S(2)}, u32[]{:S(2)}) collective-permute-start(bf16[1,2,448,128]{3,2,1,0:T(8,128)(2,1)S(1)} %broadcast_select_fusion.2.own.a_ref), channel_id=1, source_target_pairs={{0,8},{8,0},{16,24},{24,16},{1,9},{9,1},{17,25},{25,17},{2,10},{10... | collective-permute-start | bytes 688136 | tf_op jit(solution)/shard_map/ppermute | solution.py:216
  22.9 8.4 %collective-permute-start.5 = (bf16[1,448,128]{2,1,0:T(8,128)(2,1)S(1)}, bf16[1,448,128]{2,1,0:T(8,128)(2,1)S(1)}, u32[]{:S(2)}, u32[]{:S(2)}) collective-permute-start(bf16[1,448,128]{2,1,0:T(8,128)(2,1)S(1)} %slice_bitcast_fusion.4), channel_id=1, source_target_pairs={{0,8},{8,0},{16,24},{24,16},{1,9},{9,1},{17,25},{25,17},{2,10},{10... | collective-permute-start | bytes 344072 | tf_op jit(solution)/shard_map/ppermute | solution.py:221
  24.2 7.1 %collective-permute-start.4 = (bf16[1,448,128]{2,1,0:T(8,128)(2,1)S(1)}, bf16[1,448,128]{2,1,0:T(8,128)(2,1)S(1)}, u32[]{:S(2)}, u32[]{:S(2)}) collective-permute-start(bf16[1,448,128]{2,1,0:T(8,128)(2,1)S(1)} %slice_bitcast_fusion.5), channel_id=1, source_target_pairs={{0,16},{8,24},{16,0},{24,8},{1,17},{9,25},{17,1},{25,9},{2,18},{10... | collective-permute-start | bytes 344072 | tf_op jit(solution)/shard_map/ppermute | solution.py:220
  25.8 14.1 %collective-permute-start.6 = (bf16[1,2,448,128]{3,2,1,0:T(8,128)(2,1)S(1)}, bf16[1,2,448,128]{3,2,1,0:T(8,128)(2,1)S(1)}, u32[]{:S(2)}, u32[]{:S(2)}) collective-permute-start(bf16[1,2,448,128]{3,2,1,0:T(8,128)(2,1)S(1)} %get-tuple-element.58), channel_id=1, source_target_pairs={{0,4},{1,5},{2,6},{3,7},{4,0},{5,1},{6,2},{7,3},{8,12},{9,13},{10,... | collective-permute-start | bytes 688136 | tf_op jit(solution)/shard_map/ppermute | solution.py:240
  31.3 8.8 %collective-permute-start.7 = (bf16[1,2,448,128]{3,2,1,0:T(8,128)(2,1)S(1)}, bf16[1,2,448,128]{3,2,1,0:T(8,128)(2,1)S(1)}, u32[]{:S(2)}, u32[]{:S(2)}) collective-permute-start(bf16[1,2,448,128]{3,2,1,0:T(8,128)(2,1)S(1)} %get-tuple-element.59), channel_id=1, source_target_pairs={{0,2},{1,3},{2,0},{3,1},{4,6},{5,7},{6,4},{7,5},{8,10},{9,11},{10,... | collective-permute-start | bytes 688136 | tf_op jit(solution)/shard_map/ppermute | solution.py:241
  35.8 4.5 %copy-start.2 = (s32[3456]{0:T(1024)S(1)}, s32[3456]{0:T(1024)}, u32[]{:S(2)}) copy-start(s32[3456]{0:T(1024)} %param.6) | copy-start | bytes 41476
  40.2 2.5 %collective-permute-start.8 = (f16[1,128,3456]{2,1,0:T(8,128)(2,1)S(1)}, f16[1,128,3456]{2,1,0:T(8,128)(2,1)S(1)}, u32[]{:S(2)}, u32[]{:S(2)}) collective-permute-start(f16[1,128,3456]{2,1,0:T(8,128)(2,1)S(1)} %convert_element_type.92), channel_id=1, source_target_pairs={{0,1},{1,0},{2,3},{3,2},{4,5},{5,4},{6,7},{7,6},{8,9},{9,8},{10,11... | collective-permute-start | bytes 2654216 | tf_op jit(solution)/shard_map/ppermute | solution.py:225
  42.7 0.8 copy-start.3
  42.9 7.7 %collective-permute-start.10 = (bf16[1,2,448,128]{3,2,1,0:T(8,128)(2,1)S(1)}, bf16[1,2,448,128]{3,2,1,0:T(8,128)(2,1)S(1)}, u32[]{:S(2)}, u32[]{:S(2)}) collective-permute-start(bf16[1,2,448,128]{3,2,1,0:T(8,128)(2,1)S(1)} %collective-permute-done.6.own), channel_id=1, source_target_pairs={{0,16},{8,24},{16,0},{24,8},{1,17},{9,25},{17,1},{25,9},{2,18},{10... | collective-permute-start | bytes 688136 | tf_op jit(solution)/shard_map/ppermute | solution.py:216
  43.6 7.7 %collective-permute-start.9 = (bf16[1,2,448,128]{3,2,1,0:T(8,128)(2,1)S(1)}, bf16[1,2,448,128]{3,2,1,0:T(8,128)(2,1)S(1)}, u32[]{:S(2)}, u32[]{:S(2)}) collective-permute-start(bf16[1,2,448,128]{3,2,1,0:T(8,128)(2,1)S(1)} %collective-permute-done.6.own), channel_id=1, source_target_pairs={{0,8},{8,0},{16,24},{24,16},{1,9},{9,1},{17,25},{25,17},{2,10},{10... | collective-permute-start | bytes 688136 | tf_op jit(solution)/shard_map/ppermute | solution.py:216
  44.8 22.0 %collective-permute-start.18 = (f16[128,3456]{1,0:T(8,128)(2,1)S(1)}, f16[128,3456]{1,0:T(8,128)(2,1)S(1)}, u32[]{:S(2)}, u32[]{:S(2)}) collective-permute-start(f16[128,3456]{1,0:T(8,128)(2,1)S(1)} %bitcast_convert_fusion.2), channel_id=1, source_target_pairs={{0,2},{1,3},{6,4},{7,5},{8,10},{9,11},{14,12},{15,13},{16,18},{17,... | collective-permute-start | bytes 2654216 | tf_op jit(solution)/shard_map/ppermute | solution.py:247
  50.7 6.2 %collective-permute-start.12 = (bf16[1,448,128]{2,1,0:T(8,128)(2,1)S(1)}, bf16[1,448,128]{2,1,0:T(8,128)(2,1)S(1)}, u32[]{:S(2)}, u32[]{:S(2)}) collective-permute-start(bf16[1,448,128]{2,1,0:T(8,128)(2,1)S(1)} %slice_bitcast_fusion.2), channel_id=1, source_target_pairs={{0,8},{8,0},{16,24},{24,16},{1,9},{9,1},{17,25},{25,17},{2,10},{10... | collective-permute-start | bytes 344072 | tf_op jit(solution)/shard_map/ppermute | solution.py:221
  51.3 6.1 %collective-permute-start.11 = (bf16[1,448,128]{2,1,0:T(8,128)(2,1)S(1)}, bf16[1,448,128]{2,1,0:T(8,128)(2,1)S(1)}, u32[]{:S(2)}, u32[]{:S(2)}) collective-permute-start(bf16[1,448,128]{2,1,0:T(8,128)(2,1)S(1)} %slice_bitcast_fusion.3), channel_id=1, source_target_pairs={{0,16},{8,24},{16,0},{24,8},{1,17},{9,25},{17,1},{25,9},{2,18},{10... | collective-permute-start | bytes 344072 | tf_op jit(solution)/shard_map/ppermute | solution.py:220
  52.7 12.6 %collective-permute-start.15 = (bf16[2,2,448,128]{3,2,1,0:T(8,128)(2,1)S(1)}, bf16[2,2,448,128]{3,2,1,0:T(8,128)(2,1)S(1)}, u32[]{:S(2)}, u32[]{:S(2)}) collective-permute-start(bf16[2,2,448,128]{3,2,1,0:T(8,128)(2,1)S(1)} %pad_maximum_fusion.2.own), channel_id=1, source_target_pairs={{0,16},{8,24},{16,0},{24,8},{1,17},{9,25},{17,1},{25,9},{2,18},{10... | collective-permute-start | bytes 1376264 | tf_op jit(solution)/shard_map/ppermute | solution.py:216
  55.4 10.9 %collective-permute-start.14 = (bf16[2,2,448,128]{3,2,1,0:T(8,128)(2,1)S(1)}, bf16[2,2,448,128]{3,2,1,0:T(8,128)(2,1)S(1)}, u32[]{:S(2)}, u32[]{:S(2)}) collective-permute-start(bf16[2,2,448,128]{3,2,1,0:T(8,128)(2,1)S(1)} %pad_maximum_fusion.2.own), channel_id=1, source_target_pairs={{0,8},{8,0},{16,24},{24,16},{1,9},{9,1},{17,25},{25,17},{2,10},{10... | collective-permute-start | bytes 1376264 | tf_op jit(solution)/shard_map/ppermute | solution.py:216
  62.2 4.5 %copy-start.1 = (f32[4,32,3456]{2,1,0:T(8,128)S(1)}, f32[4,32,3456]{2,1,0:T(8,128)}, u32[]{:S(2)}) copy-start(f32[4,32,3456]{2,1,0:T(8,128)} %param.4) | copy-start | bytes 5308420
  62.3 5.3 %collective-permute-start.13 = (f16[1,128,3456]{2,1,0:T(8,128)(2,1)S(1)}, f16[1,128,3456]{2,1,0:T(8,128)(2,1)S(1)}, u32[]{:S(2)}, u32[]{:S(2)}) collective-permute-start(f16[1,128,3456]{2,1,0:T(8,128)(2,1)S(1)} %convert_element_type.95), channel_id=1, source_target_pairs={{0,1},{1,0},{2,3},{3,2},{4,5},{5,4},{6,7},{7,6},{8,9},{9,8},{10,11... | collective-permute-start | bytes 2654216 | tf_op jit(solution)/shard_map/ppermute | solution.py:225
  67.1 21.8 %collective-permute-start.20 = (f16[2,32,3456]{2,1,0:T(8,128)(2,1)S(1)}, f16[2,32,3456]{2,1,0:T(8,128)(2,1)S(1)}, u32[]{:S(2)}, u32[]{:S(2)}) collective-permute-start(f16[2,32,3456]{2,1,0:T(8,128)(2,1)S(1)} %get-tuple-element.96), channel_id=1, source_target_pairs={{1,0},{2,1},{3,2},{4,3},{5,4},{6,5},{7,6},{0,7},{9,8},{10,9},{11,1... | collective-permute-start | bytes 1327112 | tf_op jit(solution)/shard_map/ppermute | solution.py:259
  67.2 21.8 %collective-permute-start.19 = (f16[2,32,3456]{2,1,0:T(8,128)(2,1)S(1)}, f16[2,32,3456]{2,1,0:T(8,128)(2,1)S(1)}, u32[]{:S(2)}, u32[]{:S(2)}) collective-permute-start(f16[2,32,3456]{2,1,0:T(8,128)(2,1)S(1)} %get-tuple-element.97), channel_id=1, source_target_pairs={{0,1},{1,2},{2,3},{3,4},{4,5},{5,6},{6,7},{7,0},{8,9},{9,10},{10,1... | collective-permute-start | bytes 1327112 | tf_op jit(solution)/shard_map/ppermute | solution.py:258
  67.9 7.3 %collective-permute-start.16 = (bf16[2,448,128]{2,1,0:T(8,128)(2,1)S(1)}, bf16[2,448,128]{2,1,0:T(8,128)(2,1)S(1)}, u32[]{:S(2)}, u32[]{:S(2)}) collective-permute-start(bf16[2,448,128]{2,1,0:T(8,128)(2,1)S(1)} %slice_bitcast_fusion.1), channel_id=1, source_target_pairs={{0,16},{8,24},{16,0},{24,8},{1,17},{9,25},{17,1},{25,9},{2,18},{10... | collective-permute-start | bytes 688136 | tf_op jit(solution)/shard_map/ppermute | solution.py:220
  68.8 11.2 %collective-permute-start.17 = (bf16[2,448,128]{2,1,0:T(8,128)(2,1)S(1)}, bf16[2,448,128]{2,1,0:T(8,128)(2,1)S(1)}, u32[]{:S(2)}, u32[]{:S(2)}) collective-permute-start(bf16[2,448,128]{2,1,0:T(8,128)(2,1)S(1)} %slice_bitcast_fusion), channel_id=1, source_target_pairs={{0,8},{8,0},{16,24},{24,16},{1,9},{9,1},{17,25},{25,17},{2,10},{10... | collective-permute-start | bytes 688136 | tf_op jit(solution)/shard_map/ppermute | solution.py:221
  70.7 27.6 %collective-permute-start.23 = (f16[128,3456]{1,0:T(8,128)(2,1)S(1)}, f16[128,3456]{1,0:T(8,128)(2,1)S(1)}, u32[]{:S(2)}, u32[]{:S(2)}) collective-permute-start(f16[128,3456]{1,0:T(8,128)(2,1)S(1)} %fusion.21), channel_id=1, source_target_pairs={{2,4},{3,5},{4,2},{5,3},{10,12},{11,13},{12,10},{13,11},{18,20},{1... | collective-permute-start | bytes 2654216 | tf_op jit(solution)/shard_map/ppermute | solution.py:254
  75.2 23.1 %collective-permute-start.22 = (f16[128,3456]{1,0:T(8,128)(2,1)S(1)}, f16[128,3456]{1,0:T(8,128)(2,1)S(1)}, u32[]{:S(2)}, u32[]{:S(2)}) collective-permute-start(f16[128,3456]{1,0:T(8,128)(2,1)S(1)} %bitcast_convert_fusion.1), channel_id=1, source_target_pairs={{0,2},{1,3},{6,4},{7,5},{8,10},{9,11},{14,12},{15,13},{16,18},{17,... | collective-permute-start | bytes 2654216 | tf_op jit(solution)/shard_map/ppermute | solution.py:255
  90.5 7.8 %collective-permute-start.21 = (f16[2,128,3456]{2,1,0:T(8,128)(2,1)S(1)}, f16[2,128,3456]{2,1,0:T(8,128)(2,1)S(1)}, u32[]{:S(2)}, u32[]{:S(2)}) collective-permute-start(f16[2,128,3456]{2,1,0:T(8,128)(2,1)S(1)} %convert_element_type.103), channel_id=1, source_target_pairs={{0,1},{1,0},{2,3},{3,2},{4,5},{5,4},{6,7},{7,6},{8,9},{9,8},{10,11... | collective-permute-start | bytes 5308424 | tf_op jit(solution)/shard_map/ppermute | solution.py:225
  99.1 23.4 %collective-permute-start.26 = (f16[128,3456]{1,0:T(8,128)(2,1)S(1)}, f16[128,3456]{1,0:T(8,128)(2,1)S(1)}, u32[]{:S(2)}, u32[]{:S(2)}) collective-permute-start(f16[128,3456]{1,0:T(8,128)(2,1)S(1)} %get-tuple-element.94), channel_id=1, source_target_pairs={{4,6},{5,7},{2,0},{3,1},{12,14},{13,15},{10,8},{11,9},{20,22},{21,... | collective-permute-start | bytes 2654216 | tf_op jit(solution)/shard_map/ppermute | solution.py:269
  100.6 21.9 %collective-permute-start.24 = (f16[128,3456]{1,0:T(8,128)(2,1)S(1)}, f16[128,3456]{1,0:T(8,128)(2,1)S(1)}, u32[]{:S(2)}, u32[]{:S(2)}) collective-permute-start(f16[128,3456]{1,0:T(8,128)(2,1)S(1)} %bitcast_convert_fusion), channel_id=1, source_target_pairs={{0,2},{1,3},{6,4},{7,5},{8,10},{9,11},{14,12},{15,13},{16,18},{17,... | collective-permute-start | bytes 2654216 | tf_op jit(solution)/shard_map/ppermute | solution.py:270
  105.3 17.2 %collective-permute-start.25 = (f16[128,3456]{1,0:T(8,128)(2,1)S(1)}, f16[128,3456]{1,0:T(8,128)(2,1)S(1)}, u32[]{:S(2)}, u32[]{:S(2)}) collective-permute-start(f16[128,3456]{1,0:T(8,128)(2,1)S(1)} %get-tuple-element.93), channel_id=1, source_target_pairs={{2,4},{3,5},{4,2},{5,3},{10,12},{11,13},{12,10},{13,11},{18,20},{1... | collective-permute-start | bytes 2654216 | tf_op jit(solution)/shard_map/ppermute | solution.py:271

commit v7 on v6

--- a/solution.py
+++ b/solution.py
@@ -257,7 +257,7 @@
     edges = after(distribution, a0) * (HALF_MAX / own_top)
     from_below = lax.ppermute(edges[tile_len - 2 :].astype(F16), "cell", ring)
     from_above = lax.ppermute(edges[:2].astype(F16), "cell", [(j, i) for i, j in ring])
-    z1, z3, both0, _ = lax.optimization_barrier((z1, z3, both[0], gb[2]))
+    z1, z3, both0, _ = lax.optimization_barrier((z1, z3, both[0], gb[1]))
     slot_c = jnp.where(is_end, z1, z3)
     slot_d = jnp.where(is_end, both0, z1)
     gcd = gather_x_y(jnp.concatenate([slot_c, slot_d]))

time: 125 us -> 125 us (level)
  no operation moved by 1% of the time
where the time goes in v7:
time: 125 us; the launch traced here: 124 us
  waiting for transfers between devices  44.1 us (35%)
  starting transfers between devices  41.9 us (34%)
  Pallas kernels  23.6 us (19%)
  other arithmetic  8.47 us (7%)
  local copies, waits for them, and re-layouts  3.93 us (3%)
  between operations  2.37 us (2%)
    pallas_call x3, Pallas kernels, product(): pl.pallas_call(functools.partial(product_kernel, piece=piece, bound=HALF_...  17.6 us
    ppermute x1, waiting for transfers between devices, chain_body(): a2 = lax.ppermute(after(pc.astype(F16), a1, mc2), 'cell', ends)  14 us
    ppermute x6, waiting for transfers between devices, gather_x_y(): return (own, lax.ppermute(own, 'vel', in_x), lax.ppermute(own, 'vel', in_y))  10.4 us
    ppermute x6, starting transfers between devices, gather_x_y(): return (own, lax.ppermute(own, 'vel', in_x), lax.ppermute(own, 'vel', in_y))  7.22 us
    ppermute x1, waiting for transfers between devices, chain_body(): a1 = lax.ppermute(after(mb, a0, mb1), 'cell', ends)  6.35 us
    ppermute x1, starting transfers between devices, chain_body(): slot_b = lax.ppermute(both2, 'cell', across(2))  5.53 us
    ppermute x1, starting transfers between devices, chain_body(): z3 = lax.ppermute(both[3], 'cell', across(3))  5.04 us
    ppermute x1, starting transfers between devices, chain_body(): a1 = lax.ppermute(after(mb, a0, mb1), 'cell', ends)  4.79 us
  transfers between devices with their start and end apart: 27, of which 14 were waited for; matrix products, arithmetic and copies ran while one was open for 6% of the time, Pallas kernels for 18%

profile of v7, /device:TPU:0, one launch (start us, length us, event | category | flops | bytes accessed | tf_op | source)
XLA Modules:
  0.0 124.4 jit_solution(16699221915124033884)
XLA Ops:
  0.0 0.1 pad_add_fusion.place
  0.1 1.5 %copy-done = f32[4,32,3456]{2,1,0:T(8,128)S(1)} copy-done((f32[4,32,3456]{2,1,0:T(8,128)S(1)}, f32[4,32,3456]{2,1,0:T(8,128)}, u32[]{:S(2)}) %copy-start) | copy-done | bytes 1769496
  1.6 1.1 pieces.1
  2.6 0.5 collective-permute-start
  3.2 1.4 %collective-permute-done = bf16[4,448,128]{2,1,0:T(8,128)(2,1)S(1)} collective-permute-done((bf16[4,448,128]{2,1,0:T(8,128)(2,1)S(1)}, bf16[4,448,128]{2,1,0:T(8,128)(2,1)S(1)}, u32[]{:S(2)}, u32[]{:S(2)}) %collective-permute-start) | collective-permute-done | bytes 458784 | tf_op jit(solution)/shard_map/ppermute | solution.py:232
  4.7 5.0 %collective-permute-start.1 = (bf16[1,2,448,128]{3,2,1,0:T(8,128)(2,1)S(1)}, bf16[1,2,448,128]{3,2,1,0:T(8,128)(2,1)S(1)}, u32[]{:S(2)}, u32[]{:S(2)}) collective-permute-start(bf16[1,2,448,128]{3,2,1,0:T(8,128)(2,1)S(1)} %maximum_bitcast_fusion.2), channel_id=1, source_target_pairs={{0,6},{1,7},{2,4},{3,5},{4,2},{5,3},{6,0},{7,1},{8,14},{9,15},{10,... | collective-permute-start | bytes 688136 | tf_op jit(solution)/shard_map/ppermute | solution.py:236
  9.7 4.4 %load.1.c_ref = bf16[1728,3456]{1,0:T(8,128)(2,1)S(1)} custom-call(bf16[1728,3456]{1,0:T(8,128)(2,1)} %bitcast.57), custom_call_target="tpu_custom_call" | custom-call | flops 1 | bytes 23887872 | tf_op jit(solution)/shard_map/load/pallas_call | solution.py:150
  14.2 1.6 %collective-permute-done.1 = bf16[1,2,448,128]{3,2,1,0:T(8,128)(2,1)S(1)} collective-permute-done((bf16[1,2,448,128]{3,2,1,0:T(8,128)(2,1)S(1)}, bf16[1,2,448,128]{3,2,1,0:T(8,128)(2,1)S(1)}, u32[]{:S(2)}, u32[]{:S(2)}) %collective-permute-start.1) | collective-permute-done | bytes 229408 | tf_op jit(solution)/shard_map/ppermute | solution.py:236
  15.7 1.6 %collective-permute-start.3 = (bf16[1,2,448,128]{3,2,1,0:T(8,128)(2,1)S(1)}, bf16[1,2,448,128]{3,2,1,0:T(8,128)(2,1)S(1)}, u32[]{:S(2)}, u32[]{:S(2)}) collective-permute-start(bf16[1,2,448,128]{3,2,1,0:T(8,128)(2,1)S(1)} %broadcast_select_fusion.2.own.a_ref), channel_id=1, source_target_pairs={{0,16},{8,24},{16,0},{24,8},{1,17},{9,25},{17,1},{25,9},{2,18},{10... | collective-permute-start | bytes 688136 | tf_op jit(solution)/shard_map/ppermute | solution.py:216
  17.3 1.5 %collective-permute-start.2 = (bf16[1,2,448,128]{3,2,1,0:T(8,128)(2,1)S(1)}, bf16[1,2,448,128]{3,2,1,0:T(8,128)(2,1)S(1)}, u32[]{:S(2)}, u32[]{:S(2)}) collective-permute-start(bf16[1,2,448,128]{3,2,1,0:T(8,128)(2,1)S(1)} %broadcast_select_fusion.2.own.a_ref), channel_id=1, source_target_pairs={{0,8},{8,0},{16,24},{24,16},{1,9},{9,1},{17,25},{25,17},{2,10},{10... | collective-permute-start | bytes 688136 | tf_op jit(solution)/shard_map/ppermute | solution.py:216
  18.8 4.1 %collective-permute-done.3.gy = bf16[1,2,448,128]{3,2,1,0:T(8,128)(2,1)S(1)} collective-permute-done((bf16[1,2,448,128]{3,2,1,0:T(8,128)(2,1)S(1)}, bf16[1,2,448,128]{3,2,1,0:T(8,128)(2,1)S(1)}, u32[]{:S(2)}, u32[]{:S(2)}) %collective-permute-start.3) | collective-permute-done | bytes 229408 | tf_op jit(solution)/shard_map/ppermute | solution.py:216
  22.9 1.3 %collective-permute-start.5 = (bf16[1,448,128]{2,1,0:T(8,128)(2,1)S(1)}, bf16[1,448,128]{2,1,0:T(8,128)(2,1)S(1)}, u32[]{:S(2)}, u32[]{:S(2)}) collective-permute-start(bf16[1,448,128]{2,1,0:T(8,128)(2,1)S(1)} %slice_bitcast_fusion.4), channel_id=1, source_target_pairs={{0,8},{8,0},{16,24},{24,16},{1,9},{9,1},{17,25},{25,17},{2,10},{10... | collective-permute-start | bytes 344072 | tf_op jit(solution)/shard_map/ppermute | solution.py:221
  24.2 1.6 %collective-permute-start.4 = (bf16[1,448,128]{2,1,0:T(8,128)(2,1)S(1)}, bf16[1,448,128]{2,1,0:T(8,128)(2,1)S(1)}, u32[]{:S(2)}, u32[]{:S(2)}) collective-permute-start(bf16[1,448,128]{2,1,0:T(8,128)(2,1)S(1)} %slice_bitcast_fusion.5), channel_id=1, source_target_pairs={{0,16},{8,24},{16,0},{24,8},{1,17},{9,25},{17,1},{25,9},{2,18},{10... | collective-permute-start | bytes 344072 | tf_op jit(solution)/shard_map/ppermute | solution.py:220
  25.8 5.5 %collective-permute-start.6 = (bf16[1,2,448,128]{3,2,1,0:T(8,128)(2,1)S(1)}, bf16[1,2,448,128]{3,2,1,0:T(8,128)(2,1)S(1)}, u32[]{:S(2)}, u32[]{:S(2)}) collective-permute-start(bf16[1,2,448,128]{3,2,1,0:T(8,128)(2,1)S(1)} %get-tuple-element.58), channel_id=1, source_target_pairs={{0,4},{1,5},{2,6},{3,7},{4,0},{5,1},{6,2},{7,3},{8,12},{9,13},{10,... | collective-permute-start | bytes 688136 | tf_op jit(solution)/shard_map/ppermute | solution.py:240
  31.3 4.4 %product.3 = (f32[1,128,3456]{2,1,0:T(8,128)S(1)}, f32[1,128,3456]{2,1,0:T(8,128)S(1)}, f32[1,2,8,128]{3,2,1,0:T(8,128)S(1)}) custom-call(s32[3]{0:T(128)S(1)} %pad_add_fusion.place, bf16[1,2,448,128]{3,2,1,0:T(8,128)(2,1)S(1)} %broadcast_select_fusion.2.own.a_ref, bf16[1,2,448,128]{3,2,1,0:T(8,128)(2,1)S(1)} %collective-permute-done.2.gx, ...), custom_call_target="tpu_custom_call" | custom-call | flops 3057647616 | bytes 15482880 | tf_op jit(solution)/shard_map/product/pallas_call | solution.py:127
  35.8 4.1 %collective-permute-done.6.own = bf16[1,2,448,128]{3,2,1,0:T(8,128)(2,1)S(1)} collective-permute-done((bf16[1,2,448,128]{3,2,1,0:T(8,128)(2,1)S(1)}, bf16[1,2,448,128]{3,2,1,0:T(8,128)(2,1)S(1)}, u32[]{:S(2)}, u32[]{:S(2)}) %collective-permute-start.6) | collective-permute-done | bytes 229408 | tf_op jit(solution)/shard_map/ppermute | solution.py:240
  40.0 0.2 collective-permute-done.7
  40.1 0.1 convert_element_type.92
  40.2 0.1 collective-permute-start.8
  40.3 2.4 %collective-permute-done.8 = f16[1,128,3456]{2,1,0:T(8,128)(2,1)S(1)} collective-permute-done((f16[1,128,3456]{2,1,0:T(8,128)(2,1)S(1)}, f16[1,128,3456]{2,1,0:T(8,128)(2,1)S(1)}, u32[]{:S(2)}, u32[]{:S(2)}) %collective-permute-start.8) | collective-permute-done | bytes 884768 | tf_op jit(solution)/shard_map/ppermute | solution.py:225
  42.7 0.2 bitcast_convert_fusion.2
  42.9 0.6 collective-permute-start.10
  43.6 1.2 collective-permute-start.9
  44.8 3.4 %collective-permute-start.18 = (f16[128,3456]{1,0:T(8,128)(2,1)S(1)}, f16[128,3456]{1,0:T(8,128)(2,1)S(1)}, u32[]{:S(2)}, u32[]{:S(2)}) collective-permute-start(f16[128,3456]{1,0:T(8,128)(2,1)S(1)} %bitcast_convert_fusion.2), channel_id=1, source_target_pairs={{0,2},{1,3},{6,4},{7,5},{8,10},{9,11},{14,12},{15,13},{16,18},{17,... | collective-permute-start | bytes 2654216 | tf_op jit(solution)/shard_map/ppermute | solution.py:247
  48.2 2.4 %collective-permute-done.10.gy = bf16[1,2,448,128]{3,2,1,0:T(8,128)(2,1)S(1)} collective-permute-done((bf16[1,2,448,128]{3,2,1,0:T(8,128)(2,1)S(1)}, bf16[1,2,448,128]{3,2,1,0:T(8,128)(2,1)S(1)}, u32[]{:S(2)}, u32[]{:S(2)}) %collective-permute-start.10) | collective-permute-done | bytes 229408 | tf_op jit(solution)/shard_map/ppermute | solution.py:216
  50.7 0.6 collective-permute-start.12
  51.3 1.3 %collective-permute-start.11 = (bf16[1,448,128]{2,1,0:T(8,128)(2,1)S(1)}, bf16[1,448,128]{2,1,0:T(8,128)(2,1)S(1)}, u32[]{:S(2)}, u32[]{:S(2)}) collective-permute-start(bf16[1,448,128]{2,1,0:T(8,128)(2,1)S(1)} %slice_bitcast_fusion.3), channel_id=1, source_target_pairs={{0,16},{8,24},{16,0},{24,8},{1,17},{9,25},{17,1},{25,9},{2,18},{10... | collective-permute-start | bytes 344072 | tf_op jit(solution)/shard_map/ppermute | solution.py:220
  52.7 0.9 collective-permute-start.15
  53.6 0.5 slice.119
  54.8 0.5 slice.133
  55.4 1.5 %collective-permute-start.14 = (bf16[2,2,448,128]{3,2,1,0:T(8,128)(2,1)S(1)}, bf16[2,2,448,128]{3,2,1,0:T(8,128)(2,1)S(1)}, u32[]{:S(2)}, u32[]{:S(2)}) collective-permute-start(bf16[2,2,448,128]{3,2,1,0:T(8,128)(2,1)S(1)} %pad_maximum_fusion.2.own), channel_id=1, source_target_pairs={{0,8},{8,0},{16,24},{24,16},{1,9},{9,1},{17,25},{25,17},{2,10},{10... | collective-permute-start | bytes 1376264 | tf_op jit(solution)/shard_map/ppermute | solution.py:216
  56.9 0.6 collective-permute-done.11.dx
  57.4 4.8 %product.4 = (f32[1,128,3456]{2,1,0:T(8,128)S(1)}, f32[1,128,3456]{2,1,0:T(8,128)S(1)}, f32[1,2,8,128]{3,2,1,0:T(8,128)}) custom-call(s32[3]{0:T(128)S(1)} %pad_add_fusion.place, bf16[1,2,448,128]{3,2,1,0:T(8,128)(2,1)S(1)} %collective-permute-done.6.own, bf16[1,2,448,128]{3,2,1,0:T(8,128)(2,1)S(1)} %collective-permute-done.9.gx, ...), custom_call_target="tpu_custom_call" | custom-call | flops 3057647616 | bytes 15482880 | tf_op jit(solution)/shard_map/product/pallas_call | solution.py:127
  62.3 0.1 convert_element_type.95
  62.4 2.9 %collective-permute-done.15.gy = bf16[2,2,448,128]{3,2,1,0:T(8,128)(2,1)S(1)} collective-permute-done((bf16[2,2,448,128]{3,2,1,0:T(8,128)(2,1)S(1)}, bf16[2,2,448,128]{3,2,1,0:T(8,128)(2,1)S(1)}, u32[]{:S(2)}, u32[]{:S(2)}) %collective-permute-start.15) | collective-permute-done | bytes 458784 | tf_op jit(solution)/shard_map/ppermute | solution.py:216
  65.3 1.0 collective-permute-done.14.gx
  66.3 0.5 collective-permute-done.18
  66.8 0.1 multiply_convert_fusion
  66.9 0.1 fusion.32
  67.2 0.5 collective-permute-start.19
  67.7 0.2 bitcast_convert_fusion.1
  67.9 1.0 collective-permute-start.16
  68.8 1.5 %collective-permute-start.17 = (bf16[2,448,128]{2,1,0:T(8,128)(2,1)S(1)}, bf16[2,448,128]{2,1,0:T(8,128)(2,1)S(1)}, u32[]{:S(2)}, u32[]{:S(2)}) collective-permute-start(bf16[2,448,128]{2,1,0:T(8,128)(2,1)S(1)} %slice_bitcast_fusion), channel_id=1, source_target_pairs={{0,8},{8,0},{16,24},{24,16},{1,9},{9,1},{17,25},{25,17},{2,10},{10... | collective-permute-start | bytes 688136 | tf_op jit(solution)/shard_map/ppermute | solution.py:221
  70.3 0.4 fusion.21
  70.7 0.7 collective-permute-start.23
  71.4 0.6 edges.1
  72.0 0.6 fusion.35
  72.6 2.6 %collective-permute-done.16.dx = bf16[2,448,128]{2,1,0:T(8,128)(2,1)S(1)} collective-permute-done((bf16[2,448,128]{2,1,0:T(8,128)(2,1)S(1)}, bf16[2,448,128]{2,1,0:T(8,128)(2,1)S(1)}, u32[]{:S(2)}, u32[]{:S(2)}) %collective-permute-start.16) | collective-permute-done | bytes 229408 | tf_op jit(solution)/shard_map/ppermute | solution.py:220
  75.2 4.8 %collective-permute-start.22 = (f16[128,3456]{1,0:T(8,128)(2,1)S(1)}, f16[128,3456]{1,0:T(8,128)(2,1)S(1)}, u32[]{:S(2)}, u32[]{:S(2)}) collective-permute-start(f16[128,3456]{1,0:T(8,128)(2,1)S(1)} %bitcast_convert_fusion.1), channel_id=1, source_target_pairs={{0,2},{1,3},{6,4},{7,5},{8,10},{9,11},{14,12},{15,13},{16,18},{17,... | collective-permute-start | bytes 2654216 | tf_op jit(solution)/shard_map/ppermute | solution.py:255
  80.0 8.3 %product.5 = (f32[2,128,3456]{2,1,0:T(8,128)S(1)}, f32[2,128,3456]{2,1,0:T(8,128)S(1)}, f32[2,2,8,128]{3,2,1,0:T(8,128)S(1)}) custom-call(s32[3]{0:T(128)S(1)} %pad_add_fusion.place, bf16[2,2,448,128]{3,2,1,0:T(8,128)(2,1)S(1)} %pad_maximum_fusion.2.own, bf16[2,2,448,128]{3,2,1,0:T(8,128)(2,1)S(1)} %collective-permute-done.14.gx, ...), custom_call_target="tpu_custom_call" | custom-call | flops 6115295232 | bytes 19021824 | tf_op jit(solution)/shard_map/product/pallas_call | solution.py:127
  88.3 0.6 slice.132
  90.3 0.2 convert_element_type.103
  90.5 0.7 convert_multiply_fusion.1
  91.3 0.7 convert_multiply_fusion
  91.9 6.3 %collective-permute-done.22 = f16[128,3456]{1,0:T(8,128)(2,1)S(1)} collective-permute-done((f16[128,3456]{1,0:T(8,128)(2,1)S(1)}, f16[128,3456]{1,0:T(8,128)(2,1)S(1)}, u32[]{:S(2)}, u32[]{:S(2)}) %collective-permute-start.22) | collective-permute-done | bytes 884768 | tf_op jit(solution)/shard_map/ppermute | solution.py:255
  98.3 0.8 fusion.19
  99.1 1.3 %collective-permute-start.26 = (f16[128,3456]{1,0:T(8,128)(2,1)S(1)}, f16[128,3456]{1,0:T(8,128)(2,1)S(1)}, u32[]{:S(2)}, u32[]{:S(2)}) collective-permute-start(f16[128,3456]{1,0:T(8,128)(2,1)S(1)} %get-tuple-element.94), channel_id=1, source_target_pairs={{4,6},{5,7},{2,0},{3,1},{12,14},{13,15},{10,8},{11,9},{20,22},{21,... | collective-permute-start | bytes 2654216 | tf_op jit(solution)/shard_map/ppermute | solution.py:269
  100.4 0.2 bitcast_convert_fusion
  100.6 4.7 %collective-permute-start.24 = (f16[128,3456]{1,0:T(8,128)(2,1)S(1)}, f16[128,3456]{1,0:T(8,128)(2,1)S(1)}, u32[]{:S(2)}, u32[]{:S(2)}) collective-permute-start(f16[128,3456]{1,0:T(8,128)(2,1)S(1)} %bitcast_convert_fusion), channel_id=1, source_target_pairs={{0,2},{1,3},{6,4},{7,5},{8,10},{9,11},{14,12},{15,13},{16,18},{17,... | collective-permute-start | bytes 2654216 | tf_op jit(solution)/shard_map/ppermute | solution.py:270
  105.3 0.7 collective-permute-start.25
  106.0 2.5 %fusion.6 = f32[4,32,3456]{2,1,0:T(8,128)S(1)} fusion(f32[4,32,3456]{2,1,0:T(8,128)S(1)} %copy-done.1, f32[2,32,3456]{2,1,0:T(8,128)S(1)} %convert_multiply_fusion, f32[2,32,3456]{2,1,0:T(8,128)S(1)} %convert_multiply_fusion.1, f32[3456]{0:T(1024)S(1)} %get-tuple-element.111, f32[3456]{0:T(1024)S(1)} %get-tuple-element.110, ...), kind=kLoop, calls=%fused_computation.14 | loop fusion | flops 9732096 | bytes 5343488 | tf_op jit(solution)/shard_map/mul | solution.py:57
  108.5 14.0 %collective-permute-done.24 = f16[128,3456]{1,0:T(8,128)(2,1)S(1)} collective-permute-done((f16[128,3456]{1,0:T(8,128)(2,1)S(1)}, f16[128,3456]{1,0:T(8,128)(2,1)S(1)}, u32[]{:S(2)}, u32[]{:S(2)}) %collective-permute-start.24) | collective-permute-done | bytes 884768 | tf_op jit(solution)/shard_map/ppermute | solution.py:270
  122.5 0.3 add_add_fusion
  122.8 1.5 %multiply_add_fusion = f32[4,32,3456]{2,1,0:T(8,128)} fusion(f32[4,32,3456]{2,1,0:T(8,128)S(1)} %fusion.6, f32[4,32,3456]{2,1,0:T(8,128)S(1)} %bitcast.58, f32[4,32]{1,0:T(4,128)S(1)} %bitcast.59), kind=kLoop, calls=%fused_computation.39 | loop fusion | flops 884736 | bytes 5308928 | tf_op jit(solution)/shard_map/add | solution.py:282
  (43 shorter events, 0.7 us)
Async XLA Ops:
  0.1 1.5 %copy-start = (f32[4,32,3456]{2,1,0:T(8,128)S(1)}, f32[4,32,3456]{2,1,0:T(8,128)}, u32[]{:S(2)}) copy-start(f32[4,32,3456]{2,1,0:T(8,128)} %param.4) | copy-start | bytes 5308420
  2.6 2.0 %collective-permute-start = (bf16[4,448,128]{2,1,0:T(8,128)(2,1)S(1)}, bf16[4,448,128]{2,1,0:T(8,128)(2,1)S(1)}, u32[]{:S(2)}, u32[]{:S(2)}) collective-permute-start(bf16[4,448,128]{2,1,0:T(8,128)(2,1)S(1)} %get-tuple-element.53), channel_id=1, source_target_pairs={{0,1},{1,0},{2,3},{3,2},{4,5},{5,4},{6,7},{7,6},{8,9},{9,8},{10,11... | collective-permute-start | bytes 1376264 | tf_op jit(solution)/shard_map/ppermute | solution.py:232
  4.7 11.0 %collective-permute-start.1 = (bf16[1,2,448,128]{3,2,1,0:T(8,128)(2,1)S(1)}, bf16[1,2,448,128]{3,2,1,0:T(8,128)(2,1)S(1)}, u32[]{:S(2)}, u32[]{:S(2)}) collective-permute-start(bf16[1,2,448,128]{3,2,1,0:T(8,128)(2,1)S(1)} %maximum_bitcast_fusion.2), channel_id=1, source_target_pairs={{0,6},{1,7},{2,4},{3,5},{4,2},{5,3},{6,0},{7,1},{8,14},{9,15},{10,... | collective-permute-start | bytes 688136 | tf_op jit(solution)/shard_map/ppermute | solution.py:236
  15.7 7.1 %collective-permute-start.3 = (bf16[1,2,448,128]{3,2,1,0:T(8,128)(2,1)S(1)}, bf16[1,2,448,128]{3,2,1,0:T(8,128)(2,1)S(1)}, u32[]{:S(2)}, u32[]{:S(2)}) collective-permute-start(bf16[1,2,448,128]{3,2,1,0:T(8,128)(2,1)S(1)} %broadcast_select_fusion.2.own.a_ref), channel_id=1, source_target_pairs={{0,16},{8,24},{16,0},{24,8},{1,17},{9,25},{17,1},{25,9},{2,18},{10... | collective-permute-start | bytes 688136 | tf_op jit(solution)/shard_map/ppermute | solution.py:216
  17.3 6.9 %collective-permute-start.2 = (bf16[1,2,448,128]{3,2,1,0:T(8,128)(2,1)S(1)}, bf16[1,2,448,128]{3,2,1,0:T(8,128)(2,1)S(1)}, u32[]{:S(2)}, u32[]{:S(2)}) collective-permute-start(bf16[1,2,448,128]{3,2,1,0:T(8,128)(2,1)S(1)} %broadcast_select_fusion.2.own.a_ref), channel_id=1, source_target_pairs={{0,8},{8,0},{16,24},{24,16},{1,9},{9,1},{17,25},{25,17},{2,10},{10... | collective-permute-start | bytes 688136 | tf_op jit(solution)/shard_map/ppermute | solution.py:216
  22.9 8.4 %collective-permute-start.5 = (bf16[1,448,128]{2,1,0:T(8,128)(2,1)S(1)}, bf16[1,448,128]{2,1,0:T(8,128)(2,1)S(1)}, u32[]{:S(2)}, u32[]{:S(2)}) collective-permute-start(bf16[1,448,128]{2,1,0:T(8,128)(2,1)S(1)} %slice_bitcast_fusion.4), channel_id=1, source_target_pairs={{0,8},{8,0},{16,24},{24,16},{1,9},{9,1},{17,25},{25,17},{2,10},{10... | collective-permute-start | bytes 344072 | tf_op jit(solution)/shard_map/ppermute | solution.py:221
  24.2 7.1 %collective-permute-start.4 = (bf16[1,448,128]{2,1,0:T(8,128)(2,1)S(1)}, bf16[1,448,128]{2,1,0:T(8,128)(2,1)S(1)}, u32[]{:S(2)}, u32[]{:S(2)}) collective-permute-start(bf16[1,448,128]{2,1,0:T(8,128)(2,1)S(1)} %slice_bitcast_fusion.5), channel_id=1, source_target_pairs={{0,16},{8,24},{16,0},{24,8},{1,17},{9,25},{17,1},{25,9},{2,18},{10... | collective-permute-start | bytes 344072 | tf_op jit(solution)/shard_map/ppermute | solution.py:220
  25.8 14.1 %collective-permute-start.6 = (bf16[1,2,448,128]{3,2,1,0:T(8,128)(2,1)S(1)}, bf16[1,2,448,128]{3,2,1,0:T(8,128)(2,1)S(1)}, u32[]{:S(2)}, u32[]{:S(2)}) collective-permute-start(bf16[1,2,448,128]{3,2,1,0:T(8,128)(2,1)S(1)} %get-tuple-element.58), channel_id=1, source_target_pairs={{0,4},{1,5},{2,6},{3,7},{4,0},{5,1},{6,2},{7,3},{8,12},{9,13},{10,... | collective-permute-start | bytes 688136 | tf_op jit(solution)/shard_map/ppermute | solution.py:240
  31.3 8.8 %collective-permute-start.7 = (bf16[1,2,448,128]{3,2,1,0:T(8,128)(2,1)S(1)}, bf16[1,2,448,128]{3,2,1,0:T(8,128)(2,1)S(1)}, u32[]{:S(2)}, u32[]{:S(2)}) collective-permute-start(bf16[1,2,448,128]{3,2,1,0:T(8,128)(2,1)S(1)} %get-tuple-element.59), channel_id=1, source_target_pairs={{0,2},{1,3},{2,0},{3,1},{4,6},{5,7},{6,4},{7,5},{8,10},{9,11},{10,... | collective-permute-start | bytes 688136 | tf_op jit(solution)/shard_map/ppermute | solution.py:241
  35.8 4.5 %copy-start.2 = (s32[3456]{0:T(1024)S(1)}, s32[3456]{0:T(1024)}, u32[]{:S(2)}) copy-start(s32[3456]{0:T(1024)} %param.6) | copy-start | bytes 41476
  40.2 2.5 %collective-permute-start.8 = (f16[1,128,3456]{2,1,0:T(8,128)(2,1)S(1)}, f16[1,128,3456]{2,1,0:T(8,128)(2,1)S(1)}, u32[]{:S(2)}, u32[]{:S(2)}) collective-permute-start(f16[1,128,3456]{2,1,0:T(8,128)(2,1)S(1)} %convert_element_type.92), channel_id=1, source_target_pairs={{0,1},{1,0},{2,3},{3,2},{4,5},{5,4},{6,7},{7,6},{8,9},{9,8},{10,11... | collective-permute-start | bytes 2654216 | tf_op jit(solution)/shard_map/ppermute | solution.py:225
  42.7 0.8 copy-start.3
  42.9 7.7 %collective-permute-start.10 = (bf16[1,2,448,128]{3,2,1,0:T(8,128)(2,1)S(1)}, bf16[1,2,448,128]{3,2,1,0:T(8,128)(2,1)S(1)}, u32[]{:S(2)}, u32[]{:S(2)}) collective-permute-start(bf16[1,2,448,128]{3,2,1,0:T(8,128)(2,1)S(1)} %collective-permute-done.6.own), channel_id=1, source_target_pairs={{0,16},{8,24},{16,0},{24,8},{1,17},{9,25},{17,1},{25,9},{2,18},{10... | collective-permute-start | bytes 688136 | tf_op jit(solution)/shard_map/ppermute | solution.py:216
  43.6 7.7 %collective-permute-start.9 = (bf16[1,2,448,128]{3,2,1,0:T(8,128)(2,1)S(1)}, bf16[1,2,448,128]{3,2,1,0:T(8,128)(2,1)S(1)}, u32[]{:S(2)}, u32[]{:S(2)}) collective-permute-start(bf16[1,2,448,128]{3,2,1,0:T(8,128)(2,1)S(1)} %collective-permute-done.6.own), channel_id=1, source_target_pairs={{0,8},{8,0},{16,24},{24,16},{1,9},{9,1},{17,25},{25,17},{2,10},{10... | collective-permute-start | bytes 688136 | tf_op jit(solution)/shard_map/ppermute | solution.py:216
  44.8 22.0 %collective-permute-start.18 = (f16[128,3456]{1,0:T(8,128)(2,1)S(1)}, f16[128,3456]{1,0:T(8,128)(2,1)S(1)}, u32[]{:S(2)}, u32[]{:S(2)}) collective-permute-start(f16[128,3456]{1,0:T(8,128)(2,1)S(1)} %bitcast_convert_fusion.2), channel_id=1, source_target_pairs={{0,2},{1,3},{6,4},{7,5},{8,10},{9,11},{14,12},{15,13},{16,18},{17,... | collective-permute-start | bytes 2654216 | tf_op jit(solution)/shard_map/ppermute | solution.py:247
  50.7 6.2 %collective-permute-start.12 = (bf16[1,448,128]{2,1,0:T(8,128)(2,1)S(1)}, bf16[1,448,128]{2,1,0:T(8,128)(2,1)S(1)}, u32[]{:S(2)}, u32[]{:S(2)}) collective-permute-start(bf16[1,448,128]{2,1,0:T(8,128)(2,1)S(1)} %slice_bitcast_fusion.2), channel_id=1, source_target_pairs={{0,8},{8,0},{16,24},{24,16},{1,9},{9,1},{17,25},{25,17},{2,10},{10... | collective-permute-start | bytes 344072 | tf_op jit(solution)/shard_map/ppermute | solution.py:221
  51.3 6.1 %collective-permute-start.11 = (bf16[1,448,128]{2,1,0:T(8,128)(2,1)S(1)}, bf16[1,448,128]{2,1,0:T(8,128)(2,1)S(1)}, u32[]{:S(2)}, u32[]{:S(2)}) collective-permute-start(bf16[1,448,128]{2,1,0:T(8,128)(2,1)S(1)} %slice_bitcast_fusion.3), channel_id=1, source_target_pairs={{0,16},{8,24},{16,0},{24,8},{1,17},{9,25},{17,1},{25,9},{2,18},{10... | collective-permute-start | bytes 344072 | tf_op jit(solution)/shard_map/ppermute | solution.py:220
  52.7 12.6 %collective-permute-start.15 = (bf16[2,2,448,128]{3,2,1,0:T(8,128)(2,1)S(1)}, bf16[2,2,448,128]{3,2,1,0:T(8,128)(2,1)S(1)}, u32[]{:S(2)}, u32[]{:S(2)}) collective-permute-start(bf16[2,2,448,128]{3,2,1,0:T(8,128)(2,1)S(1)} %pad_maximum_fusion.2.own), channel_id=1, source_target_pairs={{0,16},{8,24},{16,0},{24,8},{1,17},{9,25},{17,1},{25,9},{2,18},{10... | collective-permute-start | bytes 1376264 | tf_op jit(solution)/shard_map/ppermute | solution.py:216
  55.4 10.9 %collective-permute-start.14 = (bf16[2,2,448,128]{3,2,1,0:T(8,128)(2,1)S(1)}, bf16[2,2,448,128]{3,2,1,0:T(8,128)(2,1)S(1)}, u32[]{:S(2)}, u32[]{:S(2)}) collective-permute-start(bf16[2,2,448,128]{3,2,1,0:T(8,128)(2,1)S(1)} %pad_maximum_fusion.2.own), channel_id=1, source_target_pairs={{0,8},{8,0},{16,24},{24,16},{1,9},{9,1},{17,25},{25,17},{2,10},{10... | collective-permute-start | bytes 1376264 | tf_op jit(solution)/shard_map/ppermute | solution.py:216
  62.2 4.5 %copy-start.1 = (f32[4,32,3456]{2,1,0:T(8,128)S(1)}, f32[4,32,3456]{2,1,0:T(8,128)}, u32[]{:S(2)}) copy-start(f32[4,32,3456]{2,1,0:T(8,128)} %param.4) | copy-start | bytes 5308420
  62.3 5.3 %collective-permute-start.13 = (f16[1,128,3456]{2,1,0:T(8,128)(2,1)S(1)}, f16[1,128,3456]{2,1,0:T(8,128)(2,1)S(1)}, u32[]{:S(2)}, u32[]{:S(2)}) collective-permute-start(f16[1,128,3456]{2,1,0:T(8,128)(2,1)S(1)} %convert_element_type.95), channel_id=1, source_target_pairs={{0,1},{1,0},{2,3},{3,2},{4,5},{5,4},{6,7},{7,6},{8,9},{9,8},{10,11... | collective-permute-start | bytes 2654216 | tf_op jit(solution)/shard_map/ppermute | solution.py:225
  67.1 21.8 %collective-permute-start.20 = (f16[2,32,3456]{2,1,0:T(8,128)(2,1)S(1)}, f16[2,32,3456]{2,1,0:T(8,128)(2,1)S(1)}, u32[]{:S(2)}, u32[]{:S(2)}) collective-permute-start(f16[2,32,3456]{2,1,0:T(8,128)(2,1)S(1)} %get-tuple-element.96), channel_id=1, source_target_pairs={{1,0},{2,1},{3,2},{4,3},{5,4},{6,5},{7,6},{0,7},{9,8},{10,9},{11,1... | collective-permute-start | bytes 1327112 | tf_op jit(solution)/shard_map/ppermute | solution.py:259
  67.2 21.8 %collective-permute-start.19 = (f16[2,32,3456]{2,1,0:T(8,128)(2,1)S(1)}, f16[2,32,3456]{2,1,0:T(8,128)(2,1)S(1)}, u32[]{:S(2)}, u32[]{:S(2)}) collective-permute-start(f16[2,32,3456]{2,1,0:T(8,128)(2,1)S(1)} %get-tuple-element.97), channel_id=1, source_target_pairs={{0,1},{1,2},{2,3},{3,4},{4,5},{5,6},{6,7},{7,0},{8,9},{9,10},{10,1... | collective-permute-start | bytes 1327112 | tf_op jit(solution)/shard_map/ppermute | solution.py:258
  67.9 7.3 %collective-permute-start.16 = (bf16[2,448,128]{2,1,0:T(8,128)(2,1)S(1)}, bf16[2,448,128]{2,1,0:T(8,128)(2,1)S(1)}, u32[]{:S(2)}, u32[]{:S(2)}) collective-permute-start(bf16[2,448,128]{2,1,0:T(8,128)(2,1)S(1)} %slice_bitcast_fusion.1), channel_id=1, source_target_pairs={{0,16},{8,24},{16,0},{24,8},{1,17},{9,25},{17,1},{25,9},{2,18},{10... | collective-permute-start | bytes 688136 | tf_op jit(solution)/shard_map/ppermute | solution.py:220
  68.8 11.2 %collective-permute-start.17 = (bf16[2,448,128]{2,1,0:T(8,128)(2,1)S(1)}, bf16[2,448,128]{2,1,0:T(8,128)(2,1)S(1)}, u32[]{:S(2)}, u32[]{:S(2)}) collective-permute-start(bf16[2,448,128]{2,1,0:T(8,128)(2,1)S(1)} %slice_bitcast_fusion), channel_id=1, source_target_pairs={{0,8},{8,0},{16,24},{24,16},{1,9},{9,1},{17,25},{25,17},{2,10},{10... | collective-permute-start | bytes 688136 | tf_op jit(solution)/shard_map/ppermute | solution.py:221
  70.7 27.6 %collective-permute-start.23 = (f16[128,3456]{1,0:T(8,128)(2,1)S(1)}, f16[128,3456]{1,0:T(8,128)(2,1)S(1)}, u32[]{:S(2)}, u32[]{:S(2)}) collective-permute-start(f16[128,3456]{1,0:T(8,128)(2,1)S(1)} %fusion.21), channel_id=1, source_target_pairs={{2,4},{3,5},{4,2},{5,3},{10,12},{11,13},{12,10},{13,11},{18,20},{1... | collective-permute-start | bytes 2654216 | tf_op jit(solution)/shard_map/ppermute | solution.py:254
  75.2 23.1 %collective-permute-start.22 = (f16[128,3456]{1,0:T(8,128)(2,1)S(1)}, f16[128,3456]{1,0:T(8,128)(2,1)S(1)}, u32[]{:S(2)}, u32[]{:S(2)}) collective-permute-start(f16[128,3456]{1,0:T(8,128)(2,1)S(1)} %bitcast_convert_fusion.1), channel_id=1, source_target_pairs={{0,2},{1,3},{6,4},{7,5},{8,10},{9,11},{14,12},{15,13},{16,18},{17,... | collective-permute-start | bytes 2654216 | tf_op jit(solution)/shard_map/ppermute | solution.py:255
  90.5 7.8 %collective-permute-start.21 = (f16[2,128,3456]{2,1,0:T(8,128)(2,1)S(1)}, f16[2,128,3456]{2,1,0:T(8,128)(2,1)S(1)}, u32[]{:S(2)}, u32[]{:S(2)}) collective-permute-start(f16[2,128,3456]{2,1,0:T(8,128)(2,1)S(1)} %convert_element_type.103), channel_id=1, source_target_pairs={{0,1},{1,0},{2,3},{3,2},{4,5},{5,4},{6,7},{7,6},{8,9},{9,8},{10,11... | collective-permute-start | bytes 5308424 | tf_op jit(solution)/shard_map/ppermute | solution.py:225
  99.1 23.4 %collective-permute-start.26 = (f16[128,3456]{1,0:T(8,128)(2,1)S(1)}, f16[128,3456]{1,0:T(8,128)(2,1)S(1)}, u32[]{:S(2)}, u32[]{:S(2)}) collective-permute-start(f16[128,3456]{1,0:T(8,128)(2,1)S(1)} %get-tuple-element.94), channel_id=1, source_target_pairs={{4,6},{5,7},{2,0},{3,1},{12,14},{13,15},{10,8},{11,9},{20,22},{21,... | collective-permute-start | bytes 2654216 | tf_op jit(solution)/shard_map/ppermute | solution.py:269
  100.6 21.9 %collective-permute-start.24 = (f16[128,3456]{1,0:T(8,128)(2,1)S(1)}, f16[128,3456]{1,0:T(8,128)(2,1)S(1)}, u32[]{:S(2)}, u32[]{:S(2)}) collective-permute-start(f16[128,3456]{1,0:T(8,128)(2,1)S(1)} %bitcast_convert_fusion), channel_id=1, source_target_pairs={{0,2},{1,3},{6,4},{7,5},{8,10},{9,11},{14,12},{15,13},{16,18},{17,... | collective-permute-start | bytes 2654216 | tf_op jit(solution)/shard_map/ppermute | solution.py:270
  105.3 17.2 %collective-permute-start.25 = (f16[128,3456]{1,0:T(8,128)(2,1)S(1)}, f16[128,3456]{1,0:T(8,128)(2,1)S(1)}, u32[]{:S(2)}, u32[]{:S(2)}) collective-permute-start(f16[128,3456]{1,0:T(8,128)(2,1)S(1)} %get-tuple-element.93), channel_id=1, source_target_pairs={{2,4},{3,5},{4,2},{5,3},{10,12},{11,13},{12,10},{13,11},{18,20},{1... | collective-permute-start | bytes 2654216 | tf_op jit(solution)/shard_map/ppermute | solution.py:271
